TPU v7x, 32 devices: a whole 2x2x4 slice. The times are simulated.
32 devices in a mesh: expert: 4 (over x, core), fsdp: 8 (over z, y).
Axes of the slice: x: 2, y: 2, z: 4, core: 2. Of those that a mesh axis runs over, the one named last changes fastest.
Arguments:
- hidden_in: bfloat16 [32, 1024, 768], P(('expert', 'fsdp')), may hold values from -6 to 6
- prev_logits: bfloat16 [32, 1024, 8], P(('expert', 'fsdp')), may hold values from -6 to 6
- seq_lengths: int32 [32], replicated, may hold values from 256 to 1024, as said below
- seq_order: int32 [32], replicated, may hold values from 0 to 31, as said below
- routes: int32 [32, 1024, 2], P(('expert', 'fsdp')), may hold values from 0 to 7, all different within a row; in each aligned block of 1024 rows (0 to 1023, 1024 to 2047, ..., all dimensions but the last counted through in order) at most 256 rows name the same one
- w_query: bfloat16 [768, 768], P(None, 'fsdp'), may hold values from -0.21875 to 0.21875
- w_key: bfloat16 [768, 768], P(None, 'fsdp'), may hold values from -0.21875 to 0.21875
- w_value: bfloat16 [768, 768], P(None, 'fsdp'), may hold values from -0.21875 to 0.21875
- w_output: bfloat16 [768, 768], P('fsdp'), may hold values from -1.75 to 1.75
- gain_attn: bfloat16 [768], P('fsdp'), may hold values from 0.5 to 1.5
- gain_moe: bfloat16 [768], P('fsdp'), may hold values from 0.5 to 1.5
- w_router: bfloat16 [768, 8], P('fsdp'), may hold values from -0.109375 to 0.109375
- w_gating: bfloat16 [8, 8], replicated, may hold values from -1 to 1
- w_const: bfloat16 [768, 4], P('fsdp'), may hold values from -0.21875 to 0.21875
- v_const: bfloat16 [2, 768], P(None, 'fsdp'), may hold values from -6 to 6
- w_gate: bfloat16 [4, 768, 2048], P('expert', None, 'fsdp'), may hold values from -0.21875 to 0.21875
- w_up: bfloat16 [4, 768, 2048], P('expert', None, 'fsdp'), may hold values from -0.21875 to 0.21875
- w_down: bfloat16 [4, 2048, 768], P('expert', 'fsdp'), may hold values from -1.5 to 1.5
- out_grad: bfloat16 [32, 1024, 768], P(('expert', 'fsdp')), may hold values from -6 to 6
Outputs:
- hidden_out: bfloat16 [32, 1024, 768], P(('expert', 'fsdp'))
- grad_hidden: float32 [32, 1024, 768], P(('expert', 'fsdp'))
- grad_prev: float32 [32, 1024, 8], P(('expert', 'fsdp'))
- grad_w_query: float32 [768, 768], P(None, 'fsdp')
- grad_w_key: float32 [768, 768], P(None, 'fsdp')
- grad_w_value: float32 [768, 768], P(None, 'fsdp')
- grad_w_output: float32 [768, 768], P('fsdp')
- grad_gain_attn: float32 [768], P('fsdp')
- grad_gain_moe: float32 [768], P('fsdp')
- grad_w_router: float32 [768, 8], P('fsdp')
- grad_w_gating: float32 [8, 8], replicated
- grad_w_const: float32 [768, 4], P('fsdp')
- grad_v_const: float32 [2, 768], P(None, 'fsdp')
- grad_w_gate: float32 [4, 768, 2048], P('expert', None, 'fsdp')
- grad_w_up: float32 [4, 768, 2048], P('expert', None, 'fsdp')
- grad_w_down: float32 [4, 2048, 768], P('expert', 'fsdp')
Inputs may be any that keep to these rules, and one draw needn't show every extreme that they name: `seq_lengths`: some sequence has all 1024 positions live. `seq_order`: A permutation: slot i takes a sequence whose slot of the same index along fsdp and the same place among a device's 1 slots differs from i at most in its index along expert. Each position names two different choices: ids below 4 are feed-forward experts, 4 the zero expert, 5 the copy expert, 6 and 7 the constant experts. Within the rows of one device no id is named by more than 256 routes, a bound that some block reaches.
All inputs are finite; a program needn't handle non-finite values.
Results may differ from a plain program's by a relative error of at most 0.022.
Values may be sent and summed in bfloat16 or wider, within the bound.
No kernel may reach another device: no remote copies, remote signals or barrier semaphores. Data moves between devices by JAX's collectives and lax.ppermute only.
A program may use at most 320 MiB of HBM per device.

v0:
```python
import jax
import jax.numpy as jnp
from jax import lax
from jax.sharding import PartitionSpec as P

HD = 64
CAP = 256


precise = lax.Precision.HIGHEST
norm_eps = 1e-05
rope_base = 10000.0
masked_score = -1e30


def rms_scale(values):
    return lax.rsqrt(jnp.mean(values * values, axis=-1, keepdims=True) + norm_eps)


def rope_tables(length, head_dim):
    half_dim = head_dim // 2
    inverse = rope_base ** (-(2.0 * jnp.arange(half_dim, dtype=jnp.float32)) / head_dim)
    angles = jnp.arange(length, dtype=jnp.float32)[:, None] * inverse[None, :]
    return (jnp.cos(angles), jnp.sin(angles))


def rotate(values, cosine, sine_table):
    half_dim = values.shape[-1] // 2
    front_half = values[..., :half_dim]
    back_half = values[..., half_dim:]
    cos_wide = cosine[:, None, :]
    sin_wide = sine_table[:, None, :]
    return jnp.concatenate(
        [
            front_half * cos_wide - back_half * sin_wide,
            back_half * cos_wide + front_half * sin_wide,
        ],
        axis=-1,
    )


def contract(left_side, right_side, left_dim, right_dim, exact_mode):
    return lax.dot_general(
        left_side,
        right_side,
        (((left_dim,), (right_dim,)), ((), ())),
        precision=precise if exact_mode else None,
        preferred_element_type=jnp.float32,
    )


def slot_tables(route_pairs, expert_count, capacity):
    flat_routes = route_pairs.reshape(-1)
    matches = (flat_routes[:, None] == jnp.arange(expert_count, dtype=jnp.int32)[None, :]).astype(
        jnp.int32
    )
    position = jnp.sum((jnp.cumsum(matches, axis=0) - 1) * matches, axis=1)
    is_expert = flat_routes < expert_count
    target = jnp.where(is_expert, flat_routes * capacity + position, expert_count * capacity)
    route_ids = jnp.arange(flat_routes.shape[0], dtype=jnp.int32)
    slot_route = (
        jnp.full((expert_count * capacity,), -1, jnp.int32).at[target].set(route_ids, mode="drop")
    )
    return (slot_route, jnp.where(is_expert, target, -1))


def block_mask(row_start, row_count, key_count, seq_length):
    query_pos = row_start + jnp.arange(row_count, dtype=jnp.int32)
    key_pos = jnp.arange(key_count, dtype=jnp.int32)
    return (key_pos[None, :] <= query_pos[:, None]) & (key_pos[None, :] < seq_length)


def block_scores(query_block, key_seq, allowed, factor):
    raw_scores = (
        jnp.einsum("qhd,khd->hqk", query_block, key_seq, preferred_element_type=jnp.float32)
        * factor
    )
    return jnp.where(allowed[None], raw_scores, masked_score)


def layer_pieces(gathered):
    (
        full_query,
        full_key,
        full_value,
        full_output,
        full_gain_one,
        full_gain_two,
        full_router,
        full_const,
        full_vectors,
    ) = gathered
    qkv_weights = jnp.concatenate([full_query, full_key, full_value], axis=1)
    small_weights = jnp.concatenate([full_router, full_const], axis=1).astype(jnp.float32)
    return (
        qkv_weights,
        full_output,
        full_gain_one.astype(jnp.float32),
        full_gain_two.astype(jnp.float32),
        small_weights,
        full_vectors.astype(jnp.float32),
    )


def expert_pieces(gathered):
    return (jnp.concatenate([gathered[0][0], gathered[1][0]], axis=1), gathered[2][0])


def spread_rows(values, target_hot):
    return jnp.where(target_hot[:, :, None, None], values[None], jnp.zeros((), values.dtype))


def choose_rows(stacked, source_hot):
    return jnp.sum(
        jnp.where(source_hot[:, :, None, None], stacked, jnp.zeros((), stacked.dtype)), axis=0
    ).astype(stacked.dtype)


def per_device(
    hidden_in,
    prev_logits,
    seq_lengths,
    seq_order,
    routes,
    w_query,
    w_key,
    w_value,
    w_output,
    gain_attn,
    gain_moe,
    w_router,
    w_gating,
    w_const,
    v_const,
    w_gate,
    w_up,
    w_down,
    out_grad,
):
    seq_count, length, model_width = hidden_in.shape
    row_count = seq_count * length
    head_count = model_width // HD
    expert_count = lax.axis_size("expert")
    fsdp_count = lax.axis_size("fsdp")
    route_width = w_router.shape[1]
    block_rows = min(512, length)
    factor = HD ** (-0.5)
    place_ids = jnp.arange(seq_count, dtype=jnp.int32)
    expert_ids = jnp.arange(expert_count, dtype=jnp.int32)
    fsdp_here = lax.axis_index("fsdp")
    own_slots = (lax.axis_index("expert") * fsdp_count + fsdp_here) * seq_count + place_ids
    dealt_ids = seq_order[own_slots]
    source_index = dealt_ids // seq_count // fsdp_count
    source_hot = source_index[None, :] == expert_ids[:, None]
    peer_slots = (expert_ids[:, None] * fsdp_count + fsdp_here) * seq_count + place_ids[None, :]
    target_hot = seq_order[peer_slots] == own_slots[None, :]
    dealt_lengths = seq_lengths[dealt_ids]
    dealt_parts = (
        lax.all_to_all(
            spread_rows(hidden_in, target_hot), "expert", split_axis=0, concat_axis=0, tiled=True
        ),
        lax.all_to_all(
            spread_rows(out_grad, target_hot), "expert", split_axis=0, concat_axis=0, tiled=True
        ),
        lax.all_to_all(
            spread_rows(prev_logits, target_hot), "expert", split_axis=0, concat_axis=0, tiled=True
        ),
    )
    hidden_dealt = choose_rows(dealt_parts[0], source_hot)
    grad_dealt = choose_rows(dealt_parts[1], source_hot)
    prev_dealt = choose_rows(dealt_parts[2], source_hot)
    layer_parts = (
        lax.all_gather(w_query, "fsdp", axis=1, tiled=True),
        lax.all_gather(w_key, "fsdp", axis=1, tiled=True),
        lax.all_gather(w_value, "fsdp", axis=1, tiled=True),
        lax.all_gather(w_output, "fsdp", axis=0, tiled=True),
        lax.all_gather(gain_attn, "fsdp", axis=0, tiled=True),
        lax.all_gather(gain_moe, "fsdp", axis=0, tiled=True),
        lax.all_gather(w_router, "fsdp", axis=0, tiled=True),
        lax.all_gather(w_const, "fsdp", axis=0, tiled=True),
        lax.all_gather(v_const, "fsdp", axis=1, tiled=True),
    )
    qkv_weights, out_weights, gain_one, gain_two, small_weights, const_vectors = layer_pieces(
        layer_parts
    )
    hidden = hidden_dealt.reshape(row_count, model_width).astype(jnp.float32)
    scale_one = rms_scale(hidden)
    unit_one = hidden * scale_one
    normed_one = (unit_one * gain_one).astype(jnp.bfloat16)
    projected = jnp.dot(normed_one, qkv_weights, preferred_element_type=jnp.float32)
    cosine, sine_table = rope_tables(length, HD)
    heads_shape = (seq_count, length, head_count, HD)
    query_low = rotate(projected[:, :model_width].reshape(heads_shape), cosine, sine_table).astype(
        jnp.bfloat16
    )
    key_low = rotate(
        projected[:, model_width : 2 * model_width].reshape(heads_shape), cosine, sine_table
    ).astype(jnp.bfloat16)
    value_low = projected[:, 2 * model_width :].reshape(heads_shape).astype(jnp.bfloat16)
    attended_parts = []
    log_norms = []
    seq_index = 0
    seq_length = dealt_lengths[seq_index]
    for block_start in range(0, length, block_rows):
        allowed = block_mask(block_start, block_rows, length, seq_length)
        scores = block_scores(
            query_low[seq_index, block_start : block_start + block_rows],
            key_low[seq_index],
            allowed,
            factor,
        )
        top_score = jnp.max(scores, axis=-1, keepdims=True)
        expo_scores = jnp.exp(scores - top_score)
        total_mass = jnp.sum(expo_scores, axis=-1, keepdims=True)
        probs_low = (expo_scores / total_mass).astype(jnp.bfloat16)
        log_norms.append(top_score + jnp.log(total_mass))
        attended_parts.append(
            jnp.einsum(
                "hqk,khd->qhd", probs_low, value_low[seq_index], preferred_element_type=jnp.float32
            ).astype(jnp.bfloat16)
        )
    attended = jnp.concatenate(attended_parts, axis=0).reshape(row_count, model_width)
    residual = hidden + jnp.dot(attended, out_weights, preferred_element_type=jnp.float32)
    scale_two = rms_scale(residual)
    unit_two = residual * scale_two
    normed_two = unit_two * gain_two
    normed_low = normed_two.astype(jnp.bfloat16)
    prev_flat = prev_dealt.reshape(row_count, route_width).astype(jnp.float32)
    gating_weights = w_gating.astype(jnp.float32)
    small_out = contract(normed_two, small_weights, 1, 0, True)
    logits = small_out[:, :route_width] + contract(prev_flat, gating_weights, 1, 0, True)
    router_probs = jax.nn.softmax(logits, axis=-1)
    route_pairs = routes.reshape(row_count, 2)
    route_hits = (
        route_pairs[:, :, None] == jnp.arange(route_width, dtype=jnp.int32)[None, None, :]
    ).astype(jnp.float32)
    gate_values = jnp.sum(route_hits * router_probs[:, None, :], axis=-1)
    const_weights = jax.nn.softmax(small_out[:, route_width:].reshape(row_count, 2, 2), axis=-1)
    const_rows = (
        const_weights[:, :, 0:1] * normed_two[:, None, :]
        + const_weights[:, :, 1:2] * const_vectors[None, :, :]
    )
    expert_parts = (
        lax.all_gather(w_gate, "fsdp", axis=2, tiled=True),
        lax.all_gather(w_up, "fsdp", axis=2, tiled=True),
        lax.all_gather(w_down, "fsdp", axis=1, tiled=True),
    )
    joint_weights, down_weights = expert_pieces(expert_parts)
    slot_route, route_slot = slot_tables(route_pairs, expert_count, CAP)
    send_rows = jnp.where(
        slot_route[:, None] >= 0,
        normed_low[jnp.maximum(slot_route, 0) // 2],
        jnp.zeros((), jnp.bfloat16),
    )
    received = lax.all_to_all(
        send_rows.reshape(expert_count, CAP, model_width),
        "expert",
        split_axis=0,
        concat_axis=0,
        tiled=True,
    )
    expert_in = received.reshape(expert_count * CAP, model_width)
    joint_linear = jnp.dot(expert_in, joint_weights, preferred_element_type=jnp.float32)
    hidden_units = joint_weights.shape[1] // 2
    gate_linear = joint_linear[:, :hidden_units]
    up_linear = joint_linear[:, hidden_units:]
    gate_sig = jax.nn.sigmoid(gate_linear)
    gate_act = gate_linear * gate_sig
    inner_low = (gate_act * up_linear).astype(jnp.bfloat16)
    expert_out = jnp.dot(inner_low, down_weights, preferred_element_type=jnp.float32).astype(
        jnp.bfloat16
    )
    returned = lax.all_to_all(
        expert_out.reshape(expert_count, CAP, model_width),
        "expert",
        split_axis=0,
        concat_axis=0,
        tiled=True,
    )
    returned_flat = returned.reshape(expert_count * CAP, model_width)
    expert_part = jnp.where(
        route_slot[:, None] >= 0, returned_flat[jnp.maximum(route_slot, 0)].astype(jnp.float32), 0.0
    ).reshape(row_count, 2, model_width)
    picked = route_pairs[:, :, None]
    route_out = expert_part + jnp.where(picked == expert_count + 1, normed_two[:, None, :], 0.0)
    route_out = route_out + jnp.where(picked == expert_count + 2, const_rows[:, 0:1, :], 0.0)
    route_out = route_out + jnp.where(picked == expert_count + 3, const_rows[:, 1:2, :], 0.0)
    mixed_out = residual + jnp.sum(gate_values[:, :, None] * route_out, axis=1)
    hidden_out = mixed_out.astype(jnp.bfloat16).reshape(seq_count, length, model_width)
    layer_back = (
        lax.all_gather(w_query, "fsdp", axis=1, tiled=True),
        lax.all_gather(w_key, "fsdp", axis=1, tiled=True),
        lax.all_gather(w_value, "fsdp", axis=1, tiled=True),
        lax.all_gather(w_output, "fsdp", axis=0, tiled=True),
        lax.all_gather(gain_attn, "fsdp", axis=0, tiled=True),
        lax.all_gather(gain_moe, "fsdp", axis=0, tiled=True),
        lax.all_gather(w_router, "fsdp", axis=0, tiled=True),
        lax.all_gather(w_const, "fsdp", axis=0, tiled=True),
        lax.all_gather(v_const, "fsdp", axis=1, tiled=True),
    )
    expert_back = (
        lax.all_gather(w_gate, "fsdp", axis=2, tiled=True),
        lax.all_gather(w_up, "fsdp", axis=2, tiled=True),
        lax.all_gather(w_down, "fsdp", axis=1, tiled=True),
    )
    qkv_back, out_back, gain_one_back, gain_two_back, small_back, vectors_back = layer_pieces(
        layer_back
    )
    joint_back, down_back = expert_pieces(expert_back)
    grad_mixed = grad_dealt.reshape(row_count, model_width).astype(jnp.float32)
    grad_gates = jnp.sum(grad_mixed[:, None, :] * route_out, axis=-1)
    route_grad = gate_values[:, :, None] * grad_mixed[:, None, :]
    flat_grad = route_grad.reshape(2 * row_count, model_width)
    send_grad = jnp.where(
        slot_route[:, None] >= 0, flat_grad[jnp.maximum(slot_route, 0)], 0.0
    ).astype(jnp.bfloat16)
    grad_received = lax.all_to_all(
        send_grad.reshape(expert_count, CAP, model_width),
        "expert",
        split_axis=0,
        concat_axis=0,
        tiled=True,
    )
    grad_expert_out = grad_received.reshape(expert_count * CAP, model_width)
    grad_down = contract(inner_low, grad_expert_out, 0, 0, False)
    grad_inner = contract(grad_expert_out, down_back, 1, 1, False)
    grad_joint = jnp.concatenate(
        [
            grad_inner * up_linear * gate_sig * (1.0 + gate_linear * (1.0 - gate_sig)),
            grad_inner * gate_act,
        ],
        axis=1,
    ).astype(jnp.bfloat16)
    grad_joint_w = contract(expert_in, grad_joint, 0, 0, False)
    grad_expert_in = contract(grad_joint, joint_back, 1, 1, False).astype(jnp.bfloat16)
    grad_returned = lax.all_to_all(
        grad_expert_in.reshape(expert_count, CAP, model_width),
        "expert",
        split_axis=0,
        concat_axis=0,
        tiled=True,
    )
    grad_returned_flat = grad_returned.reshape(expert_count * CAP, model_width)
    grad_from_experts = jnp.where(
        route_slot[:, None] >= 0,
        grad_returned_flat[jnp.maximum(route_slot, 0)].astype(jnp.float32),
        0.0,
    ).reshape(row_count, 2, model_width)
    copy_grad = jnp.sum(jnp.where(picked == expert_count + 1, route_grad, 0.0), axis=1)
    const_grad = jnp.stack(
        [
            jnp.sum(jnp.where(picked == expert_count + 2 + const_index, route_grad, 0.0), axis=1)
            for const_index in range(2)
        ],
        axis=1,
    )
    grad_const_mix = jnp.stack(
        [
            jnp.sum(const_grad * normed_two[:, None, :], axis=-1),
            jnp.sum(const_grad * vectors_back[None, :, :], axis=-1),
        ],
        axis=-1,
    )
    grad_const_logits = const_weights * (
        grad_const_mix - jnp.sum(const_weights * grad_const_mix, axis=-1, keepdims=True)
    )
    grad_vectors = jnp.sum(const_weights[:, :, 1:2] * const_grad, axis=0)
    grad_probs = jnp.sum(route_hits * grad_gates[:, :, None], axis=1)
    grad_logits = router_probs * (
        grad_probs - jnp.sum(router_probs * grad_probs, axis=-1, keepdims=True)
    )
    grad_small = jnp.concatenate([grad_logits, grad_const_logits.reshape(row_count, 4)], axis=1)
    grad_small_w = contract(normed_two, grad_small, 0, 0, True)
    grad_gating = contract(prev_flat, grad_logits, 0, 0, True)
    grad_prev = contract(grad_logits, gating_weights, 1, 1, True)
    grad_normed_two = (
        jnp.sum(grad_from_experts, axis=1)
        + copy_grad
        + jnp.sum(const_weights[:, :, 0:1] * const_grad, axis=1)
        + contract(grad_small, small_back, 1, 1, True)
    )
    grad_gain_two = jnp.sum(grad_normed_two * unit_two, axis=0)
    scaled_two = grad_normed_two * gain_two_back
    grad_residual = grad_mixed + scale_two * (
        scaled_two - unit_two * jnp.mean(scaled_two * unit_two, axis=-1, keepdims=True)
    )
    grad_attn_low = grad_residual.astype(jnp.bfloat16)
    grad_out_w = contract(attended, grad_attn_low, 0, 0, False)
    grad_attended = (
        contract(grad_attn_low, out_back, 1, 1, False).astype(jnp.bfloat16).reshape(heads_shape)
    )
    grad_query_parts = []
    norm_index = 0
    seq_index = 0
    seq_length = dealt_lengths[seq_index]
    key_grad = jnp.zeros((length, head_count, HD), jnp.float32)
    value_grad = jnp.zeros((length, head_count, HD), jnp.float32)
    for block_start in range(0, length, block_rows):
        allowed = block_mask(block_start, block_rows, length, seq_length)
        query_block = query_low[seq_index, block_start : block_start + block_rows]
        scores = block_scores(query_block, key_low[seq_index], allowed, factor)
        block_probs = jnp.exp(scores - log_norms[norm_index])
        norm_index = norm_index + 1
        grad_block = grad_attended[seq_index, block_start : block_start + block_rows]
        grad_probs_attn = jnp.einsum(
            "qhd,khd->hqk", grad_block, value_low[seq_index], preferred_element_type=jnp.float32
        )
        grad_scores = (
            block_probs
            * (grad_probs_attn - jnp.sum(block_probs * grad_probs_attn, axis=-1, keepdims=True))
        ).astype(jnp.bfloat16)
        grad_query_parts.append(
            jnp.einsum(
                "hqk,khd->qhd", grad_scores, key_low[seq_index], preferred_element_type=jnp.float32
            )
            * factor
        )
        key_grad = (
            key_grad
            + jnp.einsum(
                "hqk,qhd->khd", grad_scores, query_block, preferred_element_type=jnp.float32
            )
            * factor
        )
        value_grad = value_grad + jnp.einsum(
            "hqk,qhd->khd",
            block_probs.astype(jnp.bfloat16),
            grad_block,
            preferred_element_type=jnp.float32,
        )
    grad_key_parts = [key_grad]
    grad_value_parts = [value_grad]
    grad_query = rotate(
        jnp.concatenate(grad_query_parts, axis=0).reshape(heads_shape), cosine, -sine_table
    ).reshape(row_count, model_width)
    grad_key = rotate(jnp.stack(grad_key_parts, axis=0), cosine, -sine_table).reshape(
        row_count, model_width
    )
    grad_value = jnp.stack(grad_value_parts, axis=0).reshape(row_count, model_width)
    grad_qkv = jnp.concatenate([grad_query, grad_key, grad_value], axis=1).astype(jnp.bfloat16)
    grad_qkv_w = contract(normed_one, grad_qkv, 0, 0, False)
    grad_normed_one = contract(grad_qkv, qkv_back, 1, 1, False)
    grad_gain_one = jnp.sum(grad_normed_one * unit_one, axis=0)
    scaled_one = grad_normed_one * gain_one_back
    grad_hidden = grad_residual + scale_one * (
        scaled_one - unit_one * jnp.mean(scaled_one * unit_one, axis=-1, keepdims=True)
    )
    shared_terms = (
        grad_qkv_w[:, :model_width],
        grad_qkv_w[:, model_width : 2 * model_width],
        grad_qkv_w[:, 2 * model_width :],
        grad_out_w,
        grad_gain_one,
        grad_gain_two,
        grad_small_w[:, :route_width],
        grad_small_w[:, route_width:],
        grad_vectors,
    )
    shared_scattered = (
        lax.psum_scatter(
            shared_terms[0].astype(jnp.bfloat16), "fsdp", scatter_dimension=1, tiled=True
        ).astype(jnp.float32),
        lax.psum_scatter(
            shared_terms[1].astype(jnp.bfloat16), "fsdp", scatter_dimension=1, tiled=True
        ).astype(jnp.float32),
        lax.psum_scatter(
            shared_terms[2].astype(jnp.bfloat16), "fsdp", scatter_dimension=1, tiled=True
        ).astype(jnp.float32),
        lax.psum_scatter(
            shared_terms[3].astype(jnp.bfloat16), "fsdp", scatter_dimension=0, tiled=True
        ).astype(jnp.float32),
        lax.psum_scatter(
            shared_terms[4].astype(jnp.bfloat16), "fsdp", scatter_dimension=0, tiled=True
        ).astype(jnp.float32),
        lax.psum_scatter(
            shared_terms[5].astype(jnp.bfloat16), "fsdp", scatter_dimension=0, tiled=True
        ).astype(jnp.float32),
        lax.psum_scatter(
            shared_terms[6].astype(jnp.bfloat16), "fsdp", scatter_dimension=0, tiled=True
        ).astype(jnp.float32),
        lax.psum_scatter(
            shared_terms[7].astype(jnp.bfloat16), "fsdp", scatter_dimension=0, tiled=True
        ).astype(jnp.float32),
        lax.psum_scatter(
            shared_terms[8].astype(jnp.bfloat16), "fsdp", scatter_dimension=1, tiled=True
        ).astype(jnp.float32),
    )
    shared_total = (
        lax.psum(shared_scattered[0].astype(jnp.bfloat16), "expert").astype(jnp.float32),
        lax.psum(shared_scattered[1].astype(jnp.bfloat16), "expert").astype(jnp.float32),
        lax.psum(shared_scattered[2].astype(jnp.bfloat16), "expert").astype(jnp.float32),
        lax.psum(shared_scattered[3].astype(jnp.bfloat16), "expert").astype(jnp.float32),
        lax.psum(shared_scattered[4].astype(jnp.bfloat16), "expert").astype(jnp.float32),
        lax.psum(shared_scattered[5].astype(jnp.bfloat16), "expert").astype(jnp.float32),
        lax.psum(shared_scattered[6].astype(jnp.bfloat16), "expert").astype(jnp.float32),
        lax.psum(shared_scattered[7].astype(jnp.bfloat16), "expert").astype(jnp.float32),
        lax.psum(shared_scattered[8].astype(jnp.bfloat16), "expert").astype(jnp.float32),
    )
    gating_total = lax.psum(grad_gating, ("expert", "fsdp"))
    expert_grads = (
        lax.psum_scatter(
            grad_joint_w[None, :, :hidden_units].astype(jnp.bfloat16),
            "fsdp",
            scatter_dimension=2,
            tiled=True,
        ).astype(jnp.float32),
        lax.psum_scatter(
            grad_joint_w[None, :, hidden_units:].astype(jnp.bfloat16),
            "fsdp",
            scatter_dimension=2,
            tiled=True,
        ).astype(jnp.float32),
        lax.psum_scatter(
            grad_down[None].astype(jnp.bfloat16), "fsdp", scatter_dimension=1, tiled=True
        ).astype(jnp.float32),
    )
    slot_results = (
        hidden_out.astype(jnp.float32),
        grad_hidden.reshape(seq_count, length, model_width),
        grad_prev.reshape(seq_count, length, route_width),
    )
    back_parts = (
        lax.all_to_all(
            spread_rows(slot_results[0], source_hot).astype(jnp.bfloat16),
            "expert",
            split_axis=0,
            concat_axis=0,
            tiled=True,
        ).astype(jnp.float32),
        lax.all_to_all(
            spread_rows(slot_results[1], source_hot).astype(jnp.bfloat16),
            "expert",
            split_axis=0,
            concat_axis=0,
            tiled=True,
        ).astype(jnp.float32),
        lax.all_to_all(
            spread_rows(slot_results[2], source_hot).astype(jnp.bfloat16),
            "expert",
            split_axis=0,
            concat_axis=0,
            tiled=True,
        ).astype(jnp.float32),
    )
    hidden_final = choose_rows(back_parts[0], target_hot).astype(jnp.bfloat16)
    grad_hidden_final = choose_rows(back_parts[1], target_hot)
    grad_prev_final = choose_rows(back_parts[2], target_hot)
    return (
        hidden_final,
        grad_hidden_final,
        grad_prev_final,
        shared_total[0],
        shared_total[1],
        shared_total[2],
        shared_total[3],
        shared_total[4],
        shared_total[5],
        shared_total[6],
        gating_total,
        shared_total[7],
        shared_total[8],
        expert_grads[0],
        expert_grads[1],
        expert_grads[2],
    )


def solution(mesh):
    placed = (
        P(("expert", "fsdp"), None, None),
        P(("expert", "fsdp"), None, None),
        P(),
        P(),
        P(("expert", "fsdp"), None, None),
        P(None, "fsdp"),
        P(None, "fsdp"),
        P(None, "fsdp"),
        P("fsdp", None),
        P("fsdp"),
        P("fsdp"),
        P("fsdp", None),
        P(),
        P("fsdp", None),
        P(None, "fsdp"),
        P("expert", None, "fsdp"),
        P("expert", None, "fsdp"),
        P("expert", "fsdp", None),
        P(("expert", "fsdp"), None, None),
    )
    return jax.shard_map(
        per_device,
        mesh=mesh,
        in_specs=placed,
        out_specs=(
            P(("expert", "fsdp"), None, None),
            P(("expert", "fsdp"), None, None),
            P(("expert", "fsdp"), None, None),
            P(None, "fsdp"),
            P(None, "fsdp"),
            P(None, "fsdp"),
            P("fsdp", None),
            P("fsdp"),
            P("fsdp"),
            P("fsdp", None),
            P(),
            P("fsdp", None),
            P(None, "fsdp"),
            P("expert", None, "fsdp"),
            P("expert", None, "fsdp"),
            P("expert", "fsdp", None),
        ),
        check_vma=False,
    )
```

profile of v0, /device:TPU:0, one launch (start us, length us, event | category | flops | bytes accessed | tf_op | source)
XLA Modules:
  0.0 1619.2 jit_solution(2051622164510212728)
XLA Ops:
  16.4 8.0 scatter_custom_fusion
  30.7 6.9 broadcast_select_fusion.1
  44.1 70.1 %all-to-all-done = bf16[4,1,1024,768]{3,2,1,0:T(8,128)(2,1)} async-done(((bf16[4,1,1024,768]{3,2,1,0:T(8,128)(2,1)}), bf16[4,1,1024,768]{3,2,1,0:T(8,128)(2,1)}, u32[]{:S(2)}, u32[]{:S(2)}) %all-to-all-start) | async-done | bytes 6291488 | tf_op jit(solution)/shard_map/all_to_all | solution.py:159
  127.1 22.3 %all-reduce.5 = (bf16[768]{0:T(1024)(128)(2,1)S(1)}, bf16[768]{0:T(1024)(128)(2,1)S(1)}) all-reduce(bf16[768]{0:T(1024)(128)(2,1)S(1)} %dynamic-update-slice.2, bf16[768]{0:T(1024)(128)(2,1)S(1)} %dynamic-update-slice.3), channel_id=1, replica_groups=mesh['expert'=4,'fsdp'=8] {'fsdp'}, use_global_device_ids=true, to_apply=%add | all-reduce | flops 1536 | bytes 6144
  150.0 16.2 %all-gather.2 = bf16[8,96,2]{1,2,0:T(2,128)(2,1)S(1)} all-gather(bf16[1,96,2]{1,2,0:T(2,128)(2,1)S(1)} %bitcast.245), channel_id=1, replica_groups=mesh['expert'=4,'fsdp'=8] {'fsdp'}, dimensions={0}, use_global_device_ids=true | all-gather | bytes 3456 | tf_op jit(solution)/shard_map/all_gather | solution.py:181
  166.9 18.2 %all-gather.1 = bf16[8,96,4]{1,2,0:T(4,128)(2,1)S(1)} all-gather(bf16[1,96,4]{1,2,0:T(4,128)(2,1)S(1)} %bitcast.244), channel_id=1, replica_groups=mesh['expert'=4,'fsdp'=8] {'fsdp'}, dimensions={0}, use_global_device_ids=true | all-gather | bytes 6912 | tf_op jit(solution)/shard_map/all_gather | solution.py:180
  185.2 26.3 %all-gather = bf16[8,96,8]{1,2,0:T(8,128)(2,1)S(1)} all-gather(bf16[1,96,8]{1,2,0:T(8,128)(2,1)S(1)} %bitcast.243), channel_id=1, replica_groups=mesh['expert'=4,'fsdp'=8] {'fsdp'}, dimensions={0}, use_global_device_ids=true | all-gather | bytes 13824 | tf_op jit(solution)/shard_map/all_gather | solution.py:179
  228.9 10.2 select_reduce_fusion.3
  241.4 6.3 fusion.63
  265.6 11.4 fusion.14
  277.0 14.6 fusion.13
  291.6 13.3 fusion.2
  305.0 8.5 fusion.50
  313.5 14.0 fusion.1
  329.5 8.0 fusion.49
  353.1 8.7 mul.644
  384.9 8.1 multiply_add_fusion
  396.3 9.4 fusion.24
  415.2 7.7 fusion.42
  426.9 12.6 fusion.108
  450.0 8.6 broadcast_in_dim.452
  458.6 6.8 broadcast_in_dim.431
  465.3 8.5 broadcast_in_dim.449
  473.9 6.9 broadcast_in_dim.428
  480.8 8.7 broadcast_in_dim.446
  489.8 9.4 gather_fusion.2
  499.3 10.1 multiply_reduce_fusion.5
  521.9 23.1 %all_to_all.50 = bf16[4,256,768]{2,1,0:T(8,128)(2,1)S(1)} all-to-all(bf16[4,256,768]{2,1,0:T(8,128)(2,1)S(1)} %select_convert_fusion.2), channel_id=1, replica_groups=mesh['expert'=4,'fsdp'=8] {'expert'}, dimensions={0} | all-to-all | bytes 3145728 | tf_op jit(solution)/shard_map/all_to_all | solution.py:317
  545.0 12.3 multiply_convert_fusion.3
  557.4 11.3 fusion.45
  575.0 8.0 reshape.722
  583.6 8.8 all-to-all-done.7
  592.5 9.5 gather_fusion.4
  602.0 7.9 reshape.723
  609.9 60.9 %fusion.16 = (f32[1024,768]{1,0:T(8,128)}, f32[1024,768]{1,0:T(8,128)}, f32[1024,768]{1,0:T(8,128)}, f32[1024,768]{1,0:T(8,128)}, f32[1024,768]{1,0:T(8,128)}) fusion(pred[1024,2]{1,0:T(8,128)(4,1)S(1)} %copy-done.49, f32[1024,768]{1,0:T(8,128)} %copy-done.6, f32[1024,2]{1,0:T(8,128)} %copy-done.35, pred[1024,2]{1,0:T(8,128)(4,1)S(1)} %copy-done.47, ...), kind=kLoop, calls=%fused_computation.45 | loop fusion | flops 24379392 | bytes 40910848 | tf_op jit(solution)/shard_map/reduce_sum | solution.py:349
  685.9 25.7 %multiply_reduce_fusion.2 = (bf16[2,768]{1,0:T(2,128)(2,1)}, f32[1024,2]{1,0:T(8,128)}, f32[1024,2]{1,0:T(8,128)}, f32[1024,768]{1,0:T(8,128)}) fusion(f32[1024,2]{1,0:T(8,128)} %bitcast.211, f32[1024,1,768]{2,1,0:T(1,128)} %stack.22, f32[1024,1,768]{2,1,0:T(1,128)} %stack.21, f32[1024,768]{1,0:T(8,128)S(1)} %copy-done.4, f32[2,768]{1,0:T(2,128)S(1)} %bitcast.236, ...), kind=kLoop, calls=%fused_computation.50 | loop fusion | flops 13363712 | bytes 12624896 | tf_op jit(solution)/shard_map/reduce_sum | solution.py:367
  724.9 7.0 multiply_reduce_fusion.8
  736.8 13.2 fusion.5
  750.0 18.1 %multiply_reduce_fusion = (f32[12,512]{1,0:T(8,128)S(1)}, f32[12,512,1024]{2,1,0:T(8,128)}) fusion(f32[12,512]{1,0:T(8,128)S(1)} %copy-done.56, f32[12,512,1024]{2,1,0:T(8,128)} %get-tuple-element.215, pred[512,1024]{1,0:T(8,128)(4,1)S(1)} %copy-done.18, bf16[1024,12,64]{0,2,1:T(8,128)(2,1)S(1)} %bitcast.198, bf16[1,1024,12,64]{1,3,2,0:T(8,128)(2,1)} %bitcast.227), kind=kOutput, calls=%fused_computation.8 | convolution fusion | flops 836757504 | bytes 53264384 | tf_op jit(solution)/shard_map/qhd,khd->hqk/dot_general | solution.py:405
  768.1 17.9 %multiply_reduce_fusion.1 = (f32[12,512]{1,0:T(8,128)S(1)}, f32[12,512,1024]{2,1,0:T(8,128)}) fusion(f32[12,512]{1,0:T(8,128)S(1)} %copy-done.57, f32[12,512,1024]{2,1,0:T(8,128)} %get-tuple-element.217, pred[512,1024]{1,0:T(8,128)(4,1)S(1)} %copy-done.33, bf16[1024,12,64]{0,2,1:T(8,128)(2,1)S(1)} %bitcast.199, bf16[1,1024,12,64]{1,3,2,0:T(8,128)(2,1)} %bitcast.228), kind=kOutput, calls=%fused_computation.11 | convolution fusion | flops 836757504 | bytes 53264384 | tf_op jit(solution)/shard_map/qhd,khd->hqk/dot_general | solution.py:405
  786.0 21.8 %multiply_convert_fusion.1 = bf16[12,512,1024]{2,1,0:T(8,128)(2,1)} fusion(f32[12,512,1024]{2,1,0:T(8,128)} %get-tuple-element.226, f32[12,512]{1,0:T(8,128)S(1)} %get-tuple-element.225, f32[12,512]{1,0:T(8,128)S(1)} %copy-done.57, f32[12,512,1024]{2,1,0:T(8,128)} %get-tuple-element.217, pred[512,1024]{1,0:T(8,128)(4,1)S(1)} %copy-done.33), kind=kLoop, calls=%fused_computation.10 | loop fusion | flops 37748736 | bytes 63488000 | tf_op jit(solution)/shard_map/convert_element_type | solution.py:411
  807.9 8.6 multiply_bitcast_fusion.2
  816.5 7.0 fusion.103
  823.5 13.8 add_convert_fusion
  837.3 21.6 %multiply_convert_fusion = bf16[12,512,1024]{2,1,0:T(8,128)(2,1)} fusion(f32[12,512,1024]{2,1,0:T(8,128)} %get-tuple-element.224, f32[12,512]{1,0:T(8,128)S(1)} %get-tuple-element.223, f32[12,512]{1,0:T(8,128)S(1)} %copy-done.56, f32[12,512,1024]{2,1,0:T(8,128)} %get-tuple-element.215, pred[512,1024]{1,0:T(8,128)(4,1)S(1)} %copy-done.18), kind=kLoop, calls=%fused_computation.7 | loop fusion | flops 37748736 | bytes 63488000 | tf_op jit(solution)/shard_map/convert_element_type | solution.py:411
  858.9 8.5 multiply_bitcast_fusion.1
  867.4 6.9 multiply_bitcast_fusion
  879.3 7.1 convolution_convert_fusion.1
  902.1 46.8 %reduce-scatter.35.cloned.1.call-done = bf16[96,768]{1,0:T(8,128)(2,1)} async-done(((bf16[768,768]{1,0:T(8,128)(2,1)}), bf16[96,768]{1,0:T(8,128)(2,1)}) %reduce-scatter.35.cloned.1.call-update) | async-done | bytes 147472
  950.6 64.8 %reduce-scatter.33.cloned.1.call-done = bf16[96,768]{1,0:T(8,128)(2,1)} async-done(((bf16[768,768]{1,0:T(8,128)(2,1)}), bf16[96,768]{1,0:T(8,128)(2,1)}) %reduce-scatter.33.cloned.1.call-update) | async-done | bytes 147472
  1017.1 64.6 %reduce-scatter.31.cloned.1.call-done = bf16[96,768]{1,0:T(8,128)(2,1)} async-done(((bf16[768,768]{1,0:T(8,128)(2,1)}), bf16[96,768]{1,0:T(8,128)(2,1)}) %reduce-scatter.31.cloned.1.call-update) | async-done | bytes 147472
  1083.4 64.7 %reduce-scatter.23.cloned.1.call-done = bf16[96,768]{1,0:T(8,128)(2,1)} async-done(((bf16[768,768]{1,0:T(8,128)(2,1)}), bf16[96,768]{1,0:T(8,128)(2,1)}) %reduce-scatter.23.cloned.1.call-update) | async-done | bytes 147472 | tf_op jit(solution)/shard_map/reduce_scatter | solution.py:469
  1148.2 7.9 fusion.36
  1161.0 10.7 convolution_convert_fusion
  1176.9 7.4 fusion.30
  1188.1 6.6 select_convert_fusion.1
  1200.6 70.1 %all-to-all-done.4 = bf16[4,1,1024,768]{3,2,1,0:T(8,128)(2,1)} async-done(((bf16[4,1,1024,768]{3,2,1,0:T(8,128)(2,1)}), bf16[4,1,1024,768]{3,2,1,0:T(8,128)(2,1)}, u32[]{:S(2)}, u32[]{:S(2)}) %all-to-all-start.4) | async-done | bytes 6291488 | tf_op jit(solution)/shard_map/all_to_all | solution.py:523
  1276.8 102.1 %psum.77 = f32[8,8]{1,0:T(8,128)} all-reduce(f32[8,8]{1,0:T(8,128)S(1)} %fusion.115), channel_id=1, replica_groups=mesh['expert'=4,'fsdp'=8] {'expert','fsdp'}, use_global_device_ids=true, to_apply=%region_53.54 | all-reduce | flops 64 | bytes 512 | tf_op jit(solution)/shard_map/psum | solution.py:499
  1379.7 21.6 %all-reduce.4 = (bf16[768]{0:T(1024)(128)(2,1)S(1)}, bf16[768]{0:T(1024)(128)(2,1)S(1)}) all-reduce(bf16[768]{0:T(1024)(128)(2,1)S(1)} %get-tuple-element.140, bf16[768]{0:T(1024)(128)(2,1)S(1)} %copy-done.104), channel_id=6, replica_groups=mesh['expert'=4,'fsdp'=8] {'fsdp'}, use_global_device_ids=true, to_apply=%region_46.47.clone | all-reduce | flops 1536 | bytes 6144
  1403.9 6.4 all-reduce.6
  1420.0 10.2 select_reduce_fusion
  1430.2 24.7 %reduce-scatter.29.cloned.1.call-done = bf16[1,256,768]{2,1,0:T(8,128)(2,1)} async-done(((bf16[1,2048,768]{2,1,0:T(8,128)(2,1)}), bf16[1,256,768]{2,1,0:T(8,128)(2,1)}) %reduce-scatter.29.cloned.1.call-update) | async-done | bytes 393232 | tf_op jit(solution)/shard_map/reduce_scatter | solution.py:513
  1456.8 75.8 %reduce-scatter.25.cloned.1.call-done = bf16[1,768,256]{2,1,0:T(8,128)(2,1)} async-done(((bf16[1,768,2048]{2,1,0:T(8,128)(2,1)}), bf16[1,768,256]{2,1,0:T(8,128)(2,1)}) %reduce-scatter.25.cloned.1.call-update) | async-done | bytes 393232 | tf_op jit(solution)/shard_map/reduce_scatter | solution.py:501
  1534.5 75.6 %reduce-scatter.27.cloned.1.call-done = bf16[1,768,256]{2,1,0:T(8,128)(2,1)} async-done(((bf16[1,768,2048]{2,1,0:T(8,128)(2,1)}), bf16[1,768,256]{2,1,0:T(8,128)(2,1)}) %reduce-scatter.27.cloned.1.call-update) | async-done | bytes 393232 | tf_op jit(solution)/shard_map/reduce_scatter | solution.py:507
  (478 shorter events, 258.8 us)
Async XLA Ops:
  7.2 482.3 %copy-start = (bf16[8,8]{1,0:T(8,128)(2,1)S(1)}, bf16[8,8]{1,0:T(8,128)(2,1)}, u32[]{:S(2)}) copy-start(bf16[8,8]{1,0:T(8,128)(2,1)} %param.31) | copy-start | bytes 388
  7.2 17.9 %copy-start.1 = (s32[32]{0:T(128)S(1)}, s32[32]{0:T(128)}, u32[]{:S(2)}) copy-start(s32[32]{0:T(128)} %param.22) | copy-start | bytes 388
  7.2 18.6 %copy-start.91 = (bf16[1,1024,8]{1,2,0:T(8,128)(2,1)S(1)}, bf16[1,1024,8]{1,2,0:T(8,128)(2,1)}, u32[]{:S(2)}) copy-start(bf16[1,1024,8]{1,2,0:T(8,128)(2,1)} %param.20) | copy-start | bytes 49156
  7.2 23.5 %copy-start.36 = (bf16[1,1024,768]{2,1,0:T(8,128)(2,1)S(1)}, bf16[1,1024,768]{2,1,0:T(8,128)(2,1)}, u32[]{:S(2)}) copy-start(bf16[1,1024,768]{2,1,0:T(8,128)(2,1)} %param.19) | copy-start | bytes 4718596
  7.2 214.5 %all-gather.11.cloned.1.call-start = ((), (), s32[]{:S(2)}) async-start(), calls=%async_computation.20 | async-start | bytes 1327104 | tf_op jit(solution)/shard_map/all_gather | solution.py:173
  8.0 216.2 %all-gather.13.cloned.1.call-start = ((), (), s32[]{:S(2)}) async-start(), calls=%async_computation.21 | async-start | bytes 1327104 | tf_op jit(solution)/shard_map/all_gather | solution.py:174
  8.7 217.8 %all-gather.15.cloned.1.call-start = ((), (), s32[]{:S(2)}) async-start(), calls=%async_computation.22 | async-start | bytes 1327104 | tf_op jit(solution)/shard_map/all_gather | solution.py:175
  9.4 329.5 %all-gather.17.cloned.1.call-start = ((), (), s32[]{:S(2)}) async-start(), calls=%async_computation.23 | async-start | bytes 1327104 | tf_op jit(solution)/shard_map/all_gather | solution.py:176
  10.0 383.0 %all-gather.19.cloned.1.call-start = ((), (), s32[]{:S(2)}) async-start(), calls=%async_computation.24 | async-start | bytes 3538944 | tf_op jit(solution)/shard_map/all_gather | solution.py:244
  26.5 11.1 all-to-all-start.1
  38.2 76.0 %all-to-all-start = ((bf16[4,1,1024,768]{3,2,1,0:T(8,128)(2,1)}), bf16[4,1,1024,768]{3,2,1,0:T(8,128)(2,1)}, u32[]{:S(2)}, u32[]{:S(2)}) async-start(bf16[4,1,1024,768]{3,2,1,0:T(8,128)(2,1)} %get-tuple-element.212), calls=%async_computation | async-start | bytes 12582912 | tf_op jit(solution)/shard_map/all_to_all | solution.py:159
  43.5 349.6 %all-gather.21.cloned.1.call-start = ((), (), s32[]{:S(2)}) async-start(), calls=%async_computation.25 | async-start | bytes 3538944 | tf_op jit(solution)/shard_map/all_gather | solution.py:245
  114.2 35.8 %copy-start.108 = (bf16[2,96]{1,0:T(2,128)(2,1)S(1)}, bf16[2,96]{1,0:T(2,128)(2,1)}, u32[]{:S(2)}) copy-start(bf16[2,96]{1,0:T(2,128)(2,1)} %param.33) | copy-start | bytes 1156
  114.2 52.7 %copy-start.107 = (bf16[96,4]{0,1:T(4,128)(2,1)S(1)}, bf16[96,4]{0,1:T(4,128)(2,1)}, u32[]{:S(2)}) copy-start(bf16[96,4]{0,1:T(4,128)(2,1)} %param.32) | copy-start | bytes 2308
  114.2 71.0 %copy-start.105 = (bf16[96,8]{0,1:T(8,128)(2,1)S(1)}, bf16[96,8]{0,1:T(8,128)(2,1)}, u32[]{:S(2)}) copy-start(bf16[96,8]{0,1:T(8,128)(2,1)} %param.30) | copy-start | bytes 4612
  114.2 114.7 %all-to-all-start.5 = ((bf16[4,1,1024,768]{3,2,1,0:T(8,128)(2,1)}), bf16[4,1,1024,768]{3,2,1,0:T(8,128)(2,1)}, u32[]{:S(2)}, u32[]{:S(2)}) async-start(bf16[4,1,1024,768]{3,2,1,0:T(8,128)(2,1)} %get-tuple-element.213), calls=%async_computation.5 | async-start | bytes 12582912 | tf_op jit(solution)/shard_map/all_to_all | solution.py:162
  119.6 97.5 %copy-start.115 = (s32[32]{0:T(128)S(1)}, s32[32]{0:T(128)}, u32[]{:S(2)}) copy-start(s32[32]{0:T(128)} %param.21) | copy-start | bytes 388
  119.6 101.3 %copy-start.62 = (bf16[4,1,1024,8]{2,3,1,0:T(8,128)(2,1)S(1)}, bf16[4,1,1024,8]{2,3,1,0:T(8,128)(2,1)}, u32[]{:S(2)}) copy-start(bf16[4,1,1024,8]{2,3,1,0:T(8,128)(2,1)} %copy-done.61) | copy-start | bytes 196612
  119.6 295.6 %all-gather.23.cloned.1.call-start = ((), (), s32[]{:S(2)}) async-start(), calls=%async_computation.26 | async-start | bytes 3538944 | tf_op jit(solution)/shard_map/all_gather | solution.py:246
  149.4 92.0 %copy-start.87 = (f32[768]{0:T(1024)}, f32[768]{0:T(1024)S(1)}, u32[]{:S(2)}) copy-start(f32[768]{0:T(1024)S(1)} %convert_element_type.283) | copy-start | bytes 9220
  213.4 13.1 copy-start.44
  213.4 13.1 copy-start.46
  213.4 13.1 copy-start.48
  213.4 13.1 copy-start.50
  220.9 84.0 %copy-start.17 = (pred[512,1024]{1,0:T(8,128)(4,1)}, pred[512,1024]{1,0:T(8,128)(4,1)S(1)}, u32[]{:S(2)}) copy-start(pred[512,1024]{1,0:T(8,128)(4,1)S(1)} %get-tuple-element.204) | copy-start | bytes 1572868
  220.9 106.6 %copy-start.32 = (pred[512,1024]{1,0:T(8,128)(4,1)}, pred[512,1024]{1,0:T(8,128)(4,1)S(1)}, u32[]{:S(2)}) copy-start(pred[512,1024]{1,0:T(8,128)(4,1)S(1)} %get-tuple-element.203) | copy-start | bytes 1572868
  257.5 70.0 %copy-start.10 = (bf16[1024,768]{0,1:T(8,128)(2,1)}, bf16[1024,768]{0,1:T(8,128)(2,1)S(1)}, u32[]{:S(2)}) copy-start(bf16[1024,768]{0,1:T(8,128)(2,1)S(1)} %copy.190) | copy-start | bytes 4718596
  277.0 27.9 %slice-start = ((s8[25165824]{0:T(1024)(128)(4,1)}), s8[4194304]{0:T(1024)(128)(4,1)S(1)}, s32[]{:S(2)}) async-start(s8[25165824]{0:T(1024)(128)(4,1)} %bitcast.190), calls=%async_computation.38 | async-start | bytes 8388608
  277.0 27.9 %slice-start.1 = ((s8[25165824]{0:T(1024)(128)(4,1)}), s8[4194304]{0:T(1024)(128)(4,1)S(1)}, s32[]{:S(2)}) async-start(s8[25165824]{0:T(1024)(128)(4,1)} %bitcast.190), calls=%async_computation.39 | async-start | bytes 8388608
  277.0 27.9 %slice-start.2 = ((s8[25165824]{0:T(1024)(128)(4,1)}), s8[4194304]{0:T(1024)(128)(4,1)S(1)}, s32[]{:S(2)}) async-start(s8[25165824]{0:T(1024)(128)(4,1)} %bitcast.190), calls=%async_computation.40 | async-start | bytes 8388608
  277.0 27.9 %slice-start.3 = ((s8[25165824]{0:T(1024)(128)(4,1)}), s8[4194304]{0:T(1024)(128)(4,1)S(1)}, s32[]{:S(2)}) async-start(s8[25165824]{0:T(1024)(128)(4,1)} %bitcast.190), calls=%async_computation.41 | async-start | bytes 8388608
  291.6 13.4 slice-start.4
  291.6 13.4 slice-start.5
  291.6 13.4 copy-start.58
  313.5 16.0 copy-start.2
  313.5 16.0 copy-start.70
  371.8 24.5 %all-to-all-start.2 = ((bf16[4,256,768]{2,1,0:T(8,128)(2,1)}), bf16[4,256,768]{2,1,0:T(8,128)(2,1)}, u32[]{:S(2)}, u32[]{:S(2)}) async-start(bf16[4,256,768]{2,1,0:T(8,128)(2,1)} %broadcast_select_fusion.2), calls=%async_computation.2 | async-start | bytes 3145728 | tf_op jit(solution)/shard_map/all_to_all | solution.py:255
  378.5 14.5 copy-start.3
  382.7 106.8 %copy-start.60 = (f32[1024,12]{0,1:T(8,128)}, f32[1024,12]{0,1:T(8,128)S(1)}, u32[]{:S(2)}) copy-start(f32[1024,12]{0,1:T(8,128)S(1)} %fusion.113) | copy-start | bytes 147460
  422.9 66.9 %all-to-all-start.3 = ((bf16[4,256,768]{2,1,0:T(8,128)(2,1)}), bf16[4,256,768]{2,1,0:T(8,128)(2,1)S(1)}, u32[]{:S(2)}, u32[]{:S(2)}) async-start(bf16[4,256,768]{2,1,0:T(8,128)(2,1)} %bitcast.30), calls=%async_computation.3 | async-start | bytes 3145728 | tf_op jit(solution)/shard_map/all_to_all | solution.py:273
  520.0 25.1 %copy-start.111 = (bf16[1,2048,768]{2,1,0:T(8,128)(2,1)S(1)}, bf16[1,2048,768]{2,1,0:T(8,128)(2,1)}, u32[]{:S(2)}) copy-start(bf16[1,2048,768]{2,1,0:T(8,128)(2,1)} %all-gather.23.cloned.1.call-done) | copy-start | bytes 9437188
  568.7 23.8 %all-to-all-start.7 = ((bf16[4,256,768]{2,1,0:T(8,128)(2,1)}), bf16[4,256,768]{2,1,0:T(8,128)(2,1)S(1)}, u32[]{:S(2)}, u32[]{:S(2)}) async-start(bf16[4,256,768]{2,1,0:T(8,128)(2,1)} %bitcast.42), calls=%async_computation.7 | async-start | bytes 3145728 | tf_op jit(solution)/shard_map/all_to_all | solution.py:336
  572.4 376.5 %reduce-scatter.35.cloned.1.call-start = ((), (), s32[]{:S(2)}) async-start(), calls=%async_computation.33 | async-start | bytes 1327104
  685.9 28.2 %copy-start.78 = (f32[1024,2,2]{0,2,1:T(2,128)S(1)}, f32[1024,2,2]{0,2,1:T(2,128)}, u32[]{:S(2)}) copy-start(f32[1024,2,2]{0,2,1:T(2,128)} %copy-done.77) | copy-start | bytes 49156
  736.8 13.2 copy-start.11
  750.0 18.1 %copy-start.33 = (pred[512,1024]{1,0:T(8,128)(4,1)S(1)}, pred[512,1024]{1,0:T(8,128)(4,1)}, u32[]{:S(2)}) copy-start(pred[512,1024]{1,0:T(8,128)(4,1)} %copy-done.32) | copy-start | bytes 1572868
  750.0 18.1 %copy-start.57 = (f32[12,512]{1,0:T(8,128)S(1)}, f32[12,512]{1,0:T(8,128)}, u32[]{:S(2)}) copy-start(f32[12,512]{1,0:T(8,128)} %log_add_fusion.1) | copy-start | bytes 73732
  786.0 21.8 %copy-start.29 = (bf16[1024,12,32]{0,2,1:T(8,128)(2,1)S(1)}, bf16[1024,12,32]{0,2,1:T(8,128)(2,1)}, u32[]{:S(2)}) copy-start(bf16[1024,12,32]{0,2,1:T(8,128)(2,1)} %copy-done.28) | copy-start | bytes 2359300
  786.0 21.8 %copy-start.31 = (bf16[1024,12,32]{0,2,1:T(8,128)(2,1)S(1)}, bf16[1024,12,32]{0,2,1:T(8,128)(2,1)}, u32[]{:S(2)}) copy-start(bf16[1024,12,32]{0,2,1:T(8,128)(2,1)} %copy-done.30) | copy-start | bytes 2359300
  888.2 127.2 %reduce-scatter.33.cloned.1.call-start = ((), (), s32[]{:S(2)}) async-start(), calls=%async_computation.32 | async-start | bytes 1327104
  889.8 192.0 %reduce-scatter.31.cloned.1.call-start = ((), (), s32[]{:S(2)}) async-start(), calls=%async_computation.31 | async-start | bytes 1327104
  891.3 256.8 %reduce-scatter.23.cloned.1.call-start = ((), (), s32[]{:S(2)}) async-start(), calls=%async_computation.27 | async-start | bytes 1327104 | tf_op jit(solution)/shard_map/reduce_scatter | solution.py:469
  896.6 504.8 %reduce-scatter.41.cloned.1.call-start = ((), (), s32[]{:S(2)}) async-start(), calls=%async_computation.36 | async-start | bytes 221184
  897.5 504.7 %reduce-scatter.39.cloned.1.call-start = ((), (), s32[]{:S(2)}) async-start(), calls=%async_computation.35 | async-start | bytes 221184
  901.2 501.9 %reduce-scatter.37.cloned.1.call-start = ((), (), s32[]{:S(2)}) async-start(), calls=%async_computation.34 | async-start | bytes 221184
  902.1 511.0 %all-reduce.10.cloned.1.call-start = ((), (), s32[]{:S(2)}) async-start(), calls=%async_computation.37 | async-start | bytes 1474560 | tf_op jit(solution)/shard_map/psum | solution.py:489
  1148.2 306.7 %reduce-scatter.29.cloned.1.call-start = ((), (), s32[]{:S(2)}) async-start(), calls=%async_computation.30 | async-start | bytes 3538944 | tf_op jit(solution)/shard_map/reduce_scatter | solution.py:513
  1157.5 37.2 %all-to-all-start.9 = ((bf16[4,1,1024,8]{2,3,1,0:T(8,128)(2,1)}), bf16[4,1,1024,8]{2,3,1,0:T(8,128)(2,1)S(1)}, u32[]{:S(2)}, u32[]{:S(2)}) async-start(bf16[4,1,1024,8]{2,3,1,0:T(8,128)(2,1)} %select_convert_fusion.3), calls=%async_computation.9 | async-start | bytes 131072 | tf_op jit(solution)/shard_map/all_to_all | solution.py:537
  1160.8 371.8 %reduce-scatter.25.cloned.1.call-start = ((), (), s32[]{:S(2)}) async-start(), calls=%async_computation.28 | async-start | bytes 3538944 | tf_op jit(solution)/shard_map/reduce_scatter | solution.py:501
  1194.7 76.0 %all-to-all-start.4 = ((bf16[4,1,1024,768]{3,2,1,0:T(8,128)(2,1)}), bf16[4,1,1024,768]{3,2,1,0:T(8,128)(2,1)}, u32[]{:S(2)}, u32[]{:S(2)}) async-start(bf16[4,1,1024,768]{3,2,1,0:T(8,128)(2,1)} %get-tuple-element.207), calls=%async_computation.4 | async-start | bytes 12582912 | tf_op jit(solution)/shard_map/all_to_all | solution.py:523
  1200.0 410.2 %reduce-scatter.27.cloned.1.call-start = ((), (), s32[]{:S(2)}) async-start(), calls=%async_computation.29 | async-start | bytes 3538944 | tf_op jit(solution)/shard_map/reduce_scatter | solution.py:507
  1270.7 108.3 %copy-start.97 = (pred[4]{0:T(512)(128)(4,1)S(1)}, pred[4]{0:T(512)(128)(4,1)}, u32[]{:S(2)}) copy-start(pred[4]{0:T(512)(128)(4,1)} %copy-done.96) | copy-start | bytes 16
  1270.7 109.0 %copy-start.104 = (bf16[768]{0:T(1024)(128)(2,1)S(1)}, bf16[768]{0:T(1024)(128)(2,1)}, u32[]{:S(2)}) copy-start(bf16[768]{0:T(1024)(128)(2,1)} %get-tuple-element.134) | copy-start | bytes 4612
  1270.7 149.3 %all-to-all-start.8 = ((bf16[4,1,1024,768]{3,2,1,0:T(8,128)(2,1)}), bf16[4,1,1024,768]{3,2,1,0:T(8,128)(2,1)}, u32[]{:S(2)}, u32[]{:S(2)}) async-start(bf16[4,1,1024,768]{3,2,1,0:T(8,128)(2,1)} %get-tuple-element.208), calls=%async_computation.8 | async-start | bytes 12582912 | tf_op jit(solution)/shard_map/all_to_all | solution.py:530
  (86 other events, 533.5 us)
Sparse Core Ops, SparseCore 0:
  10.2 43.7 all-gather.10
  56.2 39.8 all-gather.12
  98.3 40.0 all-gather.14
  140.4 39.8 all-gather.16
  182.2 61.8 all-gather.18
  246.0 61.2 all-gather.20
  309.5 58.6 all-gather.22
  888.4 60.5 reduce-scatter.34
  952.3 63.0 reduce-scatter.32
  1018.7 63.0 reduce-scatter.30
  1085.1 63.0 reduce-scatter.22
  1151.8 60.0 reduce-scatter.40
  1215.8 60.0 reduce-scatter.38
  1279.6 60.0 reduce-scatter.36
  1342.8 33.6 all-reduce.9
  1379.9 74.9 reduce-scatter.28
  1458.4 74.1 reduce-scatter.24
  1536.1 74.0 reduce-scatter.26
where the time goes:
time: 1630 us; the launch traced here: 1620 us
  waiting for transfers between devices  574 us (35%)
  other arithmetic  259 us (16%)
  local copies, waits for them, and re-layouts  244 us (15%)
  matrix products  242 us (15%)
  blocking collectives  236 us (14%)
  starting transfers between devices  41.9 us (3%)
  between operations  21.5 us (1%)
    unnamed x24, waiting for transfers between devices  181 us
    psum x1, blocking collectives, per_device(): gating_total = lax.psum(grad_gating, ('expert', 'fsdp'))  102 us
    dot_general x14, matrix products, contract(): lax.dot_general(left_side, right_side, (((left_dim,), (right_dim,)), ((),...  77.5 us
    reduce_scatter x1, waiting for transfers between devices, per_device(): lax.psum_scatter(grad_joint_w[None, :, :hidden_units].astype(jnp.bfloat16...  75.8 us
    reduce_scatter x1, waiting for transfers between devices, per_device(): lax.psum_scatter(grad_joint_w[None, :, hidden_units:].astype(jnp.bfloat16...  75.6 us
    all_to_all x1, waiting for transfers between devices, per_device(): lax.all_to_all(spread_rows(hidden_in, target_hot), 'expert', split_axis=0...  70.1 us
    all_to_all x1, waiting for transfers between devices, per_device(): lax.all_to_all(spread_rows(slot_results[0], source_hot).astype(jnp.bfloat...  70.1 us
    reduce_scatter x1, waiting for transfers between devices, per_device(): lax.psum_scatter(shared_terms[3].astype(jnp.bfloat16), 'fsdp', scatter_di...  64.7 us
  transfers between devices with their start and end apart: 27, of which 11 were waited for; matrix products, arithmetic and copies ran while one was open for 23% of the time, Pallas kernels for 0%

commit v1 on v0

v1 whole, which is shorter than its diff:
```python
import jax
import jax.numpy as jnp
from jax import lax
from jax.experimental import pallas as pl
from jax.experimental.pallas import tpu as pltpu
from jax.sharding import PartitionSpec as P

HD = 64
CAP = 256
TB = 256
PAIR = 2 * HD
norm_eps = 1e-05
rope_base = 10000.0
masked_score = -1e30
f32 = jnp.float32
bf16 = jnp.bfloat16
i32 = jnp.int32


def nn(a, b):
    return lax.dot_general(a, b, (((1,), (0,)), ((), ())), preferred_element_type=f32)


def nt(a, b):
    return lax.dot_general(a, b, (((1,), (1,)), ((), ())), preferred_element_type=f32)


def tn(a, b):
    return lax.dot_general(a, b, (((0,), (0,)), ((), ())), preferred_element_type=f32)


def split2(x):
    high = x.astype(bf16)
    return high, (x - high.astype(f32)).astype(bf16)


def split3(x):
    high = x.astype(bf16)
    rest = x - high.astype(f32)
    mid = rest.astype(bf16)
    return high, mid, (rest - mid.astype(f32)).astype(bf16)


def call(kernel, grid, ins, outs, args, scratch=(), flops=0, nbytes=0, exps=0, vmem=48 << 20):
    return pl.pallas_call(
        kernel,
        grid=grid,
        in_specs=ins,
        out_specs=[o[2] for o in outs],
        out_shape=[jax.ShapeDtypeStruct(o[0], o[1]) for o in outs],
        scratch_shapes=list(scratch),
        compiler_params=pltpu.CompilerParams(
            dimension_semantics=("arbitrary",) * len(grid), vmem_limit_bytes=vmem
        ),
        cost_estimate=pl.CostEstimate(flops=flops, bytes_accessed=nbytes, transcendentals=exps),
    )(*args)


def whole(shape):
    zeros = (0,) * len(shape)
    return pl.BlockSpec(shape, lambda *_: zeros)


def lanes_of(shape):
    return lax.broadcasted_iota(i32, shape, len(shape) - 1)


def turn(values, cos_wide, sin_wide):
    first = lanes_of((1, PAIR)) % HD < HD // 2
    partner = jnp.where(first, pltpu.roll(values, PAIR - HD // 2, 1), pltpu.roll(values, HD // 2, 1))
    return values * cos_wide + partner * sin_wide


def qkv_kernel(hid_ref, gain_ref, w_ref, cos_ref, sin_ref, q_ref, k_ref, v_ref, n_ref):
    width = hid_ref.shape[1]
    hidden = hid_ref[...].astype(f32)
    scale = lax.rsqrt(jnp.mean(hidden * hidden, axis=-1, keepdims=True) + norm_eps)
    normed = (hidden * scale * gain_ref[...]).astype(bf16)
    n_ref[...] = normed
    cos_wide, sin_wide = cos_ref[...], sin_ref[...]
    for part, (out, factor) in enumerate(((q_ref, HD**-0.5), (k_ref, 1.0))):
        for at in range(0, width, PAIR):
            lin = nt(normed, w_ref[part, at : at + PAIR])
            out[:, at : at + PAIR] = (turn(lin, cos_wide, sin_wide) * factor).astype(bf16)
    v_ref[...] = nt(normed, w_ref[2]).astype(bf16)


def qkv_call(hidden, gain, weights, cos_wide, sin_wide):
    rows, width = hidden.shape
    row = pl.BlockSpec((TB, width), lambda i: (i, 0))
    tab = pl.BlockSpec((TB, PAIR), lambda i: (i, 0))
    return call(
        qkv_kernel,
        (rows // TB,),
        [row, whole((1, width)), whole(weights.shape), tab, tab],
        [((rows, width), bf16, row)] * 4,
        (hidden, gain, weights, cos_wide, sin_wide),
        flops=6 * rows * width * width,
        nbytes=10 * rows * width + 6 * width * width,
    )


def attend_kernel(len_ref, q_ref, k_ref, v_ref, o_ref, r_ref, e_ref):
    rows = q_ref.shape[0]
    live = len_ref[0]
    low_lanes = lanes_of((1, PAIR)) < HD
    keys = k_ref[...]
    nil = jnp.zeros_like(keys)
    key_heads = (jnp.where(low_lanes, keys, nil), jnp.where(low_lanes, nil, keys))
    value_t = v_ref[...].T
    zeros = jnp.zeros((HD, rows), bf16)
    ones = jnp.ones((HD, rows), bf16)
    value_heads = (
        jnp.concatenate([value_t[:HD], zeros, ones, zeros], axis=0),
        jnp.concatenate([zeros, value_t[HD:], zeros, ones], axis=0),
    )
    key_at = lax.broadcasted_iota(i32, (TB, TB), 0)
    causal = key_at <= lax.broadcasted_iota(i32, (TB, TB), 1)
    for i in range(rows // TB):
        query = q_ref[i * TB : (i + 1) * TB, :]
        total = jnp.zeros((2 * PAIR, TB), f32)
        for head in range(2):
            blocks = []
            for j in range(i + 1):
                score = nt(key_heads[head][j * TB : (j + 1) * TB], query)
                keep = None
                if j > 0:
                    keep = key_at < live - j * TB
                if j == i:
                    keep = causal if keep is None else keep & causal
                if keep is not None:
                    score = jnp.where(keep, score, masked_score)
                blocks.append(score)
            top = jnp.max(blocks[0], axis=0, keepdims=True)
            for block in blocks[1:]:
                top = jnp.maximum(top, jnp.max(block, axis=0, keepdims=True))
            for j, block in enumerate(blocks):
                expo = jnp.exp(block - top).astype(bf16)
                e_ref[0, head, i * (i + 1) // 2 + j] = expo
                total = total + nn(value_heads[head][:, j * TB : (j + 1) * TB], expo)
        recip = 1.0 / total[PAIR:]
        o_ref[i * TB : (i + 1) * TB, :] = (total[:PAIR] * recip).T.astype(bf16)
        r_ref[i * TB : (i + 1) * TB, :] = recip.T


def attend_call(live, query, key, value):
    rows, width = query.shape
    pairs = width // PAIR
    steps = rows // TB
    tiles = steps * (steps + 1) // 2
    col = pl.BlockSpec((rows, PAIR), lambda p: (0, p))
    expo = (1, 2, tiles, TB, TB)
    return call(
        attend_kernel,
        (pairs,),
        [pl.BlockSpec(memory_space=pltpu.SMEM), col, col, col],
        [
            ((rows, width), bf16, col),
            ((rows, width), f32, col),
            ((pairs,) + expo[1:], bf16, pl.BlockSpec(expo, lambda p: (p, 0, 0, 0, 0))),
        ],
        (live, query, key, value),
        flops=pairs * 2 * tiles * TB * TB * 4 * PAIR,
        nbytes=pairs * 2 * tiles * TB * TB * 2 + 12 * rows * width,
        exps=pairs * 2 * tiles * TB * TB,
    )


def attend_back_kernel(
    q_ref, k_ref, v_ref, e_ref, do_ref, att_ref, r_ref, cos_ref, sin_ref, dq_ref, dk_ref, dv_ref, dqt_ref
):
    rows = q_ref.shape[0]
    steps = rows // TB
    low_lanes = lanes_of((1, PAIR)) < HD

    def halves(x):
        nil = jnp.zeros_like(x)
        return jnp.where(low_lanes, x, nil), jnp.where(low_lanes, nil, x)

    scaled = do_ref[...].astype(f32) * r_ref[...]
    product_t = (scaled * att_ref[...].astype(f32)).T
    deltas = (
        jnp.sum(product_t[:HD], axis=0, keepdims=True),
        jnp.sum(product_t[HD:], axis=0, keepdims=True),
    )
    grad = scaled.astype(bf16)
    grad_heads = halves(grad)
    query_heads = halves(q_ref[...])
    value_heads = halves(v_ref[...])
    key_t = k_ref[...].T
    zeros = jnp.zeros((HD, rows), bf16)
    key_heads = (
        jnp.concatenate([key_t[:HD], zeros], axis=0),
        jnp.concatenate([zeros, key_t[HD:]], axis=0),
    )
    for j in range(steps):
        js = slice(j * TB, (j + 1) * TB)
        value_grad = jnp.zeros((TB, PAIR), f32)
        key_grad = jnp.zeros((TB, PAIR), f32)
        keys_t = jnp.concatenate([key_heads[0][:, js], key_heads[1][:, js]], axis=1)
        for i in range(j, steps):
            rs = slice(i * TB, (i + 1) * TB)
            tile = i * (i + 1) // 2 + j
            expos, scores = [], []
            for head in range(2):
                grad_prob = nt(value_heads[head][js], grad[rs])
                expo = e_ref[0, head, tile]
                expos.append(expo)
                scores.append(
                    (expo.astype(f32) * (grad_prob - deltas[head][:, rs])).astype(bf16)
                )
            value_grad = value_grad + nn(
                jnp.concatenate(expos, axis=1),
                jnp.concatenate([grad_heads[0][rs], grad_heads[1][rs]], axis=0),
            )
            key_grad = key_grad + nn(
                jnp.concatenate(scores, axis=1),
                jnp.concatenate([query_heads[0][rs], query_heads[1][rs]], axis=0),
            )
            add = nn(keys_t, jnp.concatenate(scores, axis=0))
            if j == 0:
                dqt_ref[:, rs] = add
            else:
                dqt_ref[:, rs] += add
        dv_ref[js, :] = value_grad.astype(bf16)
        dk_ref[js, :] = turn(key_grad, cos_ref[js, :], -sin_ref[js, :]).astype(bf16)
    query_grad = dqt_ref[...].T * (HD**-0.5)
    dq_ref[...] = turn(query_grad, cos_ref[...], -sin_ref[...]).astype(bf16)


def attend_back_call(query, key, value, expo, grad, attended, recip, cos_wide, sin_wide):
    rows, width = query.shape
    pairs, _, tiles = expo.shape[:3]
    col = pl.BlockSpec((rows, PAIR), lambda p: (0, p))
    tab = whole((rows, PAIR))
    e_spec = pl.BlockSpec((1,) + expo.shape[1:], lambda p: (p, 0, 0, 0, 0))
    return call(
        attend_back_kernel,
        (pairs,),
        [col, col, col, e_spec, col, col, col, tab, tab],
        [((rows, width), bf16, col)] * 3,
        (query, key, value, expo, grad, attended, recip, cos_wide, sin_wide),
        scratch=[pltpu.VMEM((PAIR, rows), f32)],
        flops=pairs * 2 * tiles * TB * TB * 8 * PAIR,
        nbytes=pairs * 2 * tiles * TB * TB * 2 + 22 * rows * width,
    )


def route_kernel(
    att_ref, hid_ref, grad_ref, wo_ref, gain_ref, sw_ref, prev_ref, gating_ref, rcol_ref, prow_ref,
    res_ref, info_ref, send_ref, nlow_ref, rg_ref,
):
    step = pl.program_id(0)
    rows = nlow_ref.shape[0]
    blocks = rows // TB
    choices = prev_ref.shape[1]

    @pl.when(step < blocks)
    def _():
        residual = hid_ref[...].astype(f32) + nn(att_ref[...], wo_ref[...])
        res_ref[...] = residual
        scale = lax.rsqrt(jnp.mean(residual * residual, axis=-1, keepdims=True) + norm_eps)
        normed = residual * scale * gain_ref[...]
        high, mid, low = split3(normed)
        small_weights = sw_ref[...]
        small = nn(high, small_weights) + nn(mid, small_weights) + nn(low, small_weights)
        logits = small + nn(prev_ref[...], gating_ref[...])
        lane = lanes_of(logits.shape)
        is_choice = lane < choices
        masked = jnp.where(is_choice, logits, masked_score)
        expo = jnp.exp(masked - jnp.max(masked, axis=-1, keepdims=True))
        probs = expo / jnp.sum(expo, axis=-1, keepdims=True)
        wide = small.shape[1]
        partner = jnp.where(lane % 2 == 0, pltpu.roll(small, wide - 1, 1), pltpu.roll(small, 1, 1))
        top = jnp.maximum(small, partner)
        own = jnp.exp(small - top)
        alpha = own / (own + jnp.exp(partner - top))
        gates = [
            jnp.sum(jnp.where(lane == rcol_ref[:, j : j + 1], probs, 0.0), axis=-1, keepdims=True)
            for j in range(2)
        ]
        info = jnp.where(is_choice, probs, alpha)
        for at, column in enumerate((gates[0], gates[1], scale)):
            info = jnp.where(lane == choices + 4 + at, column, info)
        info_ref[...] = info
        here = pl.ds(pl.multiple_of(step * TB, TB), TB)
        nlow_ref[here, :] = high
        grad = grad_ref[...].astype(f32)
        rg_ref[0, here, :] = (gates[0] * grad).astype(bf16)
        rg_ref[1, here, :] = (gates[1] * grad).astype(bf16)

    @pl.when(step >= blocks)
    def _():
        slot = (step - blocks) * CAP + lax.broadcasted_iota(i32, (CAP, rows), 0)
        hot = [jnp.where(prow_ref[j : j + 1, :] == slot, 1.0, 0.0).astype(bf16) for j in range(2)]
        send_ref[0, :CAP, :] = nn(hot[0] + hot[1], nlow_ref[...]).astype(bf16)
        send_ref[0, CAP:, :] = (nn(hot[0], rg_ref[0]) + nn(hot[1], rg_ref[1])).astype(bf16)


def route_call(attended, hidden, grad, w_out, gain, small_weights, prev, gating, rcols, prows, experts):
    rows, width = attended.shape
    blocks = rows // TB
    wide = small_weights.shape[1]

    def block(cols):
        return pl.BlockSpec((TB, cols), lambda i: (jnp.minimum(i, blocks - 1), 0))

    return call(
        route_kernel,
        (blocks + experts,),
        [
            block(width), block(width), block(width), whole(w_out.shape), whole(gain.shape),
            whole(small_weights.shape), block(prev.shape[1]), whole(gating.shape), block(2), whole(prows.shape),
        ],
        [
            ((rows, width), f32, block(width)),
            ((rows, wide), f32, block(wide)),
            (
                (experts, 2 * CAP, width),
                bf16,
                pl.BlockSpec((1, 2 * CAP, width), lambda i: (jnp.maximum(i - blocks, 0), 0, 0)),
            ),
        ],
        (attended, hidden, grad, w_out, gain, small_weights, prev, gating, rcols, prows),
        scratch=[pltpu.VMEM((rows, width), bf16), pltpu.VMEM((2, rows, width), bf16)],
        flops=2 * rows * width * width + 6 * experts * CAP * rows * width,
        nbytes=10 * rows * width + 2 * width * width + 4 * experts * CAP * width,
    )


def expert_kernel(x_ref, w_ref, y_ref, inner_ref, fa_ref, fb_ref, acc_ref):
    step = pl.program_id(0)
    rows = acc_ref.shape[0]
    rows_in = x_ref[...].reshape(rows, x_ref.shape[2])
    gate = nt(rows_in, w_ref[0, 0])
    up = nt(rows_in, w_ref[0, 1])
    sig = 1.0 / (1.0 + jnp.exp(-gate))
    act = gate * sig
    inner = (act * up).astype(bf16)
    inner_ref[0] = inner
    fa_ref[0] = (up * sig * (1.0 + gate * (1.0 - sig))).astype(bf16)
    fb_ref[0] = act.astype(bf16)
    out = nn(inner, w_ref[0, 2])

    @pl.when(step == 0)
    def _():
        acc_ref[...] = out

    @pl.when(step > 0)
    def _():
        acc_ref[...] += out

    @pl.when(step == pl.num_programs(0) - 1)
    def _():
        y_ref[...] = acc_ref[...].astype(bf16).reshape(y_ref.shape)


def expert_back_kernel(g_ref, w_ref, fa_ref, fb_ref, dx_ref, dgu_ref, acc_ref):
    step = pl.program_id(0)
    rows = acc_ref.shape[0]
    grad_in = g_ref[...].reshape(rows, g_ref.shape[2])
    grad_inner = nt(grad_in, w_ref[0, 2])
    grad_gate = (grad_inner * fa_ref[0].astype(f32)).astype(bf16)
    grad_up = (grad_inner * fb_ref[0].astype(f32)).astype(bf16)
    dgu_ref[0, 0] = grad_gate
    dgu_ref[0, 1] = grad_up
    out = nn(grad_gate, w_ref[0, 0]) + nn(grad_up, w_ref[0, 1])

    @pl.when(step == 0)
    def _():
        acc_ref[...] = out

    @pl.when(step > 0)
    def _():
        acc_ref[...] += out

    @pl.when(step == pl.num_programs(0) - 1)
    def _():
        dx_ref[...] = acc_ref[...].astype(bf16).reshape(dx_ref.shape)


def expert_weights_kernel(x_ref, g_ref, inner_ref, dgu_ref, dw_ref):
    rows = inner_ref.shape[1]
    rows_in = x_ref[...].reshape(rows, x_ref.shape[2])
    grad_in = g_ref[...].reshape(rows, g_ref.shape[2])
    dw_ref[0, 0] = tn(dgu_ref[0, 0], rows_in).astype(bf16)
    dw_ref[0, 1] = tn(dgu_ref[0, 1], rows_in).astype(bf16)
    dw_ref[0, 2] = tn(inner_ref[0], grad_in).astype(bf16)


def expert_specs(sent, weights):
    experts, _, width = sent.shape
    chunks, _, units, _ = weights.shape
    rows = experts * CAP
    return dict(
        rows=rows,
        x=pl.BlockSpec((experts, CAP, width), lambda c: (0, 0, 0)),
        g=pl.BlockSpec((experts, CAP, width), lambda c: (0, 1, 0)),
        w=pl.BlockSpec((1, 3, units, width), lambda c: (c, 0, 0, 0)),
        unit=pl.BlockSpec((1, rows, units), lambda c: (c, 0, 0)),
        pair=pl.BlockSpec((1, 2, rows, units), lambda c: (c, 0, 0, 0)),
        flops=6 * rows * width * chunks * units,
        nbytes=6 * chunks * units * (rows + width) + 4 * rows * width,
    )


def expert_call(sent, weights):
    s = expert_specs(sent, weights)
    chunks, _, units, width = weights.shape
    rows = s["rows"]
    hidden = ((chunks, rows, units), bf16, s["unit"])
    return call(
        expert_kernel,
        (chunks,),
        [s["x"], s["w"]],
        [((sent.shape[0], CAP, width), bf16, s["x"]), hidden, hidden, hidden],
        (sent, weights),
        scratch=[pltpu.VMEM((rows, width), f32)],
        flops=s["flops"],
        nbytes=s["nbytes"],
        exps=rows * chunks * units,
    )


def expert_back_call(sent, weights, factor_a, factor_b):
    s = expert_specs(sent, weights)
    chunks, _, units, width = weights.shape
    rows = s["rows"]
    return call(
        expert_back_kernel,
        (chunks,),
        [s["g"], s["w"], s["unit"], s["unit"]],
        [
            ((sent.shape[0], CAP, width), bf16, s["x"]),
            ((chunks, 2, rows, units), bf16, s["pair"]),
        ],
        (sent, weights, factor_a, factor_b),
        scratch=[pltpu.VMEM((rows, width), f32)],
        flops=s["flops"],
        nbytes=s["nbytes"],
    )


def expert_weights_call(sent, inner, dgu, weights_shape):
    chunks, _, units, width = weights_shape
    s = expert_specs(sent, jax.ShapeDtypeStruct(weights_shape, bf16))
    return call(
        expert_weights_kernel,
        (chunks,),
        [s["x"], s["g"], s["unit"], s["pair"]],
        [(weights_shape, bf16, s["w"])],
        (sent, sent, inner, dgu),
        flops=s["flops"],
        nbytes=s["nbytes"],
    )[0]


def combine_kernel(
    y_ref, res_ref, info_ref, rcol_ref, pcol_ref, grad_ref, gain_ref, vec_ref, sw_ref, prev_ref, gt_ref,
    out_ref, part_ref, gprev_ref, gsw_ref, gvec_ref, ggat_ref,
):
    step = pl.program_id(0)
    choices = prev_ref.shape[1]
    experts = y_ref.shape[0]
    slots = experts * CAP
    rows_out = y_ref[...].reshape(slots, y_ref.shape[2])
    residual = res_ref[...]
    info = info_ref[...]
    lane = lanes_of(info.shape)

    def column(at):
        return info[:, at : at + 1]

    gates = (column(choices + 4), column(choices + 5))
    normed = residual * column(choices + 6) * gain_ref[...]
    grad = grad_ref[...].astype(f32)
    vectors = (vec_ref[0:1, :], vec_ref[1:2, :])
    alphas = ((column(choices), column(choices + 1)), (column(choices + 2), column(choices + 3)))
    dot_normed = jnp.sum(grad * normed, axis=-1, keepdims=True)
    dot_vectors = [jnp.sum(grad * v, axis=-1, keepdims=True) for v in vectors]
    mixed = residual
    weight_normed = jnp.zeros_like(dot_normed)
    weight_copy = jnp.zeros_like(dot_normed)
    weight_const = [jnp.zeros_like(dot_normed), jnp.zeros_like(dot_normed)]
    grad_probs = jnp.zeros_like(info)
    slot = lanes_of((TB, slots))
    for j in range(2):
        route = rcol_ref[:, j : j + 1]
        hot = jnp.where(pcol_ref[:, j : j + 1] == slot, 1.0, 0.0).astype(bf16)
        rows_j = nn(hot, rows_out)
        is_copy = jnp.where(route == experts + 1, 1.0, 0.0)
        is_const = [jnp.where(route == experts + 2 + c, 1.0, 0.0) for c in range(2)]
        on_normed = is_copy + is_const[0] * alphas[0][0] + is_const[1] * alphas[1][0]
        grad_gate = jnp.sum(grad * rows_j, axis=-1, keepdims=True) + on_normed * dot_normed
        for c in range(2):
            grad_gate = grad_gate + is_const[c] * alphas[c][1] * dot_vectors[c]
            weight_const[c] = weight_const[c] + gates[j] * is_const[c]
        grad_probs = grad_probs + jnp.where(lane == route, grad_gate, 0.0)
        mixed = mixed + gates[j] * rows_j
        weight_normed = weight_normed + gates[j] * on_normed
        weight_copy = weight_copy + gates[j] * is_copy
    mixed = mixed + weight_normed * normed
    for c in range(2):
        mixed = mixed + weight_const[c] * alphas[c][1] * vectors[c]
    out_ref[...] = mixed.astype(bf16)
    is_choice = lane < choices
    probs = jnp.where(is_choice, info, 0.0)
    grad_small = probs * (grad_probs - jnp.sum(probs * grad_probs, axis=-1, keepdims=True))
    direct = weight_copy
    coefs = jnp.zeros_like(info)
    for c in range(2):
        grad_alpha = (weight_const[c] * dot_normed, weight_const[c] * dot_vectors[c])
        mean = alphas[c][0] * grad_alpha[0] + alphas[c][1] * grad_alpha[1]
        for k in range(2):
            grad_small = jnp.where(
                lane == choices + 2 * c + k, alphas[c][k] * (grad_alpha[k] - mean), grad_small
            )
        direct = direct + alphas[c][0] * weight_const[c]
        coefs = jnp.where(lane == c, alphas[c][1] * weight_const[c], coefs)
    high, mid, low = split3(grad_small)
    small_weights = sw_ref[...]
    part_ref[...] = direct * grad + (
        nt(high, small_weights) + nt(mid, small_weights) + nt(low, small_weights)
    )
    gating_t = gt_ref[...]
    logits_high, logits_mid, logits_low = split3(jnp.where(is_choice, grad_small, 0.0))
    grad_prev = nn(logits_high, gating_t) + nn(logits_mid, gating_t) + nn(logits_low, gating_t)
    gprev_ref[...] = grad_prev[:, :choices]
    normed_high, normed_mid = split2(normed)
    grad_sw = tn(high, normed_high) + tn(mid, normed_high) + tn(high, normed_mid)
    coef_high, coef_mid = split2(coefs)
    grad_vec = tn(coef_high, grad_ref[...]) + tn(coef_mid, grad_ref[...])
    prev = prev_ref[...]
    grad_gating = tn(prev, high) + tn(prev, mid) + tn(prev, low)

    @pl.when(step == 0)
    def _():
        gsw_ref[...] = grad_sw
        gvec_ref[...] = grad_vec
        ggat_ref[...] = grad_gating

    @pl.when(step > 0)
    def _():
        gsw_ref[...] += grad_sw
        gvec_ref[...] += grad_vec
        ggat_ref[...] += grad_gating


def combine_call(back, residual, info, rcols, pcols, grad, gain, vectors, small_weights, prev, gating_t):
    rows, width = residual.shape
    wide = info.shape[1]
    choices = prev.shape[1]
    slots = back.shape[0] * CAP

    def block(cols):
        return pl.BlockSpec((TB, cols), lambda i: (i, 0))

    return call(
        combine_kernel,
        (rows // TB,),
        [
            whole(back.shape), block(width), block(wide), block(2), block(2), block(width), whole(gain.shape),
            whole(vectors.shape), whole(small_weights.shape), block(choices), whole(gating_t.shape),
        ],
        [
            ((rows, width), bf16, block(width)),
            ((rows, width), f32, block(width)),
            ((rows, choices), f32, block(choices)),
            ((wide, width), f32, whole((wide, width))),
            ((wide, width), f32, whole((wide, width))),
            ((choices, wide), f32, whole((choices, wide))),
        ],
        (back, residual, info, rcols, pcols, grad, gain, vectors, small_weights, prev, gating_t),
        flops=4 * slots * rows * width,
        nbytes=14 * rows * width + 2 * slots * width,
    )


def residual_kernel(
    dx_ref, part_ref, res_ref, info_ref, pcol_ref, grad_ref, gain_ref, wo_ref, att_ref,
    gres_ref, gatt_ref, gwo_ref, ggain_ref, acc_ref,
):
    step = pl.program_id(0)
    experts = dx_ref.shape[0]
    slots = experts * CAP
    scale_at = info_ref.shape[1]
    del scale_at
    slot = lanes_of((TB, slots))
    hot = jnp.where(
        (pcol_ref[:, 0:1] == slot) | (pcol_ref[:, 1:2] == slot), 1.0, 0.0
    ).astype(bf16)
    grad_normed = part_ref[...] + nn(hot, dx_ref[...].reshape(slots, dx_ref.shape[2]))
    residual = res_ref[...]
    scale = lax.rsqrt(jnp.mean(residual * residual, axis=-1, keepdims=True) + norm_eps)
    unit = residual * scale
    grad_gain = jnp.sum(grad_normed * unit, axis=0, keepdims=True)
    scaled = grad_normed * gain_ref[...]
    grad_residual = grad_ref[...].astype(f32) + scale * (
        scaled - unit * jnp.mean(scaled * unit, axis=-1, keepdims=True)
    )
    gres_ref[...] = grad_residual
    low = grad_residual.astype(bf16)
    gatt_ref[...] = nt(low, wo_ref[...]).astype(bf16)
    grad_out = tn(att_ref[...], low)

    @pl.when(step == 0)
    def _():
        acc_ref[...] = grad_out
        ggain_ref[...] = grad_gain

    @pl.when(step > 0)
    def _():
        acc_ref[...] += grad_out
        ggain_ref[...] += grad_gain

    @pl.when(step == pl.num_programs(0) - 1)
    def _():
        gwo_ref[...] = acc_ref[...].astype(bf16)


def residual_call(dx, part, residual, info, pcols, grad, gain, w_out, attended):
    rows, width = residual.shape
    wide = info.shape[1]
    slots = dx.shape[0] * CAP

    def block(cols):
        return pl.BlockSpec((TB, cols), lambda i: (i, 0))

    return call(
        residual_kernel,
        (rows // TB,),
        [
            whole(dx.shape), block(width), block(width), block(wide), block(2), block(width), whole(gain.shape),
            whole(w_out.shape), block(width),
        ],
        [
            ((rows, width), f32, block(width)),
            ((rows, width), bf16, block(width)),
            ((width, width), bf16, whole((width, width))),
            ((1, width), f32, whole((1, width))),
        ],
        (dx, part, residual, info, pcols, grad, gain, w_out, attended),
        scratch=[pltpu.VMEM((width, width), f32)],
        flops=2 * slots * rows * width + 4 * rows * width * width,
        nbytes=18 * rows * width + 2 * slots * width,
    )


def qkv_weights_kernel(dq_ref, dk_ref, dv_ref, n_ref, out_ref):
    normed = n_ref[...]
    for part, ref in enumerate((dq_ref, dk_ref, dv_ref)):
        out_ref[part] = tn(ref[...], normed).astype(bf16)


def qkv_weights_call(dq, dk, dv, normed):
    rows, width = normed.shape
    col = pl.BlockSpec((rows, 256), lambda c: (0, c))
    return call(
        qkv_weights_kernel,
        (width // 256,),
        [col, col, col, whole((rows, width))],
        [((3, width, width), bf16, pl.BlockSpec((3, 256, width), lambda c: (0, c, 0)))],
        (dq, dk, dv, normed),
        flops=6 * rows * width * width,
        nbytes=8 * rows * width + 6 * width * width,
    )[0]


def hidden_kernel(dq_ref, dk_ref, dv_ref, w_ref, hid_ref, gain_ref, gres_ref, out_ref, ggain_ref):
    step = pl.program_id(0)
    grad_normed = nn(dq_ref[...], w_ref[0]) + nn(dk_ref[...], w_ref[1]) + nn(dv_ref[...], w_ref[2])
    hidden = hid_ref[...].astype(f32)
    scale = lax.rsqrt(jnp.mean(hidden * hidden, axis=-1, keepdims=True) + norm_eps)
    unit = hidden * scale
    grad_gain = jnp.sum(grad_normed * unit, axis=0, keepdims=True)
    scaled = grad_normed * gain_ref[...]
    out_ref[...] = gres_ref[...] + scale * (
        scaled - unit * jnp.mean(scaled * unit, axis=-1, keepdims=True)
    )

    @pl.when(step == 0)
    def _():
        ggain_ref[...] = grad_gain

    @pl.when(step > 0)
    def _():
        ggain_ref[...] += grad_gain


def hidden_call(dq, dk, dv, weights, hidden, gain, grad_residual):
    rows, width = hidden.shape
    row = pl.BlockSpec((TB, width), lambda i: (i, 0))
    return call(
        hidden_kernel,
        (rows // TB,),
        [row, row, row, whole(weights.shape), row, whole(gain.shape), row],
        [((rows, width), f32, row), ((1, width), f32, whole((1, width)))],
        (dq, dk, dv, weights, hidden, gain, grad_residual),
        flops=6 * rows * width * width,
        nbytes=16 * rows * width + 6 * width * width,
    )


def rope_wide(length):
    inverse = rope_base ** (-(2.0 * jnp.arange(HD // 2, dtype=f32)) / HD)
    angles = jnp.arange(length, dtype=f32)[:, None] * inverse[None, :]
    cosine, sine = jnp.cos(angles), jnp.sin(angles)
    return (
        jnp.concatenate([cosine] * 4, axis=1),
        jnp.concatenate([-sine, sine, -sine, sine], axis=1),
    )


def to_rows(flat, width):
    count = -(-flat.shape[1] // width)
    return jnp.pad(flat, ((0, 0), (0, count * width - flat.shape[1]))).reshape(
        flat.shape[0], count, width
    )


def per_device(
    hidden_in,
    prev_logits,
    seq_lengths,
    seq_order,
    routes,
    w_query,
    w_key,
    w_value,
    w_output,
    gain_attn,
    gain_moe,
    w_router,
    w_gating,
    w_const,
    v_const,
    w_gate,
    w_up,
    w_down,
    out_grad,
):
    rows, width = hidden_in.shape[1:]
    experts = lax.axis_size("expert")
    shards = lax.axis_size("fsdp")
    choices = w_router.shape[1]
    part = width // shards
    hidden = hidden_in.reshape(rows, width)
    grad = out_grad.reshape(rows, width)
    prev = prev_logits.reshape(rows, choices)

    fsdp_here = lax.axis_index("fsdp")
    own = lax.axis_index("expert") * shards + fsdp_here
    live = lax.dynamic_slice(seq_lengths, (own,), (1,))
    dealt = lax.all_gather(routes.reshape(rows, 2).T, "expert", axis=0, tiled=False)
    peers = jnp.arange(experts, dtype=i32) * shards + fsdp_here
    mine = seq_order[peers] == own
    route_rows = jnp.sum(jnp.where(mine[:, None, None], dealt, 0), axis=0)
    ids = jnp.arange(experts, dtype=i32)
    named = (route_rows[0][None, :] == ids[:, None]) | (route_rows[1][None, :] == ids[:, None])
    at = jnp.arange(rows, dtype=i32)
    earlier = (at[:, None] < at[None, :]).astype(bf16)
    counts = nn(named.astype(bf16), earlier).astype(i32)
    place_rows = jnp.stack(
        [
            jnp.where(
                r < experts,
                r * CAP + jnp.sum(jnp.where(r[None, :] == ids[:, None], counts, 0), axis=0),
                -1,
            )
            for r in (route_rows[0], route_rows[1])
        ]
    )
    route_cols = route_rows.T
    place_cols = place_rows.T
    cos_wide, sin_wide = rope_wide(rows)

    small_parts = jnp.concatenate(
        [gain_attn[:, None], gain_moe[:, None], w_router, w_const, v_const.T], axis=1
    )
    small_count = small_parts.shape[1]
    small_rows = to_rows(small_parts.T.reshape(1, -1), width)[0]
    first_pack = jnp.concatenate([w_query.T, w_key.T, w_value.T, small_rows], axis=0)
    first = lax.all_gather(first_pack, "fsdp", axis=0, tiled=False)
    w_out = lax.all_gather(w_output, "fsdp", axis=0, tiled=True)
    expert_pack = jnp.stack([w_gate[0].T, w_up[0].T, w_down[0]])
    expert_weights = lax.all_gather(expert_pack, "fsdp", axis=0, tiled=False)

    qkv_weights = (
        first[:, : 3 * part].reshape(shards, 3, part, width).transpose(1, 0, 2, 3).reshape(3, width, width)
    )
    small = (
        first[:, 3 * part :]
        .reshape(shards, -1)[:, : small_count * part]
        .reshape(shards, small_count, part)
        .transpose(1, 0, 2)
        .reshape(small_count, width)
    )
    gain_one = small[0:1].astype(f32)
    gain_two = small[1:2].astype(f32)
    small_weights = jnp.pad(small[2 : choices + 6].T, ((0, 0), (0, 128 - choices - 4)))
    vectors = small[choices + 6 :].astype(f32)
    gating_wide = jnp.pad(w_gating, ((0, 0), (0, 128 - choices)))
    gating_t = jnp.pad(w_gating.T, ((0, 128 - choices), (0, 128 - choices)))

    query, key, value, normed_one = qkv_call(hidden, gain_one, qkv_weights, cos_wide, sin_wide)
    attended, recip, expo = attend_call(live, query, key, value)
    residual, info, send = route_call(
        attended, hidden, grad, w_out, gain_two, small_weights, prev, gating_wide, route_cols, place_rows, experts
    )
    sent = lax.all_to_all(send, "expert", split_axis=0, concat_axis=0, tiled=True)
    expert_out, inner, factor_a, factor_b = expert_call(sent, expert_weights)
    returned = lax.all_to_all(expert_out, "expert", split_axis=0, concat_axis=0, tiled=True)
    expert_dx, dgu = expert_back_call(sent, expert_weights, factor_a, factor_b)
    returned_dx = lax.all_to_all(expert_dx, "expert", split_axis=0, concat_axis=0, tiled=True)
    expert_dw = expert_weights_call(sent, inner, dgu, expert_weights.shape)
    expert_sum = lax.psum_scatter(expert_dw, "fsdp", scatter_dimension=0, tiled=False)

    hidden_out, part_grad, grad_prev, grad_sw, grad_vec, grad_gating = combine_call(
        returned, residual, info, route_cols, place_cols, grad, gain_two, vectors, small_weights, prev, gating_t
    )
    grad_residual, grad_attended, grad_wo, grad_gain_two = residual_call(
        returned_dx, part_grad, residual, info, place_cols, grad, gain_two, w_out, attended
    )
    dq, dk, dv = attend_back_call(
        query, key, value, expo, grad_attended, attended, recip, cos_wide, sin_wide
    )
    grad_qkv = qkv_weights_call(dq, dk, dv, normed_one)
    grad_hidden, grad_gain_one = hidden_call(
        dq, dk, dv, qkv_weights, hidden, gain_one, grad_residual
    )

    small_grads = jnp.concatenate(
        [grad_gain_one, grad_gain_two, grad_sw[: choices + 4], grad_vec[:2]], axis=0
    )
    small_flat = small_grads.reshape(small_count, shards, part).transpose(1, 0, 2).reshape(shards, -1)
    gating_flat = grad_gating[:, :choices].reshape(1, -1)
    gating_high = gating_flat.astype(bf16)
    gating_low = (gating_flat - gating_high.astype(f32)).astype(bf16)
    gating_both = jnp.concatenate([gating_high, gating_low], axis=1)
    flat = jnp.concatenate(
        [small_flat.astype(bf16), jnp.broadcast_to(gating_both, (shards, gating_both.shape[1]))], axis=1
    )
    shared = jnp.concatenate(
        [
            grad_qkv.reshape(3, shards, part, width).transpose(1, 0, 2, 3).reshape(shards, 3 * part, width),
            grad_wo.reshape(shards, part, width),
            to_rows(flat, width),
        ],
        axis=1,
    )
    scattered = lax.psum_scatter(shared, "fsdp", scatter_dimension=0, tiled=False)
    total = lax.psum(scattered, "expert").astype(f32)
    flat_total = total[4 * part :].reshape(-1)
    small_total = flat_total[: small_count * part].reshape(small_count, part)
    gating_at = small_count * part
    pair_total = flat_total[gating_at : gating_at + 2 * choices * choices].reshape(2, choices, choices)
    expert_total = expert_sum.astype(f32)
    return (
        hidden_out[None],
        grad_hidden[None],
        grad_prev[None],
        total[:part].T,
        total[part : 2 * part].T,
        total[2 * part : 3 * part].T,
        total[3 * part : 4 * part],
        small_total[0],
        small_total[1],
        small_total[2 : choices + 2].T,
        pair_total[0] + pair_total[1],
        small_total[choices + 2 : choices + 6].T,
        small_total[choices + 6 :],
        expert_total[0].T[None],
        expert_total[1].T[None],
        expert_total[2][None],
    )


def solution(mesh):
    rows = P(("expert", "fsdp"), None, None)
    ins = (
        rows, rows, P(), P(), rows,
        P(None, "fsdp"), P(None, "fsdp"), P(None, "fsdp"), P("fsdp", None),
        P("fsdp"), P("fsdp"), P("fsdp", None), P(), P("fsdp", None), P(None, "fsdp"),
        P("expert", None, "fsdp"), P("expert", None, "fsdp"), P("expert", "fsdp", None), rows,
    )
    outs = (
        rows, rows, rows,
        P(None, "fsdp"), P(None, "fsdp"), P(None, "fsdp"), P("fsdp", None),
        P("fsdp"), P("fsdp"), P("fsdp", None), P(), P("fsdp", None), P(None, "fsdp"),
        P("expert", None, "fsdp"), P("expert", None, "fsdp"), P("expert", "fsdp", None),
    )
    return jax.shard_map(per_device, mesh=mesh, in_specs=ins, out_specs=outs, check_vma=False)
```

time: 1630 us -> 726 us (0.45)
  other arithmetic: 259 us -> 14.9 us
  matrix products: 242 us -> 0.33 us
  blocking collectives: 236 us -> 46.8 us
  local copies, waits for them, and re-layouts: 244 us -> 58.4 us
  Pallas kernels: 0 us -> 176 us
  waiting for transfers between devices: 574 us -> 404 us
  starting transfers between devices: 41.9 us -> 8.93 us
    dot_general x30 -> x1, matrix products: 242 us -> 0.33 us  [nn(): lax.dot_general(a, b, (((1,), (0,)), ((), ())), preferred_element_type=f32)]
    unnamed x24 -> x6, waiting for transfers between devices: 181 us -> 0.78 us
    pallas_call x0 -> x11, Pallas kernels: none -> 176 us  [call(): pl.pallas_call(kernel, grid=grid, in_specs=ins, out_specs=[o[2] for o in...]
    all_to_all x9 -> x2, waiting for transfers between devices: 152 us -> 0.01 us  [the longest x1 0.01 us: per_device(): lax.all_to_all(expert_out, 'expert', split_axis=0, concat_axis=0, tiled=T...]
    reduce_sum x15 -> x1, other arithmetic: 146 us -> 0.09 us  [per_device(): route_rows = jnp.sum(jnp.where(mine[:, None, None], dealt, 0), axis=0)]
    all_gather x7 -> x3, waiting for transfers between devices: 0.06 us -> 131 us  [the longest x1 77.5 us: per_device(): expert_weights = lax.all_gather(expert_pack, 'fsdp', axis=0, tiled=False)]
    psum x2 -> x0, blocking collectives: 109 us -> none  [the longest x1 102 us: per_device(): gating_total = lax.psum(grad_gating, ('expert', 'fsdp'))]
    convert_element_type x21 -> x5, other arithmetic: 73.2 us -> 2.63 us  [the longest x1 1.47 us: per_device(): expert_total = expert_sum.astype(f32)]
  transfers between devices with their start and end apart: 27 -> 8, of which waited for: 11 -> 5; matrix products, arithmetic and copies ran while one was open for 23% -> 3% of each run, Pallas kernels for 0% -> 15%
where the time goes in v1:
time: 726 us; the launch traced here: 724 us
  waiting for transfers between devices  404 us (56%)
  Pallas kernels  176 us (24%)
  local copies, waits for them, and re-layouts  58.4 us (8%)
  blocking collectives  46.8 us (6%)
  other arithmetic  14.9 us (2%)
  between operations  14.5 us (2%)
  starting transfers between devices  8.93 us (1%)
    pallas_call x11, Pallas kernels, call(): pl.pallas_call(kernel, grid=grid, in_specs=ins, out_specs=[o[2] for o in...  176 us
    reduce_scatter x1, waiting for transfers between devices, per_device(): lax.psum_scatter(expert_dw, 'fsdp', scatter_dimension=0, tiled=False)  159 us
    reduce_scatter x1, waiting for transfers between devices, per_device(): lax.psum_scatter(shared, 'fsdp', scatter_dimension=0, tiled=False)  95.9 us
    all_gather x1, waiting for transfers between devices, per_device(): expert_weights = lax.all_gather(expert_pack, 'fsdp', axis=0, tiled=False)  77.5 us
    all_gather x1, waiting for transfers between devices, per_device(): first = lax.all_gather(first_pack, 'fsdp', axis=0, tiled=False)  53.6 us
    all_to_all x1, blocking collectives, per_device(): lax.all_to_all(send, 'expert', split_axis=0, concat_axis=0, tiled=True)  40.6 us
    unnamed x91, local copies, waits for them, and re-layouts  34.7 us
    psum x1, waiting for transfers between devices, per_device(): total = lax.psum(scattered, 'expert').astype(f32)  17.6 us
  transfers between devices with their start and end apart: 8, of which 5 were waited for; matrix products, arithmetic and copies ran while one was open for 3% of the time, Pallas kernels for 15%

profile of v1, /device:TPU:0, one launch (start us, length us, event | category | flops | bytes accessed | tf_op | source)
XLA Modules:
  0.0 723.9 jit_solution(1414458763688463693)
XLA Ops:
  7.3 2.2 concatenate.25
  9.6 1.9 maximum_bitcast_fusion
  12.3 1.2 copy.67
  13.5 1.2 copy.68
  14.6 1.1 pad_maximum_fusion.1
  16.5 6.2 all-gather.4
  24.2 2.0 fusion.4
  26.2 0.9 pad_maximum_fusion.2
  27.1 53.6 %all-gather.13.cloned.1.call-done = bf16[8,290,768]{2,1,0:T(8,128)(2,1)} async-done(((bf16[1,290,768]{2,1,0:T(8,128)(2,1)}), bf16[8,290,768]{2,1,0:T(8,128)(2,1)}) %all-gather.13.cloned.1.call-update) | async-done | bytes 3563536 | tf_op jit(solution)/shard_map/all_gather | solution.py:783
  80.7 0.9 slice.141
  81.8 2.0 slice-done
  83.8 2.0 copy.63
  86.2 10.2 %shard_map.306 = (bf16[1024,768]{1,0:T(8,128)(2,1)S(1)}, bf16[1024,768]{1,0:T(8,128)(2,1)S(1)}, bf16[1024,768]{1,0:T(8,128)(2,1)S(1)}, bf16[1024,768]{1,0:T(8,128)(2,1)}) custom-call(bf16[1024,768]{1,0:T(8,128)(2,1)} %bitcast.99, f32[1,768]{1,0:T(1,128)S(1)} %reshape.208.gain_ref, bf16[3,768,768]{2,1,0:T(8,128)(2,1)} %bitcast.104, ...), custom_call_target="tpu_custom_call" | custom-call | flops 3623878656 | bytes 11403264 | tf_op jit(solution)/shard_map/pallas_call | solution.py:45
  96.4 1.1 copy-done.33
  97.5 22.2 %shard_map.307 = (bf16[1024,768]{1,0:T(8,128)(2,1)S(1)}, f32[1024,768]{1,0:T(8,128)}, bf16[6,2,10,256,256]{4,3,2,1,0:T(8,128)(2,1)}) custom-call(s32[1]{0:T(128)} %dynamic_slice.3.len_ref, bf16[1024,768]{1,0:T(8,128)(2,1)S(1)} %get-tuple-element.47.q_ref, bf16[1024,768]{1,0:T(8,128)(2,1)S(1)} %get-tuple-element.48.k_ref, bf16[1024,768]{1,0:T(8,128)(2,1)} %copy-done.33), custom_call_target="tpu_custom_call" | custom-call | flops 4026531840 | bytes 25165824 | tf_op jit(solution)/shard_map/pallas_call | solution.py:45
  119.7 1.1 copy-done.28
  120.8 1.2 copy-done.31
  122.0 1.1 copy-done.32
  123.2 1.4 copy-done.19
  124.6 1.3 copy-done.20
  125.8 1.4 copy-done.29
  127.3 15.9 %shard_map.308 = (f32[1024,768]{1,0:T(8,128)}, f32[1024,128]{1,0:T(8,128)S(1)}, bf16[4,512,768]{2,1,0:T(8,128)(2,1)}) custom-call(bf16[1024,768]{1,0:T(8,128)(2,1)S(1)} %copy-done.29, bf16[1024,768]{1,0:T(8,128)(2,1)S(1)} %bitcast.101, bf16[1024,768]{1,0:T(8,128)(2,1)} %bitcast.130, bf16[768,768]{1,0:T(8,128)(2,1)S(1)} %copy-done.20, ...), custom_call_target="tpu_custom_call" | custom-call | flops 6039797760 | bytes 12189696 | tf_op jit(solution)/shard_map/pallas_call | solution.py:45
  143.2 0.8 copy-done.34
  144.0 40.6 %all_to_all.15.x_ref.g_ref = bf16[4,512,768]{2,1,0:T(8,128)(2,1)S(1)} all-to-all(bf16[4,512,768]{2,1,0:T(8,128)(2,1)} %get-tuple-element.51), channel_id=1, replica_groups=mesh['expert'=4,'fsdp'=8] {'expert'}, dimensions={0} | all-to-all | bytes 6291456 | tf_op jit(solution)/shard_map/all_to_all | solution.py:810
  184.6 77.5 %all-gather.11.cloned.1.call-done = bf16[24,256,768]{2,1,0:T(8,128)(2,1)} async-done(((bf16[3,256,768]{2,1,0:T(8,128)(2,1)}), bf16[24,256,768]{2,1,0:T(8,128)(2,1)}) %all-gather.11.cloned.1.call-update) | async-done | bytes 9437200 | tf_op jit(solution)/shard_map/all_gather | solution.py:786
  262.1 18.2 %shard_map.309 = (bf16[4,256,768]{2,1,0:T(8,128)(2,1)S(1)}, bf16[8,1024,256]{2,1,0:T(8,128)(2,1)}, bf16[8,1024,256]{2,1,0:T(8,128)(2,1)}, bf16[8,1024,256]{2,1,0:T(8,128)(2,1)}) custom-call(bf16[4,512,768]{2,1,0:T(8,128)(2,1)S(1)} %all_to_all.15.x_ref.g_ref, bf16[8,3,256,768]{3,2,1,0:T(8,128)(2,1)} %bitcast.128), custom_call_target="tpu_custom_call" | custom-call | flops 9663676416 | bytes 25165824 | tf_op jit(solution)/shard_map/pallas_call | solution.py:45
  280.2 1.1 copy-done.3
  281.4 4.3 all-to-all-start.1
  285.7 23.0 %shard_map.311 = (bf16[4,256,768]{2,1,0:T(8,128)(2,1)S(1)}, bf16[8,2,1024,256]{3,2,1,0:T(8,128)(2,1)}) custom-call(bf16[4,512,768]{2,1,0:T(8,128)(2,1)S(1)} %all_to_all.15.x_ref.g_ref, bf16[8,3,256,768]{3,2,1,0:T(8,128)(2,1)} %bitcast.129, bf16[8,1024,256]{2,1,0:T(8,128)(2,1)} %get-tuple-element.57.fa_ref, bf16[8,1024,256]{2,1,0:T(8,128)(2,1)} %get-tuple-element.58.fb_ref), custom_call_target="tpu_custom_call" | custom-call | flops 9663676416 | bytes 25165824 | tf_op jit(solution)/shard_map/pallas_call | solution.py:45
  308.7 1.2 copy-done.2
  309.9 4.3 all-to-all-start.2
  314.3 1.0 copy.69
  315.5 1.0 copy-done.12
  316.6 1.0 copy-done.13
  317.6 0.9 copy-done.16
  318.6 1.0 copy-done.35
  319.6 19.5 %shard_map.310 = (bf16[1024,768]{1,0:T(8,128)(2,1)}, f32[1024,768]{1,0:T(8,128)}, f32[1024,8]{1,0:T(8,128)S(1)}, f32[128,768]{1,0:T(8,128)S(1)}, f32[128,768]{1,0:T(8,128)S(1)}, /*index=5*/f32[8,128]{1,0:T(8,128)S(1)}) custom-call(bf16[4,256,768]{2,1,0:T(8,128)(2,1)} %all-to-all-done.1.y_ref, f32[1024,768]{1,0:T(8,128)} %get-tuple-element.53.res_ref, ...), custom_call_target="tpu_custom_call" | custom-call | flops 3221225472 | bytes 12582912 | tf_op jit(solution)/shard_map/pallas_call | solution.py:45
  341.4 1.0 copy-done.14
  342.4 1.3 copy-done.21
  343.7 1.0 copy-done.36
  344.7 12.7 %shard_map.312 = (f32[1024,768]{1,0:T(8,128)}, bf16[1024,768]{1,0:T(8,128)(2,1)S(1)}, bf16[768,768]{1,0:T(8,128)(2,1)S(1)}, f32[1,768]{1,0:T(1,128)S(1)}) custom-call(bf16[4,256,768]{2,1,0:T(8,128)(2,1)} %all-to-all-done.2.dx_ref, f32[1024,768]{1,0:T(8,128)} %get-tuple-element.60.part_ref, f32[1024,768]{1,0:T(8,128)} %get-tuple-element.53.res_ref, ...), custom_call_target="tpu_custom_call" | custom-call | flops 4026531840 | bytes 15728640 | tf_op jit(solution)/shard_map/pallas_call | solution.py:45
  357.4 1.0 copy-done.4
  358.4 1.2 copy-done.30
  359.6 21.9 %shard_map.313 = (bf16[1024,768]{1,0:T(8,128)(2,1)S(1)}, bf16[1024,768]{1,0:T(8,128)(2,1)S(1)}, bf16[1024,768]{1,0:T(8,128)(2,1)S(1)}) custom-call(bf16[1024,768]{1,0:T(8,128)(2,1)} %copy-done.31, bf16[1024,768]{1,0:T(8,128)(2,1)} %copy-done.32, bf16[1024,768]{1,0:T(8,128)(2,1)} %copy-done.33, bf16[6,2,10,256,256]{4,3,2,1,0:T(8,128)(2,1)} %get-tuple-element.56.e_ref, ...), custom_call_target="tpu_custom_call" | custom-call | flops 8053063680 | bytes 33030144 | tf_op jit(solution)/shard_map/pallas_call | solution.py:45
  381.5 8.2 %shard_map.315 = bf16[3,768,768]{2,1,0:T(8,128)(2,1)} custom-call(bf16[1024,768]{1,0:T(8,128)(2,1)S(1)} %get-tuple-element.63.dq_ref, bf16[1024,768]{1,0:T(8,128)(2,1)S(1)} %get-tuple-element.64.dk_ref, bf16[1024,768]{1,0:T(8,128)(2,1)S(1)} %get-tuple-element.65.dv_ref, bf16[1024,768]{1,0:T(8,128)(2,1)} %get-tuple-element.69.n_ref), custom_call_target="tpu_custom_call" | custom-call | flops 3623878656 | bytes 9830400 | tf_op jit(solution)/shard_map/pallas_call | solution.py:45
  389.7 4.0 copy.71
  393.8 1.4 copy-done.23
  395.2 1.4 copy-done.25
  396.6 1.4 copy-done.27
  398.0 8.9 %shard_map.314 = (f32[1024,768]{1,0:T(8,128)}, f32[1,768]{1,0:T(1,128)S(1)}) custom-call(bf16[1024,768]{1,0:T(8,128)(2,1)S(1)} %copy-done.23, bf16[1024,768]{1,0:T(8,128)(2,1)S(1)} %copy-done.25, bf16[1024,768]{1,0:T(8,128)(2,1)S(1)} %copy-done.27, bf16[3,768,768]{2,1,0:T(8,128)(2,1)} %bitcast.105, bf16[1024,768]{1,0:T(8,128)(2,1)} %bitcast.100, ...), custom_call_target="tpu_custom_call" | custom-call | flops 3623878656 | bytes 16121856 | tf_op jit(solution)/shard_map/pallas_call | solution.py:45
  407.0 0.8 slice.186
  408.9 5.6 pad_maximum_fusion
  414.5 95.9 %reduce-scatter.3.cloned.1.call-done = bf16[1,387,768]{2,1,0:T(8,128)(2,1)} async-done(((bf16[8,387,768]{2,1,0:T(8,128)(2,1)}), bf16[1,387,768]{2,1,0:T(8,128)(2,1)}) %reduce-scatter.3.cloned.1.call-update) | async-done | bytes 594448 | tf_op jit(solution)/shard_map/reduce_scatter | solution.py:851
  510.5 15.3 %shard_map.316 = bf16[8,3,256,768]{3,2,1,0:T(8,128)(2,1)} custom-call(bf16[4,512,768]{2,1,0:T(8,128)(2,1)S(1)} %all_to_all.15.x_ref.g_ref, bf16[4,512,768]{2,1,0:T(8,128)(2,1)S(1)} %all_to_all.15.x_ref.g_ref, bf16[8,1024,256]{2,1,0:T(8,128)(2,1)} %get-tuple-element.76.inner_ref, bf16[8,2,1024,256]{3,2,1,0:T(8,128)(2,1)} %get-tuple-element.77.dgu_ref), custom_call_target="tpu_custom_call" | custom-call | flops 9663676416 | bytes 25165824 | tf_op jit(solution)/shard_map/pallas_call | solution.py:45
  525.9 1.0 copy-done.10
  527.7 17.6 %all-reduce.6.cloned.1.call-done = bf16[387,768]{1,0:T(8,128)(2,1)} async-done(((bf16[387,768]{1,0:T(8,128)(2,1)}), bf16[387,768]{1,0:T(8,128)(2,1)}) %all-reduce.6.cloned.1.call-update) | async-done | bytes 594448 | tf_op jit(solution)/shard_map/psum | solution.py:852
  547.4 1.1 convert_element_type.95
  548.6 1.6 slice.154
  552.5 0.9 slice_bitcast_fusion.3
  553.5 158.8 %reduce-scatter.5.cloned.1.call-done = bf16[1,3,256,768]{3,2,1,0:T(8,128)(2,1)} async-done(((bf16[8,3,256,768]{3,2,1,0:T(8,128)(2,1)}), bf16[1,3,256,768]{3,2,1,0:T(8,128)(2,1)}) %reduce-scatter.5.cloned.1.call-update) | async-done | bytes 1179664 | tf_op jit(solution)/shard_map/reduce_scatter | solution.py:816
  712.2 1.5 convert_element_type.96
  713.7 1.0 slice_bitcast_fusion
  714.7 1.1 copy.74
  715.9 1.1 copy.75
  (128 shorter events, 12.8 us)
Async XLA Ops:
  7.2 8.7 %copy-start = (s32[32]{0:T(128)S(1)}, s32[32]{0:T(128)}, u32[]{:S(2)}) copy-start(s32[32]{0:T(128)} %param.22) | copy-start | bytes 388
  7.2 7.4 %copy-start.37 = (bf16[1,256,768]{2,1,0:T(8,128)(2,1)S(1)}, bf16[1,256,768]{2,1,0:T(8,128)(2,1)}, u32[]{:S(2)}) copy-start(bf16[1,256,768]{2,1,0:T(8,128)(2,1)} %param.36) | copy-start | bytes 1179652
  7.2 73.5 %all-gather.13.cloned.1.call-start = ((), (), s32[]{:S(2)}) async-start(), calls=%async_computation.10 | async-start | bytes 4091904 | tf_op jit(solution)/shard_map/all_gather | solution.py:783
  11.4 5.1 copy-start.39
  11.4 111.7 %all-gather.9.cloned.1.call-start = ((), (), s32[]{:S(2)}) async-start(), calls=%async_computation.5 | async-start | bytes 1327104 | tf_op jit(solution)/shard_map/all_gather | solution.py:784
  12.2 10.8 %copy-start.38 = (bf16[1,1024,8]{1,2,0:T(8,128)(2,1)S(1)}, bf16[1,1024,8]{1,2,0:T(8,128)(2,1)}, u32[]{:S(2)}) copy-start(bf16[1,1024,8]{1,2,0:T(8,128)(2,1)} %param.20) | copy-start | bytes 49156
  12.2 11.0 %copy-start.41 = (s32[32]{0:T(128)S(1)}, s32[32]{0:T(128)}, u32[]{:S(2)}) copy-start(s32[32]{0:T(128)} %param.21) | copy-start | bytes 388
  12.2 11.6 %copy-start.40 = (bf16[8,8]{1,0:T(8,128)(2,1)S(1)}, bf16[8,8]{1,0:T(8,128)(2,1)}, u32[]{:S(2)}) copy-start(bf16[8,8]{1,0:T(8,128)(2,1)} %param.31) | copy-start | bytes 388
  12.2 249.8 %all-gather.11.cloned.1.call-start = ((), (), s32[]{:S(2)}) async-start(), calls=%async_computation.9 | async-start | bytes 10616832 | tf_op jit(solution)/shard_map/all_gather | solution.py:786
  23.0 100.2 %copy-start.11 = (s32[2,1024]{0,1:T(8,128)}, s32[2,1024]{0,1:T(8,128)S(1)}, u32[]{:S(2)}) copy-start(s32[2,1024]{0,1:T(8,128)S(1)} %copy.66) | copy-start | bytes 24580
  27.0 59.1 %copy-start.5 = (f32[1024,128]{1,0:T(8,128)}, f32[1024,128]{1,0:T(8,128)S(1)}, u32[]{:S(2)}) copy-start(f32[1024,128]{1,0:T(8,128)S(1)} %get-tuple-element.147.cos_ref) | copy-start | bytes 1572868
  27.1 59.1 %copy-start.7 = (f32[1024,128]{1,0:T(8,128)}, f32[1024,128]{1,0:T(8,128)S(1)}, u32[]{:S(2)}) copy-start(f32[1024,128]{1,0:T(8,128)S(1)} %get-tuple-element.148.sin_ref) | copy-start | bytes 1572868
  81.8 2.0 slice-start
  86.2 37.0 %copy-start.15 = (bf16[768,128]{1,0:T(8,128)(2,1)}, bf16[768,128]{1,0:T(8,128)(2,1)S(1)}, u32[]{:S(2)}) copy-start(bf16[768,128]{1,0:T(8,128)(2,1)S(1)} %pad.16.sw_ref) | copy-start | bytes 589828
  96.4 1.1 copy-start.33
  119.7 1.1 copy-start.28
  120.8 1.2 copy-start.31
  122.0 1.1 copy-start.32
  123.2 1.4 copy-start.19
  124.6 1.3 copy-start.20
  125.8 1.4 copy-start.29
  143.2 0.8 copy-start.34
  280.2 1.1 copy-start.3
  281.4 28.6 %all-to-all-start.1 = ((bf16[4,256,768]{2,1,0:T(8,128)(2,1)}), bf16[4,256,768]{2,1,0:T(8,128)(2,1)}, u32[]{:S(2)}, u32[]{:S(2)}) async-start(bf16[4,256,768]{2,1,0:T(8,128)(2,1)} %copy-done.3), calls=%async_computation.1 | async-start | bytes 3145728 | tf_op jit(solution)/shard_map/all_to_all | solution.py:812
  308.7 1.2 copy-start.2
  309.9 31.4 %all-to-all-start.2 = ((bf16[4,256,768]{2,1,0:T(8,128)(2,1)}), bf16[4,256,768]{2,1,0:T(8,128)(2,1)}, u32[]{:S(2)}, u32[]{:S(2)}) async-start(bf16[4,256,768]{2,1,0:T(8,128)(2,1)} %copy-done.2), calls=%async_computation.2 | async-start | bytes 3145728 | tf_op jit(solution)/shard_map/all_to_all | solution.py:814
  314.3 196.2 %reduce-scatter.3.cloned.1.call-start = ((), (), s32[]{:S(2)}) async-start(), calls=%async_computation.6 | async-start | bytes 5419008 | tf_op jit(solution)/shard_map/reduce_scatter | solution.py:851
  315.5 1.0 copy-start.12
  316.6 1.0 copy-start.13
  317.6 0.9 copy-start.16
  318.6 1.0 copy-start.35
  339.1 0.8 copy-start.9
  339.9 0.8 copy-start.17
  340.6 0.7 copy-start.18
  341.4 1.0 copy-start.14
  342.4 1.3 copy-start.21
  343.7 1.0 copy-start.36
  344.7 14.9 %copy-start.6 = (f32[1024,128]{1,0:T(8,128)S(1)}, f32[1024,128]{1,0:T(8,128)}, u32[]{:S(2)}) copy-start(f32[1024,128]{1,0:T(8,128)} %copy-done.5) | copy-start | bytes 1572868
  344.7 14.9 %copy-start.8 = (f32[1024,128]{1,0:T(8,128)S(1)}, f32[1024,128]{1,0:T(8,128)}, u32[]{:S(2)}) copy-start(f32[1024,128]{1,0:T(8,128)} %copy-done.7) | copy-start | bytes 1572868
  357.4 1.0 copy-start.4
  358.4 1.2 copy-start.30
  381.5 8.2 %copy-start.22 = (bf16[1024,768]{1,0:T(8,128)(2,1)}, bf16[1024,768]{1,0:T(8,128)(2,1)S(1)}, u32[]{:S(2)}) copy-start(bf16[1024,768]{1,0:T(8,128)(2,1)S(1)} %get-tuple-element.63.dq_ref) | copy-start | bytes 4718596
  381.5 8.2 %copy-start.24 = (bf16[1024,768]{1,0:T(8,128)(2,1)}, bf16[1024,768]{1,0:T(8,128)(2,1)S(1)}, u32[]{:S(2)}) copy-start(bf16[1024,768]{1,0:T(8,128)(2,1)S(1)} %get-tuple-element.64.dk_ref) | copy-start | bytes 4718596
  381.5 8.2 %copy-start.26 = (bf16[1024,768]{1,0:T(8,128)(2,1)}, bf16[1024,768]{1,0:T(8,128)(2,1)S(1)}, u32[]{:S(2)}) copy-start(bf16[1024,768]{1,0:T(8,128)(2,1)S(1)} %get-tuple-element.65.dv_ref) | copy-start | bytes 4718596
  393.8 1.4 copy-start.23
  395.2 1.4 copy-start.25
  396.6 1.4 copy-start.27
  414.5 130.8 %all-reduce.6.cloned.1.call-start = ((), (), s32[]{:S(2)}) async-start(), calls=%async_computation.7 | async-start | bytes 1204224 | tf_op jit(solution)/shard_map/psum | solution.py:852
  510.5 201.7 %reduce-scatter.5.cloned.1.call-start = ((), (), s32[]{:S(2)}) async-start(), calls=%async_computation.8 | async-start | bytes 10616832 | tf_op jit(solution)/shard_map/reduce_scatter | solution.py:816
  525.8 1.0 copy-start.10
  712.2 4.8 copy-start.1
Sparse Core Ops, SparseCore 0:
  11.6 69.0 all-gather.12
  82.9 39.5 all-gather.8
  125.2 136.8 all-gather.10
  414.6 95.8 reduce-scatter.2
  512.7 32.5 all-reduce.5
  548.7 163.4 reduce-scatter.4

commit v2 on v1

--- a/solution.py
+++ b/solution.py
@@ -1,3 +1,5 @@
+import functools
+
 import jax
 import jax.numpy as jnp
 from jax import lax
@@ -9,6 +11,7 @@
 CAP = 256
 TB = 256
 PAIR = 2 * HD
+WIDE = 128
 norm_eps = 1e-05
 rope_base = 10000.0
 masked_score = -1e30
@@ -71,11 +74,11 @@
     return values * cos_wide + partner * sin_wide
 
 
-def qkv_kernel(hid_ref, gain_ref, w_ref, cos_ref, sin_ref, q_ref, k_ref, v_ref, n_ref):
+def qkv_rows(hid_ref, gain, w_ref, cos_ref, sin_ref, q_ref, k_ref, v_ref, n_ref):
     width = hid_ref.shape[1]
     hidden = hid_ref[...].astype(f32)
     scale = lax.rsqrt(jnp.mean(hidden * hidden, axis=-1, keepdims=True) + norm_eps)
-    normed = (hidden * scale * gain_ref[...]).astype(bf16)
+    normed = (hidden * scale * gain).astype(bf16)
     n_ref[...] = normed
     cos_wide, sin_wide = cos_ref[...], sin_ref[...]
     for part, (out, factor) in enumerate(((q_ref, HD**-0.5), (k_ref, 1.0))):
@@ -85,18 +88,82 @@
     v_ref[...] = nt(normed, w_ref[2]).astype(bf16)
 
 
-def qkv_call(hidden, gain, weights, cos_wide, sin_wide):
+def qkv_kernel(gain_at, hid_ref, small_ref, w_ref, *refs):
+    gain = small_ref[gain_at : gain_at + 1, :].astype(f32)
+    qkv_rows(hid_ref, gain, w_ref, *refs)
+
+
+def qkv_pieces_kernel(gain_at, part, where_ref, hid_ref, cos_ref, sin_ref, *refs):
+    pieces, (q_ref, k_ref, v_ref, n_ref, w_ref, small_ref, vec_ref) = refs[:-7], refs[-7:]
+    count = len(pieces) // 2
+    half = part // 2
+    vectors = pieces[0].shape[0] - 3 * half
+
+    @pl.when(pl.program_id(0) == 0)
+    def _():
+        vec_ref[...] = jnp.zeros_like(vec_ref)
+        core = where_ref[count]
+        for own in range(2):
+            side = core if own == 0 else 1 - core
+            total = None
+            for r in range(count):
+                ref = pieces[own * count + r]
+                shard = where_ref[r]
+                for at in range(3):
+                    row = pl.multiple_of(shard * part + side * half, 16)
+                    w_ref[at, pl.ds(row, half), :] = ref[at * half : (at + 1) * half, :]
+                moved = pltpu.roll(ref[3 * half :, :].astype(f32), shard * part, 1)
+                total = moved if total is None else total + moved
+            vec_ref[pl.ds(pl.multiple_of(side * vectors, 8), vectors), :] = total
+        small_ref[...] = vec_ref[...].astype(bf16)
+
+    gain = small_ref[gain_at : gain_at + 1, :].astype(f32)
+    qkv_rows(hid_ref, gain, w_ref, cos_ref, sin_ref, q_ref, k_ref, v_ref, n_ref)
+
+
+def qkv_specs(hidden):
     rows, width = hidden.shape
     row = pl.BlockSpec((TB, width), lambda i: (i, 0))
-    tab = pl.BlockSpec((TB, PAIR), lambda i: (i, 0))
-    return call(
-        qkv_kernel,
-        (rows // TB,),
-        [row, whole((1, width)), whole(weights.shape), tab, tab],
-        [((rows, width), bf16, row)] * 4,
-        (hidden, gain, weights, cos_wide, sin_wide),
+    return dict(
+        row=row,
+        tab=pl.BlockSpec((TB, PAIR), lambda i: (i, 0)),
+        outs=[((rows, width), bf16, row)] * 4,
         flops=6 * rows * width * width,
         nbytes=10 * rows * width + 6 * width * width,
+    )
+
+
+def qkv_call(hidden, small, gain_at, weights, cos_wide, sin_wide):
+    s = qkv_specs(hidden)
+    return call(
+        functools.partial(qkv_kernel, gain_at),
+        (hidden.shape[0] // TB,),
+        [s["row"], whole(small.shape), whole(weights.shape), s["tab"], s["tab"]],
+        s["outs"],
+        (hidden, small, weights, cos_wide, sin_wide),
+        flops=s["flops"],
+        nbytes=s["nbytes"],
+    )
+
+
+def qkv_pieces_call(hidden, where, own, other, gain_at, part, cos_wide, sin_wide):
+    s = qkv_specs(hidden)
+    width = hidden.shape[1]
+    pieces = list(own) + list(other)
+    return call(
+        functools.partial(qkv_pieces_kernel, gain_at, part),
+        (hidden.shape[0] // TB,),
+        [pl.BlockSpec(memory_space=pltpu.SMEM), s["row"], s["tab"], s["tab"]]
+        + [whole(piece.shape) for piece in pieces],
+        s["outs"]
+        + [
+            ((3, width, width), bf16, whole((3, width, width))),
+            ((WIDE, width), bf16, whole((WIDE, width))),
+        ],
+        (where, hidden, cos_wide, sin_wide, *pieces),
+        scratch=[pltpu.VMEM((WIDE, width), f32)],
+        flops=s["flops"],
+        nbytes=s["nbytes"],
     )
 
 
@@ -247,7 +314,7 @@
 
 
 def route_kernel(
-    att_ref, hid_ref, grad_ref, wo_ref, gain_ref, sw_ref, prev_ref, gating_ref, rcol_ref, prow_ref,
+    att_ref, hid_ref, grad_ref, wo_ref, sw_ref, prev_ref, gating_ref, rcol_ref, prow_ref,
     res_ref, info_ref, send_ref, nlow_ref, rg_ref,
 ):
     step = pl.program_id(0)
@@ -260,10 +327,11 @@
         residual = hid_ref[...].astype(f32) + nn(att_ref[...], wo_ref[...])
         res_ref[...] = residual
         scale = lax.rsqrt(jnp.mean(residual * residual, axis=-1, keepdims=True) + norm_eps)
-        normed = residual * scale * gain_ref[...]
+        gain = sw_ref[choices + 5 : choices + 6, :].astype(f32)
+        normed = residual * scale * gain
         high, mid, low = split3(normed)
         small_weights = sw_ref[...]
-        small = nn(high, small_weights) + nn(mid, small_weights) + nn(low, small_weights)
+        small = nt(high, small_weights) + nt(mid, small_weights) + nt(low, small_weights)
         logits = small + nn(prev_ref[...], gating_ref[...])
         lane = lanes_of(logits.shape)
         is_choice = lane < choices
@@ -297,10 +365,10 @@
         send_ref[0, CAP:, :] = (nn(hot[0], rg_ref[0]) + nn(hot[1], rg_ref[1])).astype(bf16)
 
 
-def route_call(attended, hidden, grad, w_out, gain, small_weights, prev, gating, rcols, prows, experts):
+def route_call(attended, hidden, grad, w_out, small_weights, prev, gating, rcols, prows, experts):
     rows, width = attended.shape
     blocks = rows // TB
-    wide = small_weights.shape[1]
+    wide = WIDE
 
     def block(cols):
         return pl.BlockSpec((TB, cols), lambda i: (jnp.minimum(i, blocks - 1), 0))
@@ -309,7 +377,7 @@
         route_kernel,
         (blocks + experts,),
         [
-            block(width), block(width), block(width), whole(w_out.shape), whole(gain.shape),
+            block(width), block(width), block(width), whole(w_out.shape),
             whole(small_weights.shape), block(prev.shape[1]), whole(gating.shape), block(2), whole(prows.shape),
         ],
         [
@@ -321,142 +389,254 @@
                 pl.BlockSpec((1, 2 * CAP, width), lambda i: (jnp.maximum(i - blocks, 0), 0, 0)),
             ),
         ],
-        (attended, hidden, grad, w_out, gain, small_weights, prev, gating, rcols, prows),
+        (attended, hidden, grad, w_out, small_weights, prev, gating, rcols, prows),
         scratch=[pltpu.VMEM((rows, width), bf16), pltpu.VMEM((2, rows, width), bf16)],
         flops=2 * rows * width * width + 6 * experts * CAP * rows * width,
         nbytes=10 * rows * width + 2 * width * width + 4 * experts * CAP * width,
     )
 
 
-def expert_kernel(x_ref, w_ref, y_ref, inner_ref, fa_ref, fb_ref, acc_ref):
+def ring_order(count):
+    wide = 1 << ((count.bit_length() - 1) // 2)
+    tall = count // wide
+    if wide < 2 or wide * tall != count or tall % 2:
+        return list(range(count))
+    order = [z * wide for z in range(tall)]
+    for turn_at in range(tall):
+        z = tall - 1 - turn_at
+        across = range(1, wide) if turn_at % 2 == 0 else range(wide - 1, 0, -1)
+        order.extend(z * wide + y for y in across)
+    return order
+
+
+def ring_send(x, order, step):
+    count = len(order)
+    pairs = [(order[i], order[(i + step) % count]) for i in range(count)]
+    return lax.ppermute(x, "fsdp", pairs)
+
+
+def swap(x, experts, bit):
+    return lax.ppermute(x, "expert", [(e, e ^ bit) for e in range(experts)])
+
+
+def cut(x, axis):
+    size = x.shape[axis]
+    half = -(-size // 32) * 16
+    return lax.slice_in_dim(x, 0, half, axis=axis), lax.slice_in_dim(x, half, size, axis=axis)
+
+
+def ring_gather(x, order, axis):
+    count = len(order)
+    half = count // 2
+    pieces = [None] * count
+    pieces[0] = x
+    ahead, back = x, x
+    for k in range(1, half):
+        ahead = ring_send(ahead, order, 1)
+        back = ring_send(back, order, -1)
+        pieces[count - k] = ahead
+        pieces[k] = back
+    first = ring_send(cut(ahead, axis)[0], order, 1)
+    second = ring_send(cut(back, axis)[1], order, -1)
+    pieces[half] = jnp.concatenate([first, second], axis=axis)
+    return pieces
+
+
+def plus(a, b):
+    return (a.astype(f32) + b.astype(f32)).astype(bf16)
+
+
+class RingReduce:
+    def __init__(self, parts, order, axis):
+        self.parts, self.order, self.axis = parts, order, axis
+        self.left = len(order) // 2 - 1
+        self.flight = None
+
+    def start(self):
+        first, second = cut(self.parts[len(self.order) // 2], self.axis)
+        self.flight = (ring_send(first, self.order, 1), ring_send(second, self.order, -1))
+
+    def turn(self):
+        k, axis = self.left, self.axis
+        ahead, back = self.flight
+        mine, other = self.parts[k], self.parts[len(self.order) - k]
+        if k == len(self.order) // 2 - 1:
+            low, high = cut(mine, axis)
+            mine = jnp.concatenate([plus(low, ahead), high], axis=axis)
+            low, high = cut(other, axis)
+            other = jnp.concatenate([low, plus(high, back)], axis=axis)
+        else:
+            mine, other = plus(mine, ahead), plus(other, back)
+        self.flight = (ring_send(mine, self.order, 1), ring_send(other, self.order, -1))
+        self.left = k - 1
+
+    def result(self):
+        return self.parts[0].astype(f32) + self.flight[0].astype(f32) + self.flight[1].astype(f32)
+
+
+def ring_reduce(parts, order, axis):
+    sums = RingReduce(parts, order, axis)
+    sums.start()
+    while sums.left:
+        sums.turn()
+    return sums.result()
+
+
+def fetch_chunk(w_refs, buf, sems, turn_of):
     step = pl.program_id(0)
-    rows = acc_ref.shape[0]
-    rows_in = x_ref[...].reshape(rows, x_ref.shape[2])
-    gate = nt(rows_in, w_ref[0, 0])
-    up = nt(rows_in, w_ref[0, 1])
+    count = len(w_refs)
+
+    def copy(at, slot):
+        return pltpu.make_async_copy(w_refs[turn_of[at]], buf.at[slot], sems.at[slot])
+
+    @pl.when(step == 0)
+    def _():
+        copy(0, 0).start()
+
+    for at in range(count):
+
+        @pl.when(step == at)
+        def _():
+            if at + 1 < count:
+                copy(at + 1, (at + 1) % 2).start()
+            copy(at, at % 2).wait()
+
+    return buf.at[lax.rem(step, 2)]
+
+
+def accumulate(acc_ref, out, final):
+    step = pl.program_id(0)
+
+    @pl.when(step == 0)
+    def _():
+        acc_ref[...] = out
+
+    @pl.when(step > 0)
+    def _():
+        acc_ref[...] += out
+
+    @pl.when(step == pl.num_programs(0) - 1)
+    def _():
+        final[...] = acc_ref[...].astype(bf16).reshape(final.shape)
+
+
+def expert_kernel(x_ref, *refs):
+    w_refs, (y_ref, inner_ref, fa_ref, fb_ref, acc_ref, buf, sems) = refs[:-7], refs[-7:]
+    weights = fetch_chunk(w_refs, buf, sems, list(range(len(w_refs))))
+    rows_in = x_ref[...].reshape(acc_ref.shape[0], x_ref.shape[2])
+    gate = nt(rows_in, weights[0])
+    up = nt(rows_in, weights[1])
     sig = 1.0 / (1.0 + jnp.exp(-gate))
     act = gate * sig
     inner = (act * up).astype(bf16)
     inner_ref[0] = inner
     fa_ref[0] = (up * sig * (1.0 + gate * (1.0 - sig))).astype(bf16)
     fb_ref[0] = act.astype(bf16)
-    out = nn(inner, w_ref[0, 2])
-
-    @pl.when(step == 0)
-    def _():
-        acc_ref[...] = out
-
-    @pl.when(step > 0)
-    def _():
-        acc_ref[...] += out
-
-    @pl.when(step == pl.num_programs(0) - 1)
-    def _():
-        y_ref[...] = acc_ref[...].astype(bf16).reshape(y_ref.shape)
-
-
-def expert_back_kernel(g_ref, w_ref, fa_ref, fb_ref, dx_ref, dgu_ref, acc_ref):
-    step = pl.program_id(0)
-    rows = acc_ref.shape[0]
-    grad_in = g_ref[...].reshape(rows, g_ref.shape[2])
-    grad_inner = nt(grad_in, w_ref[0, 2])
+    accumulate(acc_ref, nn(inner, weights[2]), y_ref)
+
+
+def expert_back_kernel(g_ref, fa_ref, fb_ref, *refs):
+    w_refs, (dx_ref, dgu_ref, acc_ref, buf, sems) = refs[:-5], refs[-5:]
+    weights = fetch_chunk(w_refs, buf, sems, list(range(len(w_refs))))
+    grad_in = g_ref[...].reshape(acc_ref.shape[0], g_ref.shape[2])
+    grad_inner = nt(grad_in, weights[2])
     grad_gate = (grad_inner * fa_ref[0].astype(f32)).astype(bf16)
     grad_up = (grad_inner * fb_ref[0].astype(f32)).astype(bf16)
     dgu_ref[0, 0] = grad_gate
     dgu_ref[0, 1] = grad_up
-    out = nn(grad_gate, w_ref[0, 0]) + nn(grad_up, w_ref[0, 1])
-
-    @pl.when(step == 0)
-    def _():
-        acc_ref[...] = out
-
-    @pl.when(step > 0)
-    def _():
-        acc_ref[...] += out
-
-    @pl.when(step == pl.num_programs(0) - 1)
-    def _():
-        dx_ref[...] = acc_ref[...].astype(bf16).reshape(dx_ref.shape)
-
-
-def expert_weights_kernel(x_ref, g_ref, inner_ref, dgu_ref, dw_ref):
+    accumulate(acc_ref, nn(grad_gate, weights[0]) + nn(grad_up, weights[1]), dx_ref)
+
+
+def expert_weights_kernel(x_ref, g_ref, inner_ref, dgu_ref, *dw_refs):
+    step = pl.program_id(0)
     rows = inner_ref.shape[1]
     rows_in = x_ref[...].reshape(rows, x_ref.shape[2])
     grad_in = g_ref[...].reshape(rows, g_ref.shape[2])
-    dw_ref[0, 0] = tn(dgu_ref[0, 0], rows_in).astype(bf16)
-    dw_ref[0, 1] = tn(dgu_ref[0, 1], rows_in).astype(bf16)
-    dw_ref[0, 2] = tn(inner_ref[0], grad_in).astype(bf16)
-
-
-def expert_specs(sent, weights):
+    terms = (tn(dgu_ref[0, 0], rows_in), tn(dgu_ref[0, 1], rows_in), tn(inner_ref[0], grad_in))
+    for at, ref in enumerate(dw_refs):
+
+        @pl.when(step == at)
+        def _():
+            for part, term in enumerate(terms):
+                ref[part] = term.astype(bf16)
+
+
+def expert_specs(sent, chunks, weight):
     experts, _, width = sent.shape
-    chunks, _, units, _ = weights.shape
+    _, units, _ = weight.shape
     rows = experts * CAP
     return dict(
         rows=rows,
+        chunks=chunks,
+        units=units,
+        width=width,
         x=pl.BlockSpec((experts, CAP, width), lambda c: (0, 0, 0)),
         g=pl.BlockSpec((experts, CAP, width), lambda c: (0, 1, 0)),
-        w=pl.BlockSpec((1, 3, units, width), lambda c: (c, 0, 0, 0)),
         unit=pl.BlockSpec((1, rows, units), lambda c: (c, 0, 0)),
         pair=pl.BlockSpec((1, 2, rows, units), lambda c: (c, 0, 0, 0)),
         flops=6 * rows * width * chunks * units,
         nbytes=6 * chunks * units * (rows + width) + 4 * rows * width,
+        scratch=[
+            pltpu.VMEM((rows, width), f32),
+            pltpu.VMEM((2,) + weight.shape, bf16),
+            pltpu.SemaphoreType.DMA((2,)),
+        ],
     )
 
 
 def expert_call(sent, weights):
-    s = expert_specs(sent, weights)
-    chunks, _, units, width = weights.shape
-    rows = s["rows"]
-    hidden = ((chunks, rows, units), bf16, s["unit"])
+    chunks = len(weights)
+    s = expert_specs(sent, chunks, weights[0])
+    hidden = ((chunks, s["rows"], s["units"]), bf16, s["unit"])
     return call(
         expert_kernel,
         (chunks,),
-        [s["x"], s["w"]],
-        [((sent.shape[0], CAP, width), bf16, s["x"]), hidden, hidden, hidden],
-        (sent, weights),
-        scratch=[pltpu.VMEM((rows, width), f32)],
+        [s["x"]] + [pl.BlockSpec(memory_space=pl.ANY)] * chunks,
+        [((sent.shape[0], CAP, s["width"]), bf16, s["x"]), hidden, hidden, hidden],
+        (sent, *weights),
+        scratch=s["scratch"],
         flops=s["flops"],
         nbytes=s["nbytes"],
-        exps=rows * chunks * units,
+        exps=s["rows"] * chunks * s["units"],
     )
 
 
 def expert_back_call(sent, weights, factor_a, factor_b):
-    s = expert_specs(sent, weights)
-    chunks, _, units, width = weights.shape
-    rows = s["rows"]
+    chunks = len(weights)
+    s = expert_specs(sent, chunks, weights[0])
     return call(
         expert_back_kernel,
         (chunks,),
-        [s["g"], s["w"], s["unit"], s["unit"]],
+        [s["g"], s["unit"], s["unit"]] + [pl.BlockSpec(memory_space=pl.ANY)] * chunks,
         [
-            ((sent.shape[0], CAP, width), bf16, s["x"]),
-            ((chunks, 2, rows, units), bf16, s["pair"]),
+            ((sent.shape[0], CAP, s["width"]), bf16, s["x"]),
+            ((chunks, 2, s["rows"], s["units"]), bf16, s["pair"]),
         ],
-        (sent, weights, factor_a, factor_b),
-        scratch=[pltpu.VMEM((rows, width), f32)],
+        (sent, factor_a, factor_b, *weights),
+        scratch=s["scratch"],
         flops=s["flops"],
         nbytes=s["nbytes"],
     )
 
 
-def expert_weights_call(sent, inner, dgu, weights_shape):
-    chunks, _, units, width = weights_shape
-    s = expert_specs(sent, jax.ShapeDtypeStruct(weights_shape, bf16))
+def expert_weights_call(sent, inner, dgu, weight, chosen):
+    s = expert_specs(sent, len(chosen), weight)
+    start = chosen[0]
+    unit = pl.BlockSpec((1, s["rows"], s["units"]), lambda c: (start + c, 0, 0))
+    pair = pl.BlockSpec((1, 2, s["rows"], s["units"]), lambda c: (start + c, 0, 0, 0))
     return call(
         expert_weights_kernel,
-        (chunks,),
-        [s["x"], s["g"], s["unit"], s["pair"]],
-        [(weights_shape, bf16, s["w"])],
+        (len(chosen),),
+        [s["x"], s["g"], unit, pair],
+        [(weight.shape, bf16, whole(weight.shape))] * len(chosen),
         (sent, sent, inner, dgu),
         flops=s["flops"],
         nbytes=s["nbytes"],
-    )[0]
+    )
 
 
 def combine_kernel(
-    y_ref, res_ref, info_ref, rcol_ref, pcol_ref, grad_ref, gain_ref, vec_ref, sw_ref, prev_ref, gt_ref,
+    y_ref, res_ref, info_ref, rcol_ref, pcol_ref, grad_ref, sw_ref, prev_ref, gt_ref,
     out_ref, part_ref, gprev_ref, gsw_ref, gvec_ref, ggat_ref,
 ):
     step = pl.program_id(0)
@@ -472,9 +652,11 @@
         return info[:, at : at + 1]
 
     gates = (column(choices + 4), column(choices + 5))
-    normed = residual * column(choices + 6) * gain_ref[...]
+    small_weights = sw_ref[...]
+    gain = small_weights[choices + 5 : choices + 6].astype(f32)
+    normed = residual * column(choices + 6) * gain
     grad = grad_ref[...].astype(f32)
-    vectors = (vec_ref[0:1, :], vec_ref[1:2, :])
+    vectors = [small_weights[choices + 6 + c : choices + 7 + c].astype(f32) for c in range(2)]
     alphas = ((column(choices), column(choices + 1)), (column(choices + 2), column(choices + 3)))
     dot_normed = jnp.sum(grad * normed, axis=-1, keepdims=True)
     dot_vectors = [jnp.sum(grad * v, axis=-1, keepdims=True) for v in vectors]
@@ -518,9 +700,8 @@
         direct = direct + alphas[c][0] * weight_const[c]
         coefs = jnp.where(lane == c, alphas[c][1] * weight_const[c], coefs)
     high, mid, low = split3(grad_small)
-    small_weights = sw_ref[...]
     part_ref[...] = direct * grad + (
-        nt(high, small_weights) + nt(mid, small_weights) + nt(low, small_weights)
+        nn(high, small_weights) + nn(mid, small_weights) + nn(low, small_weights)
     )
     gating_t = gt_ref[...]
     logits_high, logits_mid, logits_low = split3(jnp.where(is_choice, grad_small, 0.0))
@@ -546,7 +727,7 @@
         ggat_ref[...] += grad_gating
 
 
-def combine_call(back, residual, info, rcols, pcols, grad, gain, vectors, small_weights, prev, gating_t):
+def combine_call(back, residual, info, rcols, pcols, grad, small_weights, prev, gating_t):
     rows, width = residual.shape
     wide = info.shape[1]
     choices = prev.shape[1]
@@ -559,8 +740,8 @@
         combine_kernel,
         (rows // TB,),
         [
-            whole(back.shape), block(width), block(wide), block(2), block(2), block(width), whole(gain.shape),
-            whole(vectors.shape), whole(small_weights.shape), block(choices), whole(gating_t.shape),
+            whole(back.shape), block(width), block(wide), block(2), block(2), block(width),
+            whole(small_weights.shape), block(choices), whole(gating_t.shape),
         ],
         [
             ((rows, width), bf16, block(width)),
@@ -570,21 +751,19 @@
             ((wide, width), f32, whole((wide, width))),
             ((choices, wide), f32, whole((choices, wide))),
         ],
-        (back, residual, info, rcols, pcols, grad, gain, vectors, small_weights, prev, gating_t),
+        (back, residual, info, rcols, pcols, grad, small_weights, prev, gating_t),
         flops=4 * slots * rows * width,
         nbytes=14 * rows * width + 2 * slots * width,
     )
 
 
 def residual_kernel(
-    dx_ref, part_ref, res_ref, info_ref, pcol_ref, grad_ref, gain_ref, wo_ref, att_ref,
+    gain_at, dx_ref, part_ref, res_ref, pcol_ref, grad_ref, sw_ref, wo_ref, att_ref,
     gres_ref, gatt_ref, gwo_ref, ggain_ref, acc_ref,
 ):
     step = pl.program_id(0)
     experts = dx_ref.shape[0]
     slots = experts * CAP
-    scale_at = info_ref.shape[1]
-    del scale_at
     slot = lanes_of((TB, slots))
     hot = jnp.where(
         (pcol_ref[:, 0:1] == slot) | (pcol_ref[:, 1:2] == slot), 1.0, 0.0
@@ -594,7 +773,7 @@
     scale = lax.rsqrt(jnp.mean(residual * residual, axis=-1, keepdims=True) + norm_eps)
     unit = residual * scale
     grad_gain = jnp.sum(grad_normed * unit, axis=0, keepdims=True)
-    scaled = grad_normed * gain_ref[...]
+    scaled = grad_normed * sw_ref[gain_at : gain_at + 1, :].astype(f32)
     grad_residual = grad_ref[...].astype(f32) + scale * (
         scaled - unit * jnp.mean(scaled * unit, axis=-1, keepdims=True)
     )
@@ -618,19 +797,18 @@
         gwo_ref[...] = acc_ref[...].astype(bf16)
 
 
-def residual_call(dx, part, residual, info, pcols, grad, gain, w_out, attended):
+def residual_call(dx, part, residual, pcols, grad, small_weights, gain_at, w_out, attended):
     rows, width = residual.shape
-    wide = info.shape[1]
     slots = dx.shape[0] * CAP
 
     def block(cols):
         return pl.BlockSpec((TB, cols), lambda i: (i, 0))
 
     return call(
-        residual_kernel,
+        functools.partial(residual_kernel, gain_at),
         (rows // TB,),
         [
-            whole(dx.shape), block(width), block(width), block(wide), block(2), block(width), whole(gain.shape),
+            whole(dx.shape), block(width), block(width), block(2), block(width), whole(small_weights.shape),
             whole(w_out.shape), block(width),
         ],
         [
@@ -639,66 +817,189 @@
             ((width, width), bf16, whole((width, width))),
             ((1, width), f32, whole((1, width))),
         ],
-        (dx, part, residual, info, pcols, grad, gain, w_out, attended),
+        (dx, part, residual, pcols, grad, small_weights, w_out, attended),
         scratch=[pltpu.VMEM((width, width), f32)],
         flops=2 * slots * rows * width + 4 * rows * width * width,
         nbytes=18 * rows * width + 2 * slots * width,
     )
 
 
-def qkv_weights_kernel(dq_ref, dk_ref, dv_ref, n_ref, out_ref):
+def qkv_weights_kernel(
+    gain_at, where_ref, dq_ref, dk_ref, dv_ref, n_ref, w_ref, small_ref, gwo_ref, ggain_ref, gsw_ref, gvec_ref,
+    ggat_ref, own_ref, other_ref, acc_ref,
+):
+    step = pl.program_id(0)
+    count, _, width = own_ref.shape
+    part = width // count
+    half = part // 2
+    shards = dq_ref.shape[1] // part
+    normed = n_ref[...]
+    core = where_ref[count]
+    gain_grad = jnp.zeros((1, width), f32)
+
+    def put(side, shard, at, value):
+        rel = where_ref[count + 1 + shard]
+
+        @pl.when(core == side)
+        def _():
+            own_ref[rel, at : at + value.shape[0], :] = value
+
+        @pl.when(core != side)
+        def _():
+            other_ref[rel, at : at + value.shape[0], :] = value
+
+    for at, ref in enumerate((dq_ref, dk_ref, dv_ref, None)):
+        if ref is None:
+            term = gwo_ref[...]
+        else:
+            full = tn(ref[...], normed)
+            gain_grad = gain_grad + jnp.sum(full * w_ref[at].astype(f32), axis=0, keepdims=True)
+            term = full.astype(bf16)
+        for m in range(shards):
+            for side in range(2):
+                row = m * part + side * half
+                put(side, step * shards + m, at * half, term[row : row + half])
+
+    @pl.when(step == 0)
+    def _():
+        acc_ref[...] = gain_grad
+
+    @pl.when(step > 0)
+    def _():
+        acc_ref[...] += gain_grad
+
+    @pl.when(step == pl.num_programs(0) - 1)
+    def _():
+        gain_one = acc_ref[...] / small_ref[gain_at : gain_at + 1, :].astype(f32)
+        vectors = jnp.concatenate(
+            [gsw_ref[:gain_at, :], gain_one, ggain_ref[...], gvec_ref[:2, :]], axis=0
+        )
+        gating_high = ggat_ref[...].astype(bf16).astype(f32)
+        gating = (gating_high, ggat_ref[...] - gating_high)
+        lanes = lanes_of((1, width)) < part
+        split = vectors.shape[0] // 2
+        spare = jnp.zeros((16 - split - 1, width), f32)
+        for m in range(count):
+            here = vectors if m == 0 else pltpu.roll(vectors, width - m * part, 1)
+            here = jnp.where(lanes, here, 0.0)
+            for side in range(2):
+                block = jnp.concatenate(
+                    [here[side * split : (side + 1) * split], gating[side], spare], axis=0
+                )
+                put(side, m, 4 * half, block.astype(bf16))
+
+
+def qkv_weights_call(where, dq, dk, dv, normed, weights, small, gain_at, gwo, ggain, gsw, gvec, ggat, count):
+    rows, width = normed.shape
+    steps = 2
+    cols = width // steps
+    col = pl.BlockSpec((rows, cols), lambda c: (0, c))
+    part = width // count
+    shape = (count, 2 * part + 16, width)
+    return call(
+        functools.partial(qkv_weights_kernel, gain_at),
+        (steps,),
+        [
+            pl.BlockSpec(memory_space=pltpu.SMEM), col, col, col, whole(normed.shape),
+            pl.BlockSpec((3, cols, width), lambda c: (0, c, 0)), whole(small.shape),
+            pl.BlockSpec((cols, width), lambda c: (c, 0)), whole(ggain.shape), whole(gsw.shape), whole(gvec.shape),
+            whole(ggat.shape),
+        ],
+        [(shape, bf16, whole(shape))] * 2,
+        (where, dq, dk, dv, normed, weights, small, gwo, ggain, gsw, gvec, ggat),
+        scratch=[pltpu.VMEM((1, width), f32)],
+        flops=6 * rows * width * width,
+        nbytes=8 * rows * width + 18 * width * width,
+    )
+
+
+def finish_kernel(choices, where_ref, mine_ref, theirs_ref, gq_ref, gk_ref, gv_ref, gwo_ref, small_ref, gat_ref):
+    part = gwo_ref.shape[0]
+    half = part // 2
+    core = where_ref[where_ref.shape[0] // 2]
+    width = gwo_ref.shape[1]
+
+    def side(which, at, size):
+        first = mine_ref[at : at + size, :].astype(f32)
+        second = theirs_ref[at : at + size, :].astype(f32)
+        return jnp.where(core == which, first, second)
+
+    for at, ref in enumerate((gq_ref, gk_ref, gv_ref, gwo_ref)):
+        both = jnp.concatenate([side(0, at * half, half), side(1, at * half, half)], axis=0)
+        if at == 3:
+            ref[...] = both
+        else:
+            ref[...] = both.T[:, :part]
+    split = (choices + 8) // 2
+    low, high = side(0, 4 * half, 16), side(1, 4 * half, 16)
+    small_ref[...] = jnp.concatenate([low[:split, :WIDE], high[:split, :WIDE]], axis=0)
+    gat_ref[...] = (low + high)[split : split + 1, :]
+
+
+def finish_call(where, mine, theirs, part, choices):
+    width = mine.shape[1]
+    thin = (width, part)
+    return call(
+        functools.partial(finish_kernel, choices),
+        (1,),
+        [pl.BlockSpec(memory_space=pltpu.SMEM), whole(mine.shape), whole(mine.shape)],
+        [
+            (thin, f32, whole(thin)),
+            (thin, f32, whole(thin)),
+            (thin, f32, whole(thin)),
+            ((part, width), f32, whole((part, width))),
+            ((choices + 8, WIDE), f32, whole((choices + 8, WIDE))),
+            ((1, width), f32, whole((1, width))),
+        ],
+        (where, mine, theirs),
+        flops=10,
+        nbytes=20 * part * width,
+    )
+
+
+def plain_weights_kernel(dq_ref, dk_ref, dv_ref, n_ref, out_ref):
     normed = n_ref[...]
     for part, ref in enumerate((dq_ref, dk_ref, dv_ref)):
-        out_ref[part] = tn(ref[...], normed).astype(bf16)
-
-
-def qkv_weights_call(dq, dk, dv, normed):
+        out_ref[part] = tn(ref[...], normed)
+
+
+def plain_weights_call(dq, dk, dv, normed):
     rows, width = normed.shape
     col = pl.BlockSpec((rows, 256), lambda c: (0, c))
     return call(
-        qkv_weights_kernel,
+        plain_weights_kernel,
         (width // 256,),
         [col, col, col, whole((rows, width))],
-        [((3, width, width), bf16, pl.BlockSpec((3, 256, width), lambda c: (0, c, 0)))],
+        [((3, width, width), f32, pl.BlockSpec((3, 256, width), lambda c: (0, c, 0)))],
         (dq, dk, dv, normed),
         flops=6 * rows * width * width,
-        nbytes=8 * rows * width + 6 * width * width,
+        nbytes=8 * rows * width + 12 * width * width,
     )[0]
 
 
-def hidden_kernel(dq_ref, dk_ref, dv_ref, w_ref, hid_ref, gain_ref, gres_ref, out_ref, ggain_ref):
-    step = pl.program_id(0)
+def hidden_kernel(gain_at, dq_ref, dk_ref, dv_ref, w_ref, hid_ref, small_ref, gres_ref, out_ref):
     grad_normed = nn(dq_ref[...], w_ref[0]) + nn(dk_ref[...], w_ref[1]) + nn(dv_ref[...], w_ref[2])
     hidden = hid_ref[...].astype(f32)
     scale = lax.rsqrt(jnp.mean(hidden * hidden, axis=-1, keepdims=True) + norm_eps)
     unit = hidden * scale
-    grad_gain = jnp.sum(grad_normed * unit, axis=0, keepdims=True)
-    scaled = grad_normed * gain_ref[...]
+    scaled = grad_normed * small_ref[gain_at : gain_at + 1, :].astype(f32)
     out_ref[...] = gres_ref[...] + scale * (
         scaled - unit * jnp.mean(scaled * unit, axis=-1, keepdims=True)
     )
 
-    @pl.when(step == 0)
-    def _():
-        ggain_ref[...] = grad_gain
-
-    @pl.when(step > 0)
-    def _():
-        ggain_ref[...] += grad_gain
-
-
-def hidden_call(dq, dk, dv, weights, hidden, gain, grad_residual):
+
+def hidden_call(dq, dk, dv, weights, hidden, small, gain_at, grad_residual):
     rows, width = hidden.shape
     row = pl.BlockSpec((TB, width), lambda i: (i, 0))
     return call(
-        hidden_kernel,
+        functools.partial(hidden_kernel, gain_at),
         (rows // TB,),
-        [row, row, row, whole(weights.shape), row, whole(gain.shape), row],
-        [((rows, width), f32, row), ((1, width), f32, whole((1, width)))],
-        (dq, dk, dv, weights, hidden, gain, grad_residual),
+        [row, row, row, whole(weights.shape), row, whole(small.shape), row],
+        [((rows, width), f32, row)],
+        (dq, dk, dv, weights, hidden, small, grad_residual),
         flops=6 * rows * width * width,
         nbytes=16 * rows * width + 6 * width * width,
-    )
+    )[0]
 
 
 def rope_wide(length):
@@ -774,101 +1075,181 @@
     place_cols = place_rows.T
     cos_wide, sin_wide = rope_wide(rows)
 
+    gain_at = choices + 4
     small_parts = jnp.concatenate(
-        [gain_attn[:, None], gain_moe[:, None], w_router, w_const, v_const.T], axis=1
-    )
-    small_count = small_parts.shape[1]
-    small_rows = to_rows(small_parts.T.reshape(1, -1), width)[0]
-    first_pack = jnp.concatenate([w_query.T, w_key.T, w_value.T, small_rows], axis=0)
-    first = lax.all_gather(first_pack, "fsdp", axis=0, tiled=False)
+        [w_router.T, w_const.T, gain_attn[None], gain_moe[None], v_const], axis=0
+    )
+    small_count = choices + 8
+    order = ring_order(shards)
+    place = jnp.asarray([order.index(m) for m in range(shards)], dtype=i32)
+    spot = place[fsdp_here]
+    core = lax.rem(lax.axis_index("expert"), 2)
+    paired = part % 32 == 0 and small_count == 16 and shards % 2 == 0 and experts & (experts - 1) == 0
+    ring = jnp.asarray(order, dtype=i32)
+    where = jnp.concatenate(
+        [ring[(spot + jnp.arange(shards, dtype=i32)) % shards], core[None], (place - spot) % shards]
+    )
+    expert_pack = jnp.stack([w_gate[0].T, w_up[0].T, w_down[0]])
     w_out = lax.all_gather(w_output, "fsdp", axis=0, tiled=True)
-    expert_pack = jnp.stack([w_gate[0].T, w_up[0].T, w_down[0]])
-    expert_weights = lax.all_gather(expert_pack, "fsdp", axis=0, tiled=False)
-
-    qkv_weights = (
-        first[:, : 3 * part].reshape(shards, 3, part, width).transpose(1, 0, 2, 3).reshape(3, width, width)
-    )
-    small = (
-        first[:, 3 * part :]
-        .reshape(shards, -1)[:, : small_count * part]
-        .reshape(shards, small_count, part)
-        .transpose(1, 0, 2)
-        .reshape(small_count, width)
-    )
-    gain_one = small[0:1].astype(f32)
-    gain_two = small[1:2].astype(f32)
-    small_weights = jnp.pad(small[2 : choices + 6].T, ((0, 0), (0, 128 - choices - 4)))
-    vectors = small[choices + 6 :].astype(f32)
-    gating_wide = jnp.pad(w_gating, ((0, 0), (0, 128 - choices)))
-    gating_t = jnp.pad(w_gating.T, ((0, 128 - choices), (0, 128 - choices)))
-
-    query, key, value, normed_one = qkv_call(hidden, gain_one, qkv_weights, cos_wide, sin_wide)
+    if paired:
+        half = part // 2
+        small_wide = jnp.pad(small_parts, ((0, 0), (0, width - part)))
+        thin = (w_query.T, w_key.T, w_value.T)
+        pack = jnp.concatenate(
+            [
+                x
+                for side in range(2)
+                for x in [w[side * half : (side + 1) * half] for w in thin]
+                + [small_wide[side * 8 : (side + 1) * 8]]
+            ],
+            axis=0,
+        )
+        tall = 3 * half + 8
+        own = ring_gather(lax.dynamic_slice_in_dim(pack, core * tall, tall), order, 0)
+        other = [lax.dynamic_slice_in_dim(pack, (1 - core) * tall, tall)]
+        other += [swap(piece, experts, 1) for piece in own[1:]]
+        expert_pack, _ = lax.optimization_barrier((expert_pack, own[shards // 2]))
+        query, key, value, normed_one, qkv_weights, small = qkv_pieces_call(
+            hidden, where, own, other, gain_at, part, cos_wide, sin_wide
+        )
+    else:
+        first_pack = jnp.concatenate(
+            [w_query.T, w_key.T, w_value.T, to_rows(small_parts.reshape(1, -1), width)[0]], axis=0
+        )
+        first = lax.all_gather(first_pack, "fsdp", axis=0, tiled=False)
+        qkv_weights = (
+            first[:, : 3 * part]
+            .reshape(shards, 3, part, width)
+            .transpose(1, 0, 2, 3)
+            .reshape(3, width, width)
+        )
+        small = (
+            first[:, 3 * part :]
+            .reshape(shards, -1)[:, : small_count * part]
+            .reshape(shards, small_count, part)
+            .transpose(1, 0, 2)
+            .reshape(small_count, width)
+        )
+        small = jnp.pad(small, ((0, WIDE - small_count), (0, 0)))
+        query, key, value, normed_one = qkv_call(
+            hidden, small, gain_at, qkv_weights, cos_wide, sin_wide
+        )
+    expert_weights = ring_gather(expert_pack, order, 1)
+    farthest = shards // 2
+    turns = [farthest] + [r for k in range(farthest - 1, 0, -1) for r in (k, shards - k)] + [0]
+    expert_weights = [expert_weights[r] for r in turns]
+
+    gating_wide = jnp.pad(w_gating, ((0, 0), (0, WIDE - choices)))
+    gating_t = jnp.pad(w_gating.T, ((0, WIDE - choices), (0, WIDE - choices)))
+
     attended, recip, expo = attend_call(live, query, key, value)
     residual, info, send = route_call(
-        attended, hidden, grad, w_out, gain_two, small_weights, prev, gating_wide, route_cols, place_rows, experts
+        attended, hidden, grad, w_out, small, prev, gating_wide, route_cols, place_rows, experts
     )
     sent = lax.all_to_all(send, "expert", split_axis=0, concat_axis=0, tiled=True)
     expert_out, inner, factor_a, factor_b = expert_call(sent, expert_weights)
     returned = lax.all_to_all(expert_out, "expert", split_axis=0, concat_axis=0, tiled=True)
     expert_dx, dgu = expert_back_call(sent, expert_weights, factor_a, factor_b)
     returned_dx = lax.all_to_all(expert_dx, "expert", split_axis=0, concat_axis=0, tiled=True)
-    expert_dw = expert_weights_call(sent, inner, dgu, expert_weights.shape)
-    expert_sum = lax.psum_scatter(expert_dw, "fsdp", scatter_dimension=0, tiled=False)
+    lead = min(3, shards)
+    groups = [list(range(lead)), list(range(lead, shards))]
+    expert_dw = [None] * shards
+    for chosen in groups:
+        terms = expert_weights_call(sent, inner, dgu, expert_pack, chosen)
+        for at, term in zip(chosen, terms):
+            expert_dw[turns[at]] = term
+    sums = RingReduce(expert_dw, order, 1)
+    sums.start()
+    returned, _ = lax.optimization_barrier((returned, (expert_dw, sums.flight)))
+    sums.turn()
 
     hidden_out, part_grad, grad_prev, grad_sw, grad_vec, grad_gating = combine_call(
-        returned, residual, info, route_cols, place_cols, grad, gain_two, vectors, small_weights, prev, gating_t
+        returned, residual, info, route_cols, place_cols, grad, small, prev, gating_t
     )
     grad_residual, grad_attended, grad_wo, grad_gain_two = residual_call(
-        returned_dx, part_grad, residual, info, place_cols, grad, gain_two, w_out, attended
-    )
+        returned_dx, part_grad, residual, place_cols, grad, small, gain_at + 1, w_out, attended
+    )
+    if sums.left:
+        grad_attended, _ = lax.optimization_barrier((grad_attended, sums.flight))
+        sums.turn()
     dq, dk, dv = attend_back_call(
         query, key, value, expo, grad_attended, attended, recip, cos_wide, sin_wide
     )
-    grad_qkv = qkv_weights_call(dq, dk, dv, normed_one)
-    grad_hidden, grad_gain_one = hidden_call(
-        dq, dk, dv, qkv_weights, hidden, gain_one, grad_residual
-    )
-
-    small_grads = jnp.concatenate(
-        [grad_gain_one, grad_gain_two, grad_sw[: choices + 4], grad_vec[:2]], axis=0
-    )
-    small_flat = small_grads.reshape(small_count, shards, part).transpose(1, 0, 2).reshape(shards, -1)
-    gating_flat = grad_gating[:, :choices].reshape(1, -1)
-    gating_high = gating_flat.astype(bf16)
-    gating_low = (gating_flat - gating_high.astype(f32)).astype(bf16)
-    gating_both = jnp.concatenate([gating_high, gating_low], axis=1)
-    flat = jnp.concatenate(
-        [small_flat.astype(bf16), jnp.broadcast_to(gating_both, (shards, gating_both.shape[1]))], axis=1
-    )
-    shared = jnp.concatenate(
-        [
-            grad_qkv.reshape(3, shards, part, width).transpose(1, 0, 2, 3).reshape(shards, 3 * part, width),
-            grad_wo.reshape(shards, part, width),
-            to_rows(flat, width),
-        ],
-        axis=1,
-    )
-    scattered = lax.psum_scatter(shared, "fsdp", scatter_dimension=0, tiled=False)
-    total = lax.psum(scattered, "expert").astype(f32)
-    flat_total = total[4 * part :].reshape(-1)
-    small_total = flat_total[: small_count * part].reshape(small_count, part)
-    gating_at = small_count * part
-    pair_total = flat_total[gating_at : gating_at + 2 * choices * choices].reshape(2, choices, choices)
-    expert_total = expert_sum.astype(f32)
+    if sums.left:
+        dq, _ = lax.optimization_barrier((dq, sums.flight))
+        sums.turn()
+    grad_hidden = hidden_call(dq, dk, dv, qkv_weights, hidden, small, gain_at, grad_residual)
+    if paired:
+        own, other = qkv_weights_call(
+            where, dq, dk, dv, normed_one, qkv_weights, small, gain_at, grad_wo, grad_gain_two, grad_sw, grad_vec,
+            jnp.pad(grad_gating[:, :choices].reshape(1, -1), ((0, 0), (0, width - choices * choices))), shards,
+        )
+        got = swap(other, experts, 1)
+        mine = ring_reduce([plus(own[r], got[r]) for r in range(shards)], order, 0).astype(bf16)
+        bit = 2
+        while bit < experts:
+            mine = plus(mine, swap(mine, experts, bit))
+            bit *= 2
+        theirs = swap(mine, experts, 1)
+        total_q, total_k, total_v, total_o, small_total, gating_row = finish_call(
+            where, mine, theirs, part, choices
+        )
+        small_total = small_total[:, :part]
+        gating_total = gating_row[0, : choices * choices].reshape(choices, choices)
+    else:
+        grad_qkv = plain_weights_call(dq, dk, dv, normed_one)
+        grad_gain_one = jnp.sum(grad_qkv * qkv_weights.astype(f32), axis=(0, 1))[None] / small[
+            gain_at : gain_at + 1
+        ].astype(f32)
+        small_grads = jnp.concatenate(
+            [grad_sw[:gain_at], grad_gain_one, grad_gain_two, grad_vec[:2]], axis=0
+        )
+        small_flat = (
+            small_grads.reshape(small_count, shards, part).transpose(1, 0, 2).reshape(shards, -1)
+        )
+        gating_flat = grad_gating[:, :choices].reshape(1, -1)
+        gating_both = jnp.concatenate(split2(gating_flat), axis=1)
+        flat = jnp.concatenate(
+            [small_flat.astype(bf16), jnp.broadcast_to(gating_both, (shards, gating_both.shape[1]))], axis=1
+        )
+        shared = jnp.concatenate(
+            [
+                grad_qkv.astype(bf16)
+                .reshape(3, shards, part, width)
+                .transpose(1, 0, 2, 3)
+                .reshape(shards, 3 * part, width),
+                grad_wo.reshape(shards, part, width),
+                to_rows(flat, width),
+            ],
+            axis=1,
+        )
+        scattered = lax.psum_scatter(shared, "fsdp", scatter_dimension=0, tiled=False)
+        total = lax.psum(scattered, "expert").astype(f32)
+        total_q, total_k, total_v = [total[at * part : (at + 1) * part].T for at in range(3)]
+        total_o = total[3 * part : 4 * part]
+        flat_total = total[4 * part :].reshape(-1)
+        small_total = flat_total[: small_count * part].reshape(small_count, part)
+        gating_at = small_count * part
+        gating_total = jnp.sum(
+            flat_total[gating_at : gating_at + 2 * choices * choices].reshape(2, choices, choices), axis=0
+        )
+    while sums.left:
+        sums.turn()
+    expert_total = sums.result()
     return (
         hidden_out[None],
         grad_hidden[None],
         grad_prev[None],
-        total[:part].T,
-        total[part : 2 * part].T,
-        total[2 * part : 3 * part].T,
-        total[3 * part : 4 * part],
-        small_total[0],
-        small_total[1],
-        small_total[2 : choices + 2].T,
-        pair_total[0] + pair_total[1],
-        small_total[choices + 2 : choices + 6].T,
-        small_total[choices + 6 :],
+        total_q,
+        total_k,
+        total_v,
+        total_o,
+        small_total[gain_at],
+        small_total[gain_at + 1],
+        small_total[:choices].T,
+        gating_total,
+        small_total[choices:gain_at].T,
+        small_total[gain_at + 2 :],
         expert_total[0].T[None],
         expert_total[1].T[None],
         expert_total[2][None],

time: 726 us -> 469 us (0.65)
  waiting for transfers between devices: 404 us -> 127 us
  starting transfers between devices: 8.93 us -> 52 us
  blocking collectives: 46.8 us -> 5.18 us
  other arithmetic: 14.9 us -> 32.6 us
  local copies, waits for them, and re-layouts: 58.4 us -> 41.3 us
  Pallas kernels: 176 us -> 188 us
    reduce_scatter x2 -> x0, waiting for transfers between devices: 255 us -> none  [the longest x1 159 us: per_device(): lax.psum_scatter(expert_dw, 'fsdp', scatter_dimension=0, tiled=False)]
    all_gather x2 -> x0, waiting for transfers between devices: 131 us -> none  [the longest x1 77.5 us: per_device(): expert_weights = lax.all_gather(expert_pack, 'fsdp', axis=0, tiled=False)]
    ppermute x0 -> x42, waiting for transfers between devices: none -> 122 us  [the longest x32 117 us: ring_send(): return lax.ppermute(x, 'fsdp', pairs)]
    all_to_all x1 -> x0, blocking collectives: 40.6 us -> none  [per_device(): lax.all_to_all(send, 'expert', split_axis=0, concat_axis=0, tiled=True)]
    ppermute x0 -> x42, starting transfers between devices: none -> 39.4 us  [the longest x32 36.8 us: ring_send(): return lax.ppermute(x, 'fsdp', pairs)]
    psum x1 -> x0, waiting for transfers between devices: 17.6 us -> none  [per_device(): total = lax.psum(scattered, 'expert').astype(f32)]
    convert_element_type x5 -> x14, other arithmetic: 2.63 us -> 18.5 us  [the longest x13 17 us: plus(): return (a.astype(f32) + b.astype(f32)).astype(bf16)]
    pallas_call x11 -> x13, Pallas kernels: 176 us -> 188 us  [call(): pl.pallas_call(kernel, grid=grid, in_specs=ins, out_specs=[o[2] for o in...]
  transfers between devices with their start and end apart: 8 -> 46, of which waited for: 5 -> 20; matrix products, arithmetic and copies ran while one was open for 3% -> 9% of each run, Pallas kernels for 15% -> 27%
where the time goes in v2:
time: 469 us; the launch traced here: 462 us
  Pallas kernels  188 us (40%)
  waiting for transfers between devices  127 us (27%)
  starting transfers between devices  52 us (11%)
  local copies, waits for them, and re-layouts  41.3 us (9%)
  other arithmetic  32.6 us (7%)
  between operations  15.3 us (3%)
  blocking collectives  5.18 us (1%)
    pallas_call x13, Pallas kernels, call(): pl.pallas_call(kernel, grid=grid, in_specs=ins, out_specs=[o[2] for o in...  188 us
    ppermute x32, waiting for transfers between devices, ring_send(): return lax.ppermute(x, 'fsdp', pairs)  117 us
    ppermute x32, starting transfers between devices, ring_send(): return lax.ppermute(x, 'fsdp', pairs)  36.8 us
    unnamed x115, local copies, waits for them, and re-layouts  30.2 us
    convert_element_type x13, other arithmetic, plus(): return (a.astype(f32) + b.astype(f32)).astype(bf16)  17 us
  transfers between devices with their start and end apart: 46, of which 20 were waited for; matrix products, arithmetic and copies ran while one was open for 9% of the time, Pallas kernels for 27%

profile of v2, /device:TPU:0, one launch (start us, length us, event | category | flops | bytes accessed | tf_op | source)
XLA Modules:
  0.0 461.6 jit_solution(3050011856670820333)
XLA Ops:
  9.9 1.4 concatenate.36
  14.1 3.0 collective-permute-start
  19.3 2.9 fusion.17
  22.9 1.7 collective-permute-start.1
  24.9 5.2 %all-gather.1 = s32[4,2,1024]{2,1,0:T(2,128)S(1)} all-gather(s32[1,2,1024]{2,1,0:T(2,128)S(1)} %bitcast.125), channel_id=2, replica_groups=mesh['expert'=4,'fsdp'=8] {'expert'}, dimensions={0}, use_global_device_ids=true | all-gather | bytes 40960 | tf_op jit(solution)/shard_map/all_gather | solution.py:1055
  30.1 2.3 collective-permute-done.4.refs_6_
  33.2 1.4 collective-permute-start.2
  36.0 4.0 collective-permute-done.5.refs_5_
  40.0 2.5 collective-permute-start.6
  42.5 2.1 pad_maximum_fusion.refs_7_
  45.8 8.0 %collective-permute-done.7 = bf16[72,768]{1,0:T(8,128)(2,1)S(1)} collective-permute-done((bf16[72,768]{1,0:T(8,128)(2,1)S(1)}, bf16[72,768]{1,0:T(8,128)(2,1)S(1)}, u32[]{:S(2)}, u32[]{:S(2)}) %collective-permute-start.7) | collective-permute-done | bytes 110624 | tf_op jit(solution)/shard_map/ppermute | solution.py:415
  54.5 1.5 collective-permute-start.19
  60.4 3.3 pad_maximum_fusion.3
  65.0 11.0 %shard_map.324 = (bf16[1024,768]{1,0:T(8,128)(2,1)}, bf16[1024,768]{1,0:T(8,128)(2,1)}, bf16[1024,768]{1,0:T(8,128)(2,1)}, bf16[1024,768]{1,0:T(8,128)(2,1)}, bf...) custom-call(s32[17]{0:T(128)S(1)} %pad_add_fusion.1.where_ref, bf16[1024,768]{1,0:T(8,128)(2,1)} %bitcast.105, ...), custom_call_target="tpu_custom_call" | custom-call | flops 3623878656 | bytes 11403264 | tf_op jit(solution)/shard_map/pallas_call | solution.py:48
  76.0 6.9 %collective-permute-done.15.refs_6_ = bf16[3,256,768]{2,1,0:T(8,128)(2,1)} collective-permute-done((bf16[3,256,768]{2,1,0:T(8,128)(2,1)}, bf16[3,256,768]{2,1,0:T(8,128)(2,1)}, u32[]{:S(2)}, u32[]{:S(2)}) %collective-permute-start.15) | collective-permute-done | bytes 1179680 | tf_op jit(solution)/shard_map/ppermute | solution.py:415
  82.9 2.5 collective-permute-start.16
  86.4 1.4 copy-done.30
  87.8 1.4 copy-done.31
  89.2 22.3 %shard_map.325 = (bf16[1024,768]{1,0:T(8,128)(2,1)S(1)}, f32[1024,768]{1,0:T(8,128)}, bf16[6,2,10,256,256]{4,3,2,1,0:T(8,128)(2,1)}) custom-call(s32[1]{0:T(128)} %dynamic_slice.12.len_ref, bf16[1024,768]{1,0:T(8,128)(2,1)S(1)} %copy-done.30, bf16[1024,768]{1,0:T(8,128)(2,1)S(1)} %copy-done.31, bf16[1024,768]{1,0:T(8,128)(2,1)} %get-tuple-element.69.v_ref), custom_call_target="tpu_custom_call" | custom-call | flops 4026531840 | bytes 25165824 | tf_op jit(solution)/shard_map/pallas_call | solution.py:48
  113.9 1.4 copy-done.28
  115.3 16.8 %shard_map.326 = (f32[1024,768]{1,0:T(8,128)}, f32[1024,128]{1,0:T(8,128)S(1)}, bf16[4,512,768]{2,1,0:T(8,128)(2,1)}) custom-call(bf16[1024,768]{1,0:T(8,128)(2,1)S(1)} %copy-done.28, bf16[1024,768]{1,0:T(8,128)(2,1)S(1)} %bitcast.107, bf16[1024,768]{1,0:T(8,128)(2,1)} %bitcast.135, bf16[768,768]{1,0:T(8,128)(2,1)S(1)} %copy-done.23, ...), custom_call_target="tpu_custom_call" | custom-call | flops 6039797760 | bytes 12189696 | tf_op jit(solution)/shard_map/pallas_call | solution.py:48
  132.9 4.7 %all-to-all-start = ((bf16[4,512,768]{2,1,0:T(8,128)(2,1)}), bf16[4,512,768]{2,1,0:T(8,128)(2,1)}, u32[]{:S(2)}, u32[]{:S(2)}) async-start(bf16[4,512,768]{2,1,0:T(8,128)(2,1)} %get-tuple-element.72), calls=%async_computation | async-start | bytes 6291456 | tf_op jit(solution)/shard_map/all_to_all | solution.py:1149
  137.6 2.1 collective-permute-start.17
  139.7 26.6 %collective-permute-done.17.refs_2_ = bf16[3,256,768]{2,1,0:T(8,128)(2,1)S(1)} collective-permute-done((bf16[3,256,768]{2,1,0:T(8,128)(2,1)}, bf16[3,256,768]{2,1,0:T(8,128)(2,1)S(1)}, u32[]{:S(2)}, u32[]{:S(2)}) %collective-permute-start.17) | collective-permute-done | bytes 1179680 | tf_op jit(solution)/shard_map/ppermute | solution.py:415
  166.3 2.0 collective-permute-start.18
  168.6 12.8 %collective-permute-done.18 = bf16[3,128,768]{2,1,0:T(8,128)(2,1)S(1)} collective-permute-done((bf16[3,128,768]{2,1,0:T(8,128)(2,1)S(1)}, bf16[3,128,768]{2,1,0:T(8,128)(2,1)S(1)}, u32[]{:S(2)}, u32[]{:S(2)}) %collective-permute-start.18) | collective-permute-done | bytes 589856 | tf_op jit(solution)/shard_map/ppermute | solution.py:415
  181.4 1.8 collective-permute-done.22
  184.3 1.3 copy-done.19
  185.5 19.9 %shard_map.327 = (bf16[4,256,768]{2,1,0:T(8,128)(2,1)}, bf16[8,1024,256]{2,1,0:T(8,128)(2,1)}, bf16[8,1024,256]{2,1,0:T(8,128)(2,1)}, bf16[8,1024,256]{2,1,0:T(8,128)(2,1)}) custom-call(bf16[4,512,768]{2,1,0:T(8,128)(2,1)} %all-to-all-done.x_ref.g_ref, bf16[3,256,768]{2,1,0:T(8,128)(2,1)S(1)} %copy-done.19, ...), custom_call_target="tpu_custom_call" | custom-call | flops 9663676416 | bytes 25165824 | tf_op jit(solution)/shard_map/pallas_call | solution.py:48
  205.4 24.7 %shard_map.328 = (bf16[4,256,768]{2,1,0:T(8,128)(2,1)}, bf16[8,2,1024,256]{3,2,1,0:T(8,128)(2,1)}) custom-call(bf16[4,512,768]{2,1,0:T(8,128)(2,1)} %all-to-all-done.x_ref.g_ref, bf16[8,1024,256]{2,1,0:T(8,128)(2,1)} %get-tuple-element.76.fa_ref, bf16[8,1024,256]{2,1,0:T(8,128)(2,1)} %get-tuple-element.77.fb_ref, bf16[3,256,768]{2,1,0:T(8,128)(2,1)S(1)} %copy-done.19, ...), custom_call_target="tpu_custom_call" | custom-call | flops 9663676416 | bytes 25165824 | tf_op jit(solution)/shard_map/pallas_call | solution.py:48
  230.1 7.1 %shard_map.330 = (bf16[3,256,768]{2,1,0:T(8,128)(2,1)S(1)}, bf16[3,256,768]{2,1,0:T(8,128)(2,1)S(1)}, bf16[3,256,768]{2,1,0:T(8,128)(2,1)S(1)}) custom-call(bf16[4,512,768]{2,1,0:T(8,128)(2,1)} %all-to-all-done.x_ref.g_ref, bf16[4,512,768]{2,1,0:T(8,128)(2,1)} %all-to-all-done.x_ref.g_ref, bf16[8,1024,256]{2,1,0:T(8,128)(2,1)} %get-tuple-element.75.inner_ref, ...), custom_call_target="tpu_custom_call" | custom-call | flops 3623878656 | bytes 11403264 | tf_op jit(solution)/shard_map/pallas_call | solution.py:48
  238.6 1.7 collective-permute-start.23
  240.7 3.6 all-to-all-start.1
  245.5 7.2 %collective-permute-done.23 = bf16[3,128,768]{2,1,0:T(8,128)(2,1)} collective-permute-done((bf16[3,128,768]{2,1,0:T(8,128)(2,1)}, bf16[3,128,768]{2,1,0:T(8,128)(2,1)}, u32[]{:S(2)}, u32[]{:S(2)}) %collective-permute-start.23) | collective-permute-done | bytes 589856 | tf_op jit(solution)/shard_map/ppermute | solution.py:415
  255.1 2.0 collective-permute-start.25
  259.8 4.5 all-to-all-done.1.y_ref
  264.3 4.4 all-to-all-start.2
  268.7 10.4 %shard_map.329 = (bf16[3,256,768]{2,1,0:T(8,128)(2,1)S(1)}, bf16[3,256,768]{2,1,0:T(8,128)(2,1)S(1)}, bf16[3,256,768]{2,1,0:T(8,128)(2,1)S(1)}, bf16[3,256,768]{2,1,0:T(8,128)(2,1)S(1)}, bf16[3,256,768]{2,1,0:T(8,128)(2,1)S(1)}) custom-call(bf16[4,512,768]{2,1,0:T(8,128)(2,1)} %all-to-all-done.x_ref.g_ref, bf16[4,512,768]{2,1,0:T(8,128)(2,1)} %all-to-all-done.x_ref.g_ref, ...), custom_call_target="tpu_custom_call" | custom-call | flops 6039797760 | bytes 16908288 | tf_op jit(solution)/shard_map/pallas_call | solution.py:48
  279.1 1.8 collective-permute-done.25
  280.9 2.6 add_convert_fusion.3
  283.5 2.3 collective-permute-start.27
  285.8 2.6 add_convert_fusion.2
  288.6 19.3 %shard_map.331 = (bf16[1024,768]{1,0:T(8,128)(2,1)}, f32[1024,768]{1,0:T(8,128)}, f32[1024,8]{1,0:T(8,128)S(1)}, f32[128,768]{1,0:T(8,128)S(1)}, f32[128,768]{1,0:T(8,128)S(1)}, /*index=5*/f32[8,128]{1,0:T(8,128)S(1)}) custom-call(bf16[4,256,768]{2,1,0:T(8,128)(2,1)S(1)} %all-to-all-done.1.y_ref, f32[1024,768]{1,0:T(8,128)} %get-tuple-element.88.res_ref, ...), custom_call_target="tpu_custom_call" | custom-call | flops 3221225472 | bytes 12582912 | tf_op jit(solution)/shard_map/pallas_call | solution.py:48
  309.5 1.3 copy-done.24
  310.9 12.6 %shard_map.332 = (f32[1024,768]{1,0:T(8,128)}, bf16[1024,768]{1,0:T(8,128)(2,1)S(1)}, bf16[768,768]{1,0:T(8,128)(2,1)S(1)}, f32[1,768]{1,0:T(1,128)S(1)}) custom-call(bf16[4,256,768]{2,1,0:T(8,128)(2,1)} %all-to-all-done.2.dx_ref, f32[1024,768]{1,0:T(8,128)} %get-tuple-element.93.part_ref, f32[1024,768]{1,0:T(8,128)} %get-tuple-element.88.res_ref, ...), custom_call_target="tpu_custom_call" | custom-call | flops 4026531840 | bytes 15728640 | tf_op jit(solution)/shard_map/pallas_call | solution.py:48
  324.6 21.9 %shard_map.333 = (bf16[1024,768]{1,0:T(8,128)(2,1)S(1)}, bf16[1024,768]{1,0:T(8,128)(2,1)S(1)}, bf16[1024,768]{1,0:T(8,128)(2,1)S(1)}) custom-call(bf16[1024,768]{1,0:T(8,128)(2,1)} %get-tuple-element.67.q_ref, bf16[1024,768]{1,0:T(8,128)(2,1)} %get-tuple-element.68.k_ref, bf16[1024,768]{1,0:T(8,128)(2,1)} %get-tuple-element.69.v_ref, ...), custom_call_target="tpu_custom_call" | custom-call | flops 8053063680 | bytes 33030144 | tf_op jit(solution)/shard_map/pallas_call | solution.py:48
  347.8 11.8 %shard_map.335 = (bf16[8,208,768]{2,1,0:T(8,128)(2,1)}, bf16[8,208,768]{2,1,0:T(8,128)(2,1)}) custom-call(s32[17]{0:T(128)S(1)} %pad_add_fusion.1.where_ref, bf16[1024,768]{1,0:T(8,128)(2,1)S(1)} %get-tuple-element.98.dq_ref, bf16[1024,768]{1,0:T(8,128)(2,1)S(1)} %get-tuple-element.99.dk_ref, bf16[1024,768]{1,0:T(8,128)(2,1)} %copy-done.3, ...), custom_call_target="tpu_custom_call" | custom-call | flops 3623878656 | bytes 16908288 | tf_op jit(solution)/shard_map/pallas_call | solution.py:48
  359.6 5.0 %collective-permute-done.29 = bf16[8,208,768]{2,1,0:T(8,128)(2,1)S(1)} collective-permute-done((bf16[8,208,768]{2,1,0:T(8,128)(2,1)}, bf16[8,208,768]{2,1,0:T(8,128)(2,1)S(1)}, u32[]{:S(2)}, u32[]{:S(2)}) %collective-permute-start.29) | collective-permute-done | bytes 2555936 | tf_op jit(solution)/shard_map/ppermute | solution.py:419
  364.6 2.1 add_convert_fusion.11
  366.8 2.0 collective-permute-start.30
  368.9 4.4 collective-permute-done.30
  373.3 2.0 collective-permute-start.31
  375.5 6.6 %collective-permute-done.31 = bf16[208,768]{1,0:T(8,128)(2,1)S(1)} collective-permute-done((bf16[208,768]{1,0:T(8,128)(2,1)S(1)}, bf16[208,768]{1,0:T(8,128)(2,1)S(1)}, u32[]{:S(2)}, u32[]{:S(2)}) %collective-permute-start.31) | collective-permute-done | bytes 319520 | tf_op jit(solution)/shard_map/ppermute | solution.py:415
  382.3 2.0 collective-permute-start.32
  384.3 5.8 %collective-permute-done.32 = bf16[208,768]{1,0:T(8,128)(2,1)S(1)} collective-permute-done((bf16[208,768]{1,0:T(8,128)(2,1)S(1)}, bf16[208,768]{1,0:T(8,128)(2,1)S(1)}, u32[]{:S(2)}, u32[]{:S(2)}) %collective-permute-start.32) | collective-permute-done | bytes 319520 | tf_op jit(solution)/shard_map/ppermute | solution.py:415
  391.5 2.7 add_convert_fusion
  395.3 2.6 add_convert_fusion.1
  398.8 1.7 collective-permute-start.33
  402.5 1.8 copy.67
  404.3 25.6 %collective-permute-done.33 = bf16[208,768]{1,0:T(8,128)(2,1)} collective-permute-done((bf16[208,768]{1,0:T(8,128)(2,1)}, bf16[208,768]{1,0:T(8,128)(2,1)}, u32[]{:S(2)}, u32[]{:S(2)}) %collective-permute-start.33) | collective-permute-done | bytes 319520 | tf_op jit(solution)/shard_map/ppermute | solution.py:415
  430.5 1.4 fusion.7
  432.8 8.9 %shard_map.334 = f32[1024,768]{1,0:T(8,128)} custom-call(bf16[1024,768]{1,0:T(8,128)(2,1)S(1)} %get-tuple-element.98.dq_ref, bf16[1024,768]{1,0:T(8,128)(2,1)S(1)} %get-tuple-element.99.dk_ref, bf16[1024,768]{1,0:T(8,128)(2,1)S(1)} %copy-done.4, bf16[3,768,768]{2,1,0:T(8,128)(2,1)} %get-tuple-element.101.w_ref, bf16[1024,768]{1,0:T(8,128)(2,1)} %bitcast.106, ...), custom_call_target="tpu_custom_call" | custom-call | flops 3623878656 | bytes 16121856 | tf_op jit(solution)/shard_map/pallas_call | solution.py:48
  441.9 2.0 convert_add_fusion
  447.3 1.5 shard_map.336
  (225 shorter events, 52.4 us)
Async XLA Ops:
  7.2 11.4 %copy-start = (s32[32]{0:T(128)S(1)}, s32[32]{0:T(128)}, u32[]{:S(2)}) copy-start(s32[32]{0:T(128)} %param.24) | copy-start | bytes 388
  7.2 105.4 %all-gather.4.cloned.1.call-start = ((), (), s32[]{:S(2)}) async-start(), calls=%async_computation.3 | async-start | bytes 1327104 | tf_op jit(solution)/shard_map/all_gather | solution.py:1093
  14.1 20.5 %copy-start.41 = (bf16[1,768,256]{2,1,0:T(8,128)(2,1)S(1)}, bf16[1,768,256]{2,1,0:T(8,128)(2,1)}, u32[]{:S(2)}) copy-start(bf16[1,768,256]{2,1,0:T(8,128)(2,1)} %param.37) | copy-start | bytes 1179652
  14.1 8.8 %collective-permute-start = (bf16[152,768]{1,0:T(8,128)(2,1)S(1)}, bf16[152,768]{1,0:T(8,128)(2,1)S(1)}, u32[]{:S(2)}, u32[]{:S(2)}) collective-permute-start(bf16[152,768]{1,0:T(8,128)(2,1)S(1)} %get-tuple-element.179.refs_0_), channel_id=1, source_target_pairs={{0,1},{2,0},{4,2},{6,4},{7,6},{5,7},{3,5},{1,3},{8,9},{10,8},{12,1... | collective-permute-start | bytes 700424 | tf_op jit(solution)/shard_map/ppermute | solution.py:415
  17.1 7.4 %collective-permute-start.3 = (bf16[152,768]{1,0:T(8,128)(2,1)S(1)}, bf16[152,768]{1,0:T(8,128)(2,1)S(1)}, u32[]{:S(2)}, u32[]{:S(2)}) collective-permute-start(bf16[152,768]{1,0:T(8,128)(2,1)S(1)} %get-tuple-element.179.refs_0_), channel_id=1, source_target_pairs={{0,2},{2,4},{4,6},{6,7},{7,5},{5,3},{3,1},{1,0},{8,10},{10,12},{12... | collective-permute-start | bytes 700424 | tf_op jit(solution)/shard_map/ppermute | solution.py:415
  22.9 10.3 %collective-permute-start.1 = (bf16[152,768]{1,0:T(8,128)(2,1)S(1)}, bf16[152,768]{1,0:T(8,128)(2,1)S(1)}, u32[]{:S(2)}, u32[]{:S(2)}) collective-permute-start(bf16[152,768]{1,0:T(8,128)(2,1)S(1)} %collective-permute-done.refs_1_), channel_id=1, source_target_pairs={{0,1},{2,0},{4,2},{6,4},{7,6},{5,7},{3,5},{1,3},{8,9},{10,8},{12,1... | collective-permute-start | bytes 700424 | tf_op jit(solution)/shard_map/ppermute | solution.py:415
  24.6 7.8 %collective-permute-start.4 = (bf16[152,768]{1,0:T(8,128)(2,1)S(1)}, bf16[152,768]{1,0:T(8,128)(2,1)S(1)}, u32[]{:S(2)}, u32[]{:S(2)}) collective-permute-start(bf16[152,768]{1,0:T(8,128)(2,1)S(1)} %collective-permute-done.3.refs_7_), channel_id=1, source_target_pairs={{0,2},{2,4},{4,6},{6,7},{7,5},{5,3},{3,1},{1,0},{8,10},{10,12},{12... | collective-permute-start | bytes 700424 | tf_op jit(solution)/shard_map/ppermute | solution.py:415
  32.4 7.5 %collective-permute-start.5 = (bf16[152,768]{1,0:T(8,128)(2,1)S(1)}, bf16[152,768]{1,0:T(8,128)(2,1)S(1)}, u32[]{:S(2)}, u32[]{:S(2)}) collective-permute-start(bf16[152,768]{1,0:T(8,128)(2,1)S(1)} %collective-permute-done.4.refs_6_), channel_id=1, source_target_pairs={{0,2},{2,4},{4,6},{6,7},{7,5},{5,3},{3,1},{1,0},{8,10},{10,12},{12... | collective-permute-start | bytes 700424 | tf_op jit(solution)/shard_map/ppermute | solution.py:415
  33.2 11.5 %collective-permute-start.2 = (bf16[152,768]{1,0:T(8,128)(2,1)S(1)}, bf16[152,768]{1,0:T(8,128)(2,1)S(1)}, u32[]{:S(2)}, u32[]{:S(2)}) collective-permute-start(bf16[152,768]{1,0:T(8,128)(2,1)S(1)} %collective-permute-done.1.refs_2_), channel_id=1, source_target_pairs={{0,1},{2,0},{4,2},{6,4},{7,6},{5,7},{3,5},{1,3},{8,9},{10,8},{12,1... | collective-permute-start | bytes 700424 | tf_op jit(solution)/shard_map/ppermute | solution.py:415
  40.0 5.8 %collective-permute-start.6 = (bf16[80,768]{1,0:T(8,128)(2,1)S(1)}, bf16[80,768]{1,0:T(8,128)(2,1)S(1)}, u32[]{:S(2)}, u32[]{:S(2)}) collective-permute-start(bf16[80,768]{1,0:T(8,128)(2,1)S(1)} %slice.244), channel_id=1, source_target_pairs={{0,2},{2,4},{4,6},{6,7},{7,5},{5,3},{3,1},{1,0},{8,10},{10,12},{12... | collective-permute-start | bytes 368648 | tf_op jit(solution)/shard_map/ppermute | solution.py:415
  44.6 12.5 %copy-start.42 = (bf16[1,1024,8]{1,2,0:T(8,128)(2,1)S(1)}, bf16[1,1024,8]{1,2,0:T(8,128)(2,1)}, u32[]{:S(2)}) copy-start(bf16[1,1024,8]{1,2,0:T(8,128)(2,1)} %param.22) | copy-start | bytes 49156
  44.7 12.2 %collective-permute-start.8 = (bf16[152,768]{1,0:T(8,128)(2,1)S(1)}, bf16[152,768]{1,0:T(8,128)(2,1)S(1)}, u32[]{:S(2)}, u32[]{:S(2)}) collective-permute-start(bf16[152,768]{1,0:T(8,128)(2,1)S(1)} %collective-permute-done.refs_1_), channel_id=1, source_target_pairs={{0,8},{8,0},{16,24},{24,16},{1,9},{9,1},{17,25},{25,17},{2,10},{10... | collective-permute-start | bytes 700424 | tf_op jit(solution)/shard_map/ppermute | solution.py:419
  44.7 12.7 %copy-start.46 = (s32[32]{0:T(128)S(1)}, s32[32]{0:T(128)}, u32[]{:S(2)}) copy-start(s32[32]{0:T(128)} %param.23) | copy-start | bytes 388
  44.7 13.3 %copy-start.38 = (s32[8]{0:T(128)S(1)}, s32[8]{0:T(128)}, u32[]{:S(2)}) copy-start(s32[8]{0:T(128)} %constant.67.clone) | copy-start | bytes 100
  44.7 9.1 %collective-permute-start.7 = (bf16[72,768]{1,0:T(8,128)(2,1)S(1)}, bf16[72,768]{1,0:T(8,128)(2,1)S(1)}, u32[]{:S(2)}, u32[]{:S(2)}) collective-permute-start(bf16[72,768]{1,0:T(8,128)(2,1)S(1)} %slice.245), channel_id=1, source_target_pairs={{0,1},{2,0},{4,2},{6,4},{7,6},{5,7},{3,5},{1,3},{8,9},{10,8},{12,1... | collective-permute-start | bytes 331784 | tf_op jit(solution)/shard_map/ppermute | solution.py:415
  53.8 29.1 %collective-permute-start.15 = (bf16[3,256,768]{2,1,0:T(8,128)(2,1)}, bf16[3,256,768]{2,1,0:T(8,128)(2,1)}, u32[]{:S(2)}, u32[]{:S(2)}) collective-permute-start(bf16[3,256,768]{2,1,0:T(8,128)(2,1)} %pad_maximum_fusion.refs_7_), channel_id=1, source_target_pairs={{0,2},{2,4},{4,6},{6,7},{7,5},{5,3},{3,1},{1,0},{8,10},{10,12},{12... | collective-permute-start | bytes 3538952 | tf_op jit(solution)/shard_map/ppermute | solution.py:415
  54.5 31.4 %collective-permute-start.19 = (bf16[3,256,768]{2,1,0:T(8,128)(2,1)}, bf16[3,256,768]{2,1,0:T(8,128)(2,1)}, u32[]{:S(2)}, u32[]{:S(2)}) collective-permute-start(bf16[3,256,768]{2,1,0:T(8,128)(2,1)} %pad_maximum_fusion.refs_7_), channel_id=1, source_target_pairs={{0,1},{2,0},{4,2},{6,4},{7,6},{5,7},{3,5},{1,3},{8,9},{10,8},{12,1... | collective-permute-start | bytes 3538952 | tf_op jit(solution)/shard_map/ppermute | solution.py:415
  56.3 3.0 collective-permute-start.14
  56.3 3.5 collective-permute-start.9
  56.8 3.0 collective-permute-start.13
  59.3 4.4 collective-permute-start.10
  59.8 3.9 collective-permute-start.12
  59.9 3.9 collective-permute-start.11
  63.7 12.2 %copy-start.13 = (f32[1024,128]{1,0:T(8,128)}, f32[1024,128]{1,0:T(8,128)S(1)}, u32[]{:S(2)}) copy-start(f32[1024,128]{1,0:T(8,128)S(1)} %get-tuple-element.191.cos_ref) | copy-start | bytes 1572868
  63.7 12.2 %copy-start.15 = (f32[1024,128]{1,0:T(8,128)}, f32[1024,128]{1,0:T(8,128)S(1)}, u32[]{:S(2)}) copy-start(f32[1024,128]{1,0:T(8,128)S(1)} %get-tuple-element.192.sin_ref) | copy-start | bytes 1572868
  76.0 36.7 %copy-start.20 = (bf16[128,768]{1,0:T(8,128)(2,1)}, bf16[128,768]{1,0:T(8,128)(2,1)S(1)}, u32[]{:S(2)}) copy-start(bf16[128,768]{1,0:T(8,128)(2,1)S(1)} %get-tuple-element.71.sw_ref.small_ref) | copy-start | bytes 589828
  82.9 54.6 %collective-permute-start.16 = (bf16[3,256,768]{2,1,0:T(8,128)(2,1)}, bf16[3,256,768]{2,1,0:T(8,128)(2,1)}, u32[]{:S(2)}, u32[]{:S(2)}) collective-permute-start(bf16[3,256,768]{2,1,0:T(8,128)(2,1)} %collective-permute-done.15.refs_6_), channel_id=1, source_target_pairs={{0,2},{2,4},{4,6},{6,7},{7,5},{5,3},{3,1},{1,0},{8,10},{10,12},{12... | collective-permute-start | bytes 3538952 | tf_op jit(solution)/shard_map/ppermute | solution.py:415
  85.9 53.8 %collective-permute-start.20 = (bf16[3,256,768]{2,1,0:T(8,128)(2,1)}, bf16[3,256,768]{2,1,0:T(8,128)(2,1)}, u32[]{:S(2)}, u32[]{:S(2)}) collective-permute-start(bf16[3,256,768]{2,1,0:T(8,128)(2,1)} %collective-permute-done.19.refs_5_), channel_id=1, source_target_pairs={{0,1},{2,0},{4,2},{6,4},{7,6},{5,7},{3,5},{1,3},{8,9},{10,8},{12,1... | collective-permute-start | bytes 3538952 | tf_op jit(solution)/shard_map/ppermute | solution.py:415
  89.2 23.4 %copy-start.2 = (bf16[1,1024,768]{2,1,0:T(8,128)(2,1)S(1)}, bf16[1,1024,768]{2,1,0:T(8,128)(2,1)}, u32[]{:S(2)}) copy-start(bf16[1,1024,768]{2,1,0:T(8,128)(2,1)} %param.21) | copy-start | bytes 4718596
  132.9 51.4 %all-to-all-start = ((bf16[4,512,768]{2,1,0:T(8,128)(2,1)}), bf16[4,512,768]{2,1,0:T(8,128)(2,1)}, u32[]{:S(2)}, u32[]{:S(2)}) async-start(bf16[4,512,768]{2,1,0:T(8,128)(2,1)} %get-tuple-element.72), calls=%async_computation | async-start | bytes 6291456 | tf_op jit(solution)/shard_map/all_to_all | solution.py:1149
  137.6 28.6 %collective-permute-start.17 = (bf16[3,256,768]{2,1,0:T(8,128)(2,1)}, bf16[3,256,768]{2,1,0:T(8,128)(2,1)S(1)}, u32[]{:S(2)}, u32[]{:S(2)}) collective-permute-start(bf16[3,256,768]{2,1,0:T(8,128)(2,1)} %collective-permute-done.16.refs_4_), channel_id=1, source_target_pairs={{0,2},{2,4},{4,6},{6,7},{7,5},{5,3},{3,1},{1,0},{8,10},{10,12},{12... | collective-permute-start | bytes 3538952 | tf_op jit(solution)/shard_map/ppermute | solution.py:415
  139.6 28.6 %collective-permute-start.21 = (bf16[3,256,768]{2,1,0:T(8,128)(2,1)}, bf16[3,256,768]{2,1,0:T(8,128)(2,1)S(1)}, u32[]{:S(2)}, u32[]{:S(2)}) collective-permute-start(bf16[3,256,768]{2,1,0:T(8,128)(2,1)} %collective-permute-done.20.refs_3_), channel_id=1, source_target_pairs={{0,1},{2,0},{4,2},{6,4},{7,6},{5,7},{3,5},{1,3},{8,9},{10,8},{12,1... | collective-permute-start | bytes 3538952 | tf_op jit(solution)/shard_map/ppermute | solution.py:415
  166.3 15.1 %collective-permute-start.18 = (bf16[3,128,768]{2,1,0:T(8,128)(2,1)S(1)}, bf16[3,128,768]{2,1,0:T(8,128)(2,1)S(1)}, u32[]{:S(2)}, u32[]{:S(2)}) collective-permute-start(bf16[3,128,768]{2,1,0:T(8,128)(2,1)S(1)} %slice.248), channel_id=1, source_target_pairs={{0,2},{2,4},{4,6},{6,7},{7,5},{5,3},{3,1},{1,0},{8,10},{10,12},{12... | collective-permute-start | bytes 1769480 | tf_op jit(solution)/shard_map/ppermute | solution.py:415
  168.3 14.9 %collective-permute-start.22 = (bf16[3,128,768]{2,1,0:T(8,128)(2,1)S(1)}, bf16[3,128,768]{2,1,0:T(8,128)(2,1)S(1)}, u32[]{:S(2)}, u32[]{:S(2)}) collective-permute-start(bf16[3,128,768]{2,1,0:T(8,128)(2,1)S(1)} %slice.249), channel_id=1, source_target_pairs={{0,1},{2,0},{4,2},{6,4},{7,6},{5,7},{3,5},{1,3},{8,9},{10,8},{12,1... | collective-permute-start | bytes 1769480 | tf_op jit(solution)/shard_map/ppermute | solution.py:415
  238.6 14.1 %collective-permute-start.23 = (bf16[3,128,768]{2,1,0:T(8,128)(2,1)}, bf16[3,128,768]{2,1,0:T(8,128)(2,1)}, u32[]{:S(2)}, u32[]{:S(2)}) collective-permute-start(bf16[3,128,768]{2,1,0:T(8,128)(2,1)} %get-tuple-element.177), channel_id=1, source_target_pairs={{0,2},{2,4},{4,6},{6,7},{7,5},{5,3},{3,1},{1,0},{8,10},{10,12},{12... | collective-permute-start | bytes 1769480 | tf_op jit(solution)/shard_map/ppermute | solution.py:415
  240.3 16.7 %collective-permute-start.24 = (bf16[3,128,768]{2,1,0:T(8,128)(2,1)}, bf16[3,128,768]{2,1,0:T(8,128)(2,1)}, u32[]{:S(2)}, u32[]{:S(2)}) collective-permute-start(bf16[3,128,768]{2,1,0:T(8,128)(2,1)} %get-tuple-element.176), channel_id=1, source_target_pairs={{0,1},{2,0},{4,2},{6,4},{7,6},{5,7},{3,5},{1,3},{8,9},{10,8},{12,1... | collective-permute-start | bytes 1769480 | tf_op jit(solution)/shard_map/ppermute | solution.py:415
  240.7 23.6 %all-to-all-start.1 = ((bf16[4,256,768]{2,1,0:T(8,128)(2,1)}), bf16[4,256,768]{2,1,0:T(8,128)(2,1)S(1)}, u32[]{:S(2)}, u32[]{:S(2)}) async-start(bf16[4,256,768]{2,1,0:T(8,128)(2,1)} %get-tuple-element.74), calls=%async_computation.1 | async-start | bytes 3145728 | tf_op jit(solution)/shard_map/all_to_all | solution.py:1151
  255.1 25.8 %collective-permute-start.25 = (bf16[3,256,768]{2,1,0:T(8,128)(2,1)}, bf16[3,256,768]{2,1,0:T(8,128)(2,1)}, u32[]{:S(2)}, u32[]{:S(2)}) collective-permute-start(bf16[3,256,768]{2,1,0:T(8,128)(2,1)} %pad_maximum_fusion.1), channel_id=1, source_target_pairs={{0,2},{2,4},{4,6},{6,7},{7,5},{5,3},{3,1},{1,0},{8,10},{10,12},{12... | collective-permute-start | bytes 3538952 | tf_op jit(solution)/shard_map/ppermute | solution.py:415
  259.4 26.4 %collective-permute-start.26 = (bf16[3,256,768]{2,1,0:T(8,128)(2,1)}, bf16[3,256,768]{2,1,0:T(8,128)(2,1)}, u32[]{:S(2)}, u32[]{:S(2)}) collective-permute-start(bf16[3,256,768]{2,1,0:T(8,128)(2,1)} %pad_maximum_fusion.2), channel_id=1, source_target_pairs={{0,1},{2,0},{4,2},{6,4},{7,6},{5,7},{3,5},{1,3},{8,9},{10,8},{12,1... | collective-permute-start | bytes 3538952 | tf_op jit(solution)/shard_map/ppermute | solution.py:415
  264.3 45.2 %all-to-all-start.2 = ((bf16[4,256,768]{2,1,0:T(8,128)(2,1)}), bf16[4,256,768]{2,1,0:T(8,128)(2,1)}, u32[]{:S(2)}, u32[]{:S(2)}) async-start(bf16[4,256,768]{2,1,0:T(8,128)(2,1)} %get-tuple-element.92), calls=%async_computation.2 | async-start | bytes 3145728 | tf_op jit(solution)/shard_map/all_to_all | solution.py:1153
  283.5 64.3 %collective-permute-start.27 = (bf16[3,256,768]{2,1,0:T(8,128)(2,1)}, bf16[3,256,768]{2,1,0:T(8,128)(2,1)}, u32[]{:S(2)}, u32[]{:S(2)}) collective-permute-start(bf16[3,256,768]{2,1,0:T(8,128)(2,1)} %add_convert_fusion.3), channel_id=1, source_target_pairs={{0,2},{2,4},{4,6},{6,7},{7,5},{5,3},{3,1},{1,0},{8,10},{10,12},{12... | collective-permute-start | bytes 3538952 | tf_op jit(solution)/shard_map/ppermute | solution.py:415
  288.4 59.3 %collective-permute-start.28 = (bf16[3,256,768]{2,1,0:T(8,128)(2,1)}, bf16[3,256,768]{2,1,0:T(8,128)(2,1)}, u32[]{:S(2)}, u32[]{:S(2)}) collective-permute-start(bf16[3,256,768]{2,1,0:T(8,128)(2,1)} %add_convert_fusion.2), channel_id=1, source_target_pairs={{0,1},{2,0},{4,2},{6,4},{7,6},{5,7},{3,5},{1,3},{8,9},{10,8},{12,1... | collective-permute-start | bytes 3538952 | tf_op jit(solution)/shard_map/ppermute | solution.py:415
  309.4 14.0 %copy-start.34 = (f32[128,768]{1,0:T(8,128)}, f32[128,768]{1,0:T(8,128)S(1)}, u32[]{:S(2)}) copy-start(f32[128,768]{1,0:T(8,128)S(1)} %get-tuple-element.108.gvec_ref) | copy-start | bytes 1179652
  310.9 13.8 %copy-start.14 = (f32[1024,128]{1,0:T(8,128)S(1)}, f32[1024,128]{1,0:T(8,128)}, u32[]{:S(2)}) copy-start(f32[1024,128]{1,0:T(8,128)} %copy-done.13) | copy-start | bytes 1572868
  310.9 13.8 %copy-start.16 = (f32[1024,128]{1,0:T(8,128)S(1)}, f32[1024,128]{1,0:T(8,128)}, u32[]{:S(2)}) copy-start(f32[1024,128]{1,0:T(8,128)} %copy-done.15) | copy-start | bytes 1572868
  324.6 23.1 %copy-start.22 = (bf16[128,768]{1,0:T(8,128)(2,1)S(1)}, bf16[128,768]{1,0:T(8,128)(2,1)}, u32[]{:S(2)}) copy-start(bf16[128,768]{1,0:T(8,128)(2,1)} %copy-done.20) | copy-start | bytes 589828
  324.6 23.1 %copy-start.33 = (f32[128,768]{1,0:T(8,128)S(1)}, f32[128,768]{1,0:T(8,128)}, u32[]{:S(2)}) copy-start(f32[128,768]{1,0:T(8,128)} %copy-done.32) | copy-start | bytes 1179652
  324.6 23.1 %copy-start.35 = (f32[128,768]{1,0:T(8,128)S(1)}, f32[128,768]{1,0:T(8,128)}, u32[]{:S(2)}) copy-start(f32[128,768]{1,0:T(8,128)} %copy-done.34) | copy-start | bytes 1179652
  359.6 5.0 %collective-permute-start.29 = (bf16[8,208,768]{2,1,0:T(8,128)(2,1)}, bf16[8,208,768]{2,1,0:T(8,128)(2,1)S(1)}, u32[]{:S(2)}, u32[]{:S(2)}) collective-permute-start(bf16[8,208,768]{2,1,0:T(8,128)(2,1)} %get-tuple-element.111), channel_id=1, source_target_pairs={{0,8},{8,0},{16,24},{24,16},{1,9},{9,1},{17,25},{25,17},{2,10},{10... | collective-permute-start | bytes 7667720 | tf_op jit(solution)/shard_map/ppermute | solution.py:419
  364.6 36.9 %copy-start.40 = (bf16[8,208,768]{2,1,0:T(8,128)(2,1)}, bf16[8,208,768]{2,1,0:T(8,128)(2,1)S(1)}, u32[]{:S(2)}) copy-start(bf16[8,208,768]{2,1,0:T(8,128)(2,1)S(1)} %collective-permute-done.29) | copy-start | bytes 7667716
  366.8 6.5 %collective-permute-start.30 = (bf16[112,768]{1,0:T(8,128)(2,1)S(1)}, bf16[112,768]{1,0:T(8,128)(2,1)S(1)}, u32[]{:S(2)}, u32[]{:S(2)}) collective-permute-start(bf16[112,768]{1,0:T(8,128)(2,1)S(1)} %slice_bitcast_fusion.3), channel_id=1, source_target_pairs={{0,2},{2,4},{4,6},{6,7},{7,5},{5,3},{3,1},{1,0},{8,10},{10,12},{12... | collective-permute-start | bytes 516104 | tf_op jit(solution)/shard_map/ppermute | solution.py:415
  368.8 6.5 %collective-permute-start.34 = (bf16[96,768]{1,0:T(8,128)(2,1)S(1)}, bf16[96,768]{1,0:T(8,128)(2,1)S(1)}, u32[]{:S(2)}, u32[]{:S(2)}) collective-permute-start(bf16[96,768]{1,0:T(8,128)(2,1)S(1)} %slice_bitcast_fusion.5), channel_id=1, source_target_pairs={{0,1},{2,0},{4,2},{6,4},{7,6},{5,7},{3,5},{1,3},{8,9},{10,8},{12,1... | collective-permute-start | bytes 442376 | tf_op jit(solution)/shard_map/ppermute | solution.py:415
  368.8 13.3 %copy-start.39 = (bf16[8,208,768]{2,1,0:T(8,128)(2,1)S(1)}, bf16[8,208,768]{2,1,0:T(8,128)(2,1)}, u32[]{:S(2)}) copy-start(bf16[8,208,768]{2,1,0:T(8,128)(2,1)} %get-tuple-element.110) | copy-start | bytes 7667716
  373.3 8.8 %collective-permute-start.31 = (bf16[208,768]{1,0:T(8,128)(2,1)S(1)}, bf16[208,768]{1,0:T(8,128)(2,1)S(1)}, u32[]{:S(2)}, u32[]{:S(2)}) collective-permute-start(bf16[208,768]{1,0:T(8,128)(2,1)S(1)} %pad_maximum_fusion.5), channel_id=1, source_target_pairs={{0,2},{2,4},{4,6},{6,7},{7,5},{5,3},{3,1},{1,0},{8,10},{10,12},{12... | collective-permute-start | bytes 958472 | tf_op jit(solution)/shard_map/ppermute | solution.py:415
  375.4 8.9 %collective-permute-start.35 = (bf16[208,768]{1,0:T(8,128)(2,1)S(1)}, bf16[208,768]{1,0:T(8,128)(2,1)S(1)}, u32[]{:S(2)}, u32[]{:S(2)}) collective-permute-start(bf16[208,768]{1,0:T(8,128)(2,1)S(1)} %pad_maximum_fusion.6), channel_id=1, source_target_pairs={{0,1},{2,0},{4,2},{6,4},{7,6},{5,7},{3,5},{1,3},{8,9},{10,8},{12,1... | collective-permute-start | bytes 958472 | tf_op jit(solution)/shard_map/ppermute | solution.py:415
  382.3 7.9 %collective-permute-start.32 = (bf16[208,768]{1,0:T(8,128)(2,1)S(1)}, bf16[208,768]{1,0:T(8,128)(2,1)S(1)}, u32[]{:S(2)}, u32[]{:S(2)}) collective-permute-start(bf16[208,768]{1,0:T(8,128)(2,1)S(1)} %fusion.4), channel_id=1, source_target_pairs={{0,2},{2,4},{4,6},{6,7},{7,5},{5,3},{3,1},{1,0},{8,10},{10,12},{12... | collective-permute-start | bytes 958472 | tf_op jit(solution)/shard_map/ppermute | solution.py:415
  391.1 10.5 %collective-permute-start.36 = (bf16[208,768]{1,0:T(8,128)(2,1)S(1)}, bf16[208,768]{1,0:T(8,128)(2,1)S(1)}, u32[]{:S(2)}, u32[]{:S(2)}) collective-permute-start(bf16[208,768]{1,0:T(8,128)(2,1)S(1)} %get-tuple-element.169), channel_id=1, source_target_pairs={{0,1},{2,0},{4,2},{6,4},{7,6},{5,7},{3,5},{1,3},{8,9},{10,8},{12,1... | collective-permute-start | bytes 958472 | tf_op jit(solution)/shard_map/ppermute | solution.py:415
  394.2 47.7 %collective-permute-start.41 = (bf16[3,256,768]{2,1,0:T(8,128)(2,1)}, bf16[3,256,768]{2,1,0:T(8,128)(2,1)}, u32[]{:S(2)}, u32[]{:S(2)}) collective-permute-start(bf16[3,256,768]{2,1,0:T(8,128)(2,1)} %add_convert_fusion), channel_id=1, source_target_pairs={{0,1},{2,0},{4,2},{6,4},{7,6},{5,7},{3,5},{1,3},{8,9},{10,8},{12,1... | collective-permute-start | bytes 3538952 | tf_op jit(solution)/shard_map/ppermute | solution.py:415
  397.9 44.0 %collective-permute-start.40 = (bf16[3,256,768]{2,1,0:T(8,128)(2,1)}, bf16[3,256,768]{2,1,0:T(8,128)(2,1)}, u32[]{:S(2)}, u32[]{:S(2)}) collective-permute-start(bf16[3,256,768]{2,1,0:T(8,128)(2,1)} %add_convert_fusion.1), channel_id=1, source_target_pairs={{0,2},{2,4},{4,6},{6,7},{7,5},{5,3},{3,1},{1,0},{8,10},{10,12},{12... | collective-permute-start | bytes 3538952 | tf_op jit(solution)/shard_map/ppermute | solution.py:415
  398.8 31.1 %collective-permute-start.33 = (bf16[208,768]{1,0:T(8,128)(2,1)}, bf16[208,768]{1,0:T(8,128)(2,1)}, u32[]{:S(2)}, u32[]{:S(2)}) collective-permute-start(bf16[208,768]{1,0:T(8,128)(2,1)} %get-tuple-element.168), channel_id=1, source_target_pairs={{0,2},{2,4},{4,6},{6,7},{7,5},{5,3},{3,1},{1,0},{8,10},{10,12},{12... | collective-permute-start | bytes 958472 | tf_op jit(solution)/shard_map/ppermute | solution.py:415
  402.4 28.1 %collective-permute-start.37 = (bf16[208,768]{1,0:T(8,128)(2,1)}, bf16[208,768]{1,0:T(8,128)(2,1)}, u32[]{:S(2)}, u32[]{:S(2)}) collective-permute-start(bf16[208,768]{1,0:T(8,128)(2,1)} %fusion.3), channel_id=1, source_target_pairs={{0,1},{2,0},{4,2},{6,4},{7,6},{5,7},{3,5},{1,3},{8,9},{10,8},{12,1... | collective-permute-start | bytes 958472 | tf_op jit(solution)/shard_map/ppermute | solution.py:415
  404.3 28.5 %copy-start.4 = (bf16[1024,768]{1,0:T(8,128)(2,1)S(1)}, bf16[1024,768]{1,0:T(8,128)(2,1)}, u32[]{:S(2)}) copy-start(bf16[1024,768]{1,0:T(8,128)(2,1)} %copy-done.3) | copy-start | bytes 4718596
  431.9 9.8 %collective-permute-start.38 = (bf16[208,768]{1,0:T(8,128)(2,1)S(1)}, bf16[208,768]{1,0:T(8,128)(2,1)S(1)}, u32[]{:S(2)}, u32[]{:S(2)}) collective-permute-start(bf16[208,768]{1,0:T(8,128)(2,1)S(1)} %fusion.7), channel_id=1, source_target_pairs={{0,16},{8,24},{16,0},{24,8},{1,17},{9,25},{17,1},{25,9},{2,18},{10... | collective-permute-start | bytes 958472 | tf_op jit(solution)/shard_map/ppermute | solution.py:419
  441.8 5.5 %collective-permute-start.39 = (bf16[208,768]{1,0:T(8,128)(2,1)S(1)}, bf16[208,768]{1,0:T(8,128)(2,1)S(1)}, u32[]{:S(2)}, u32[]{:S(2)}) collective-permute-start(bf16[208,768]{1,0:T(8,128)(2,1)S(1)} %add_convert_fusion.6.mine_ref), channel_id=1, source_target_pairs={{0,8},{8,0},{16,24},{24,16},{1,9},{9,1},{17,25},{25,17},{2,10},{10... | collective-permute-start | bytes 958472 | tf_op jit(solution)/shard_map/ppermute | solution.py:419
  (30 other events, 108.8 us)
Sparse Core Ops, SparseCore 0:
  17.4 45.8 all-gather.3
